TPU v7x, 32 devices: a whole 2x2x4 slice. The times are simulated.
32 devices in a mesh: seg: 4 (over x, core), ops: 8 (over z, y).
Axes of the slice: x: 2, y: 2, z: 4, core: 2. Of those that a mesh axis runs over, the one named last changes fastest.
Arguments:
- amat: bfloat16 [16384, 128], P(('seg', 'ops')), may hold values from -6 to 6
- lam: float32 [16384], P(('seg', 'ops')), may hold values from 0.3 to 3
- hdiag: float32 [16384, 128], P(('seg', 'ops')), may hold values from 0.25 to 8
- left_ops: bfloat16 [4, 48, 4096, 128], P('seg', 'ops'), may hold values from -0.5 to 0.5
- right_operators: bfloat16 [4, 48, 4096, 128], P('seg', 'ops'), may hold values from -0.078125 to 0.078125
- couple: int32 [4, 48, 32], P('seg', 'ops'), may hold values from 0 to 31
- blockmask: int32 [4, 48, 32], P('seg', 'ops'), may hold values 0 or 1
Outputs:
- sigma_two: float32 [16384, 128], P(('seg', 'ops'))
- theta: float32 [4], P('seg')
Inputs may be any that keep to these rules, and one draw needn't show every extreme that they name: couple[s, k, i] is the sector of the vector that term k of segment s carries into sector i.
All inputs are finite; a program needn't handle non-finite values. No bound on the sum of `blockmask` on one device may be relied on, other than what follows from the above.
Results may differ from a plain program's by a relative error of at most 0.009.
Values may be sent and summed in bfloat16 or wider, within the bound.
No kernel may reach another device: no remote copies, remote signals or barrier semaphores. Data moves between devices by JAX's collectives and lax.ppermute only.
A program may use at most 64 MiB of HBM per device.

v0:
```python
from functools import partial

import jax
import jax.numpy as jnp
from jax import lax
from jax.sharding import PartitionSpec as P


def shifted(array, axis, by):
    devices = lax.axis_size(axis)
    pairs = [(i, i + by) for i in range(devices) if 0 <= i + by < devices]
    return lax.ppermute(array, axis, pairs)


def row_per_term(blocks, left, right, links, live, width, start, count):
    nterms = left.shape[0]
    nblock = max(count // width, 1)
    inside = min(count, width)
    lrows = left.reshape(nterms, nblock, inside, width)
    rblock = right.reshape(nterms, nblock, width, width)
    picked = blocks[links]
    inner_block = jnp.einsum("knra,knab->knrb", lrows, picked, preferred_element_type=jnp.float32)
    inner_block = (inner_block * live[:, :, None, None]).astype(jnp.bfloat16)
    result = jnp.einsum("knrb,kndb->nrd", inner_block, rblock, preferred_element_type=jnp.float32)
    return result.reshape(count, width)


def body(amat, lam, hdiag, left_ops, right_operators, couple, blockmask):
    width = amat.shape[1]
    links = couple[0]
    nsector = links.shape[1]
    bond = width * nsector
    left = left_ops[0]
    right = right_operators[0]
    live = blockmask[0].astype(jnp.float32)
    segment = lax.axis_index("seg")
    earlier = shifted(lam, "seg", 1)
    weights = jnp.where(segment == 0, jnp.ones_like(earlier), earlier)
    psi = (weights[:, None] * amat.astype(jnp.float32)).astype(jnp.bfloat16)

    def apply_terms(vector):
        whole = lax.all_gather(vector, "ops", axis=0, tiled=True)
        blocks = whole.reshape(nsector, width, width)
        rows_of = partial(row_per_term, blocks, left, right, links, live, width)
        summed = lax.psum_scatter(rows_of(0, bond), "ops", scatter_dimension=0, tiled=True)
        return summed + hdiag * vector.astype(jnp.float32)

    sigma_one = apply_terms(psi)
    psi_float = psi.astype(jnp.float32)
    numer, denom = lax.psum((jnp.sum(psi_float * sigma_one), jnp.sum(psi_float * psi_float)), "ops")
    quotient = numer / denom
    correction = ((sigma_one - quotient * psi_float) / hdiag).astype(jnp.bfloat16)
    sigma_two = apply_terms(correction)
    return (sigma_two, quotient.reshape(1))


def solution(mesh):
    placed = (
        P(("seg", "ops"), None),
        P(("seg", "ops")),
        P(("seg", "ops"), None),
        P("seg", "ops", None, None),
        P("seg", "ops", None, None),
        P("seg", "ops", None),
        P("seg", "ops", None),
    )
    return jax.shard_map(
        body,
        mesh=mesh,
        in_specs=placed,
        out_specs=(P(("seg", "ops"), None), P("seg")),
        check_vma=False,
    )
```

profile of v0, /device:TPU:0, one launch (start us, length us, event | category | flops | bytes accessed | tf_op | source)
XLA Modules:
  0.0 300.4 jit_solution(6029675187855948964)
XLA Ops:
  7.2 0.0 all-gather.3.cloned.1.call-start
  7.2 2.4 collective-permute-start
  9.6 1.0 collective-permute-done
  10.6 1.7 multiply_convert_fusion.2
  12.3 0.0 all-gather.3.cloned.1.call-update
  12.3 0.0 reduce-scatter.3.cloned.1.call-start
  12.4 0.7 convert_element_type.40
  13.1 0.7 fusion.38
  13.8 0.1 reshape.61
  13.9 0.1 copy.17
  14.0 43.2 %all-gather.3.cloned.1.call-done = bf16[4096,128]{1,0:T(8,128)(2,1)} async-done(((bf16[512,128]{1,0:T(8,128)(2,1)}), bf16[4096,128]{1,0:T(8,128)(2,1)}) %all-gather.3.cloned.1.call-update) | async-done | bytes 1048592 | tf_op jit(solution)/shard_map/all_gather | solution.py:42
  57.2 9.3 %gather_fusion = bf16[192,128,128]{2,1,0:T(8,128)(2,1)} fusion(bf16[32,128,128]{2,1,0:T(8,128)(2,1)} %bitcast.24, s32[1024]{0:T(1024)S(1)} %pad_clamp_fusion), kind=kCustom, calls=%fused_computation | custom fusion | bytes 12583680 | tf_op jit(solution)/shard_map/gather | solution.py:21
  66.5 0.0 copy-start
  66.5 0.0 copy-start.1
  66.5 9.3 %fusion.1 = f32[32,128,128,1]{2,1,3,0:T(8,128)} fusion(f32[6,32]{0,1:T(8,128)S(1)} %bitcast.30, bf16[6,32,128,128]{3,2,1,0:T(8,128)(2,1)} %bitcast.32, bf16[6,32,128,128]{3,2,1,0:T(8,128)(2,1)} %bitcast.27, bf16[6,32,128,128]{3,2,1,0:T(8,128)(2,1)} %bitcast.34), kind=kOutput, calls=%fused_computation.5 | convolution fusion | flops 1616904192 | bytes 20972288 | tf_op jit(solution)/shard_map/knrb,kndb->nrd/dot_general | solution.py:24
  75.8 0.0 reduce-scatter.3.cloned.1.call-update
  75.8 0.0 all-gather.5.cloned.1.call-start
  75.9 67.1 %reduce-scatter.3.cloned.1.call-done = f32[512,128]{1,0:T(8,128)} async-done(((f32[4096,128]{1,0:T(8,128)}), f32[512,128]{1,0:T(8,128)}) %reduce-scatter.3.cloned.1.call-update) | async-done | bytes 262160 | tf_op jit(solution)/shard_map/reduce_scatter | solution.py:45
  143.0 0.0 copy-done
  143.0 0.0 copy-done.1
  143.0 1.7 fusion.34
  144.7 19.7 %all-reduce = (f32[]{:T(128)}, f32[]{:T(128)}) all-reduce(f32[]{:T(128)} %get-tuple-element.3, f32[]{:T(128)} %get-tuple-element.2), channel_id=1, replica_groups=mesh['seg'=4,'ops'=8] {'ops'}, use_global_device_ids=true, to_apply=%region_2.3 | all-reduce | flops 2 | bytes 16 | tf_op jit(solution)/shard_map/psum | solution.py:50
  165.8 1.8 fusion.37
  167.6 0.0 all-gather.5.cloned.1.call-update
  167.6 0.0 reduce-scatter.5.cloned.1.call-start
  167.6 37.6 %all-gather.5.cloned.1.call-done = bf16[4096,128]{1,0:T(8,128)(2,1)} async-done(((bf16[512,128]{1,0:T(8,128)(2,1)}), bf16[4096,128]{1,0:T(8,128)(2,1)}) %all-gather.5.cloned.1.call-update) | async-done | bytes 1048592 | tf_op jit(solution)/shard_map/all_gather | solution.py:42
  205.2 9.3 %gather_fusion.1 = bf16[192,128,128]{2,1,0:T(8,128)(2,1)} fusion(bf16[32,128,128]{2,1,0:T(8,128)(2,1)} %bitcast.25, s32[1024]{0:T(1024)S(1)} %pad_clamp_fusion), kind=kCustom, calls=%fused_computation.1 | custom fusion | bytes 12583680 | tf_op jit(solution)/shard_map/gather | solution.py:21
  214.5 9.3 %fusion.4 = f32[32,128,128,1]{2,1,3,0:T(8,128)} fusion(f32[6,32]{0,1:T(8,128)S(1)} %bitcast.31, bf16[6,32,128,128]{3,2,1,0:T(8,128)(2,1)} %bitcast.33, bf16[6,32,128,128]{3,2,1,0:T(8,128)(2,1)} %bitcast.26, bf16[6,32,128,128]{3,2,1,0:T(8,128)(2,1)} %bitcast.35), kind=kOutput, calls=%fused_computation.7 | convolution fusion | flops 1616904192 | bytes 20972288 | tf_op jit(solution)/shard_map/knrb,kndb->nrd/dot_general | solution.py:24
  223.8 0.0 reduce-scatter.5.cloned.1.call-update
  223.9 67.2 %reduce-scatter.5.cloned.1.call-done = f32[512,128]{1,0:T(8,128)} async-done(((f32[4096,128]{1,0:T(8,128)}), f32[512,128]{1,0:T(8,128)}) %reduce-scatter.5.cloned.1.call-update) | async-done | bytes 262160 | tf_op jit(solution)/shard_map/reduce_scatter | solution.py:45
  291.0 0.0 copy-done.2
  291.0 1.7 multiply_add_fusion
  (3 shorter events, 0.0 us)
Async XLA Ops:
  7.2 50.0 %all-gather.3.cloned.1.call-start = ((), (), s32[]{:S(2)}) async-start(), calls=%async_computation.2 | async-start | bytes 1179648 | tf_op jit(solution)/shard_map/all_gather | solution.py:42
  7.2 3.4 %collective-permute-start = (f32[512]{0:T(512)}, f32[512]{0:T(512)S(1)}, u32[]{:S(2)}, u32[]{:S(2)}) collective-permute-start(f32[512]{0:T(512)} %param.8), channel_id=1, source_target_pairs={{0,8},{8,16},{16,24},{1,9},{9,17},{17,25},{2,10},{10,18},{18,26},{... | collective-permute-start | bytes 6152 | tf_op jit(solution)/shard_map/ppermute | solution.py:12
  12.3 130.7 %reduce-scatter.3.cloned.1.call-start = ((), (), s32[]{:S(2)}) async-start(), calls=%async_computation.3 | async-start | bytes 2359296 | tf_op jit(solution)/shard_map/reduce_scatter | solution.py:45
  66.5 76.5 %copy-start = (f32[512,128]{1,0:T(8,128)S(1)}, f32[512,128]{1,0:T(8,128)}, u32[]{:S(2)}) copy-start(f32[512,128]{1,0:T(8,128)} %param.9) | copy-start | bytes 786436
  66.5 76.5 %copy-start.1 = (bf16[512,128]{1,0:T(8,128)(2,1)S(1)}, bf16[512,128]{1,0:T(8,128)(2,1)}, u32[]{:S(2)}) copy-start(bf16[512,128]{1,0:T(8,128)(2,1)} %param.7) | copy-start | bytes 393220
  75.8 129.4 %all-gather.5.cloned.1.call-start = ((), (), s32[]{:S(2)}) async-start(), calls=%async_computation.4 | async-start | bytes 1179648 | tf_op jit(solution)/shard_map/all_gather | solution.py:42
  167.6 123.4 %reduce-scatter.5.cloned.1.call-start = ((), (), s32[]{:S(2)}) async-start(), calls=%async_computation.5 | async-start | bytes 2359296 | tf_op jit(solution)/shard_map/reduce_scatter | solution.py:45
  214.5 76.5 %copy-start.2 = (bf16[512,128]{1,0:T(8,128)(2,1)S(1)}, bf16[512,128]{1,0:T(8,128)(2,1)}, u32[]{:S(2)}) copy-start(bf16[512,128]{1,0:T(8,128)(2,1)} %fusion.37) | copy-start | bytes 393220
Sparse Core Ops, SparseCore 0:
  12.5 44.6 all-gather.2
  76.0 67.0 reduce-scatter.2
  167.7 37.4 all-gather.4
  224.0 67.0 reduce-scatter.4
where the time goes:
time: 301 us; the launch traced here: 300 us
  waiting for transfers between devices  216 us (72%)
  blocking collectives  19.7 us (7%)
  local copies, waits for them, and re-layouts  18.7 us (6%)
  matrix products  18.6 us (6%)
  between operations  16.3 us (5%)
  other arithmetic  8.23 us (3%)
    reduce_scatter x2, waiting for transfers between devices, apply_terms(): lax.psum_scatter(rows_of(0, bond), 'ops', scatter_dimension=0, tiled=True)  134 us
    all_gather x2, waiting for transfers between devices, apply_terms(): whole = lax.all_gather(vector, 'ops', axis=0, tiled=True)  80.9 us
    psum x1, blocking collectives, body(): lax.psum((jnp.sum(psi_float * sigma_one), jnp.sum(psi_float * psi_float))...  19.7 us
    dot_general x2, matrix products, row_per_term(): jnp.einsum('knrb,kndb->nrd', inner_block, rblock, preferred_element_type=...  18.6 us
    gather x2, local copies, waits for them, and re-layouts, row_per_term(): picked = blocks[links]  18.5 us
  transfers between devices with their start and end apart: 5, of which 5 were waited for; matrix products, arithmetic and copies ran while one was open for 1% of the time, Pallas kernels for 0%

commit v1 on v0

v1 whole, which is shorter than its diff:
```python
from functools import partial

import jax
import jax.numpy as jnp
from jax import lax
from jax.experimental import pallas as pl
from jax.experimental.pallas import tpu as pltpu
from jax.sharding import PartitionSpec as P


def shifted(array, axis, by):
    devices = lax.axis_size(axis)
    pairs = [(i, i + by) for i in range(devices) if 0 <= i + by < devices]
    return lax.ppermute(array, axis, pairs)


def row_per_term(blocks, left, right, links, live, width, count):
    nterms = left.shape[0]
    nblock = count // width
    lrows = left.reshape(nterms, nblock, width, width)
    rblock = right.reshape(nterms, nblock, width, width)
    picked = blocks[links]
    inner_block = jnp.einsum("knra,knab->knrb", lrows, picked, preferred_element_type=jnp.float32)
    inner_block = (inner_block * live[:, :, None, None]).astype(jnp.bfloat16)
    result = jnp.einsum("knrb,kndb->nrd", inner_block, rblock, preferred_element_type=jnp.float32)
    return result.reshape(count, width)


def gathered_body(amat, lam, hdiag, left_ops, right_operators, couple, blockmask):
    width = amat.shape[1]
    links = couple[0]
    nsector = links.shape[1]
    bond = width * nsector
    live = blockmask[0].astype(jnp.float32)
    earlier = shifted(lam, "seg", 1)
    weights = jnp.where(lax.axis_index("seg") == 0, jnp.ones_like(earlier), earlier)
    psi = (weights[:, None] * amat.astype(jnp.float32)).astype(jnp.bfloat16)

    def apply_terms(vector):
        whole = lax.all_gather(vector, "ops", axis=0, tiled=True)
        blocks = whole.reshape(nsector, width, width)
        part = row_per_term(blocks, left_ops[0], right_operators[0], links, live, width, bond)
        summed = lax.psum_scatter(part, "ops", scatter_dimension=0, tiled=True)
        return summed + hdiag * vector.astype(jnp.float32)

    sigma_one = apply_terms(psi)
    psi_float = psi.astype(jnp.float32)
    numer, denom = lax.psum((jnp.sum(psi_float * sigma_one), jnp.sum(psi_float * psi_float)), "ops")
    quotient = numer / denom
    correction = ((sigma_one - quotient * psi_float) / hdiag).astype(jnp.bfloat16)
    sigma_two = apply_terms(correction)
    return (sigma_two, quotient.reshape(1))


def scaled_products(vector, links, left, right, chunks, per, store):
    nterms, width = left.shape[1], left.shape[3]
    nsector = vector.shape[0] // width - 1

    def inner_of(i):
        rows = pl.ds(pl.multiple_of(i * width, width), width)
        blocks = []
        for k in range(nterms):
            at = pl.multiple_of(links[k * nsector + i] * width, width)
            product = jnp.dot(left[0, k, rows, :], vector[pl.ds(at, width), :], preferred_element_type=jnp.float32)
            blocks.append(product.astype(jnp.bfloat16))
        return jnp.concatenate(blocks, axis=1), rows

    def outer_of(inner, rows):
        factors = jnp.concatenate([right[0, k, rows, :] for k in range(nterms)], axis=1)
        return lax.dot_general(inner, factors, (((1,), (1,)), ((), ())), preferred_element_type=jnp.float32)

    waiting = None
    for t, chunk in enumerate(chunks):
        for i in range(per):
            now = inner_of(chunk * per + i)
            if waiting is not None:
                store(*waiting[:2], outer_of(*waiting[2]))
            waiting = (t, i, now)
    store(*waiting[:2], outer_of(*waiting[2]))


def rows_at(chunk, rows):
    return pl.ds(pl.multiple_of(chunk * rows, rows), rows)


def squares(total, own):
    return jnp.sum((total * own).reshape(-1, 8, total.shape[1]), axis=0)


def first_kernel(line, first, dots, place, links, left, right, *refs):
    npiece = 2 * line
    pieces, vector, outs = refs[:npiece], refs[npiece], refs[npiece + 1 :]
    rows, width = pieces[0].shape
    for p in range(npiece):
        chunk = place[0] ^ (2 * (p % line)) ^ (p // line)
        vector[rows_at(chunk, rows), :] = pieces[p][...]
    vector[npiece * rows :, :] = jnp.zeros((width, width), vector.dtype)
    chunks = [place[0] ^ (2 * d) ^ 1 for d in first]
    if dots:
        outs[-1][...] = jnp.zeros_like(outs[-1])

    def store(t, i, sums):
        at = slice(i * width, (i + 1) * width)
        outs[t][at, :] = sums.astype(outs[t].dtype)
        if dots:
            start = pl.multiple_of(chunks[t] * rows + i * width, width)
            outs[-1][...] += squares(sums, vector[pl.ds(start, width), :].astype(jnp.float32))

    scaled_products(vector, links, left, right, chunks, rows // width, store)


def second_kernel(line, rest, dots, place, links, left, right, vector, *refs):
    width = vector.shape[1]
    if dots:
        hdiag, before, *outs, numer, denom = refs
        rows = hdiag.shape[0]
        own = vector[rows_at(place[0], rows), :].astype(jnp.float32)
        numer[...] = before[...] + squares(hdiag[...] * own, own)
        whole = vector[: 2 * line * rows, :].astype(jnp.float32)
        denom[...] = squares(whole, whole)
    else:
        outs = refs
        rows = outs[0].shape[0]
    chunks = [place[0] ^ (2 * d) ^ 1 for d in rest] + [place[0] ^ (2 * d) for d in range(line)]

    def store(t, i, sums):
        at = slice(i * width, (i + 1) * width)
        outs[t][at, :] = sums.astype(outs[t].dtype)
        if dots:
            start = pl.multiple_of(chunks[t] * rows + i * width, width)
            numer[...] += squares(sums, vector[pl.ds(start, width), :].astype(jnp.float32))

    scaled_products(vector, links, left, right, chunks, rows // width, store)


TAIL = 16


def pass_kernel(kept, came, mine, other, out):
    rows, width = kept.shape
    out[:rows, :] = (kept[...] + came[...].astype(jnp.float32)).astype(out.dtype)
    part = jnp.sum(mine[...] + other[...], axis=0, keepdims=True)
    row = lax.broadcasted_iota(jnp.int32, (TAIL, width), 0)
    tail = jnp.zeros((TAIL, width), jnp.float32)
    for r in range(3):
        rounded = part.astype(out.dtype).astype(jnp.float32)
        tail = jnp.where(row == r, rounded, tail)
        part = part - rounded
    out[rows:, :] = tail.astype(out.dtype)


def correct_kernel(nmore, *refs):
    kept, came, more, refs = refs[0], refs[1], refs[2 : 2 + nmore], refs[2 + nmore :]
    psi, hdiag, mine, other, denom, correction, theta = refs
    rows = psi.shape[0]
    total = kept[...] + came[...].astype(jnp.float32)
    numer = jnp.sum(mine[...] + other[...], keepdims=True)
    for m in more:
        total = total + m[:rows, :].astype(jnp.float32)
        numer = numer + jnp.sum(m[rows:, :].astype(jnp.float32), keepdims=True)
    quotient = numer / jnp.sum(denom[...], keepdims=True)
    vector = psi[...].astype(jnp.float32)
    sigma = total + hdiag[...] * vector
    correction[...] = ((sigma - quotient * vector) / hdiag[...]).astype(correction.dtype)
    theta[...] = jnp.broadcast_to(quotient, theta.shape)


def load_kernel(source, target, sems):
    copies = [pltpu.make_async_copy(source.at[:, k], target.at[:, k], sems.at[k]) for k in range(source.shape[1])]
    for copy in copies:
        copy.start()
    for copy in copies:
        copy.wait()


VMEM = pl.BlockSpec(memory_space=pltpu.VMEM)
SMEM = pl.BlockSpec(memory_space=pltpu.SMEM)


def on_chip(kernel, out_shape, nscalar, *args, limit=8 << 20):
    outs = pl.pallas_call(
        kernel,
        out_shape=out_shape,
        in_specs=[SMEM] * nscalar + [VMEM] * (len(args) - nscalar),
        out_specs=[VMEM] * len(out_shape),
        compiler_params=pltpu.CompilerParams(vmem_limit_bytes=limit),
    )(*args)
    return list(outs)


def loaded(operators):
    return pl.pallas_call(
        load_kernel,
        out_shape=pltpu.VMEM(operators.shape, operators.dtype),
        in_specs=[pl.BlockSpec(memory_space=pltpu.HBM)],
        out_specs=VMEM,
        scratch_shapes=[pltpu.SemaphoreType.DMA((operators.shape[1],))],
        compiler_params=pltpu.CompilerParams(vmem_limit_bytes=1 << 20),
    )(pltpu.with_memory_space_constraint(operators, pltpu.HBM))


def far_first(line):
    return sorted(range(line), key=lambda d: -d.bit_length())


def paired_body(amat, lam, hdiag, left_ops, right_operators, couple, blockmask):
    rows, width = amat.shape
    nsector = couple.shape[2]
    devices = lax.axis_size("ops")
    line = devices // 2
    place = lax.axis_index("ops").astype(jnp.int32).reshape(1)
    links = jnp.where(blockmask[0] != 0, couple[0], nsector).reshape(-1)
    shape = jax.ShapeDtypeStruct
    tile = shape((8, width), jnp.float32)
    sent, kept = shape((rows, width), jnp.bfloat16), shape((rows, width), jnp.float32)

    def exchange(array, by):
        return lax.ppermute(array, "ops", [(o, o ^ by) for o in range(devices)])

    far = far_first(line)
    first, rest = far[:1], far[1:]

    def gather(piece):
        column = {0: piece}
        for d in far:
            if d:
                column[d] = exchange(piece, 2 * d)
        other = {d: exchange(column[d], 1) for d in range(line)}
        return [column[d] for d in range(line)] + [other[d] for d in range(line)]

    def apply_terms(piece, left, right, dots):
        left = pltpu.with_memory_space_constraint(left, pltpu.VMEM)
        right = pltpu.with_memory_space_constraint(right, pltpu.VMEM)
        pieces = gather(piece)
        whole = shape((devices * rows + width, width), jnp.bfloat16)
        vector, *lead = on_chip(
            partial(first_kernel, line, first, dots),
            [whole] + [sent] * len(first) + [tile] * dots,
            2, place, links, left, right, *pieces,
        )
        extra = (hdiag, lead[-1]) if dots else ()
        outs = on_chip(
            partial(second_kernel, line, rest, dots),
            [sent] * len(rest) + [kept] * line + [tile] * (2 * dots),
            2, place, links, left, right, vector, *extra,
        )
        leave = dict(zip(first + rest, lead[: len(first)] + outs[: len(rest)]))
        stay = outs[len(rest) : len(rest) + line]
        sums = ()
        if dots:
            mine, denom = outs[len(rest) + line :]
            other = exchange(mine, 1)
            sums = (mine, other, denom)
        came = {d: exchange(leave[d], 1) for d in far}
        more = []
        for d in far:
            if d and dots:
                message = on_chip(pass_kernel, [shape((rows + TAIL, width), jnp.bfloat16)], 0, stay[d], came[d], mine, other)[0]
            elif d:
                message = (stay[d] + came[d].astype(jnp.float32)).astype(jnp.bfloat16)
            if d:
                more.append(exchange(message, 2 * d))
        return [stay[0], came[0]] + more, sums

    links, left_ops, right_operators = lax.optimization_barrier((links, left_ops, right_operators))
    left = loaded(left_ops)
    right = loaded(right_operators)
    earlier = shifted(lam, "seg", 1)
    weights = jnp.where(lax.axis_index("seg") == 0, jnp.ones_like(earlier), earlier)
    psi = (weights[:, None] * amat.astype(jnp.float32)).astype(jnp.bfloat16)
    terms, sums = apply_terms(psi, left, right, True)
    correction, theta = on_chip(partial(correct_kernel, line - 1), [sent, tile], 0, *terms, psi, hdiag, *sums)
    terms, _ = apply_terms(correction, left, right, False)
    sigma_two = sum(t.astype(jnp.float32) for t in terms) + hdiag * correction.astype(jnp.float32)
    return (sigma_two, theta[0, :1])


def is_paired(devices, nsector):
    return devices >= 2 and devices & (devices - 1) == 0 and nsector % devices == 0


def body(amat, lam, hdiag, left_ops, right_operators, couple, blockmask):
    form = paired_body if is_paired(lax.axis_size("ops"), couple.shape[2]) else gathered_body
    return form(amat, lam, hdiag, left_ops, right_operators, couple, blockmask)


def solution(mesh):
    placed = (
        P(("seg", "ops"), None),
        P(("seg", "ops")),
        P(("seg", "ops"), None),
        P("seg", "ops", None, None),
        P("seg", "ops", None, None),
        P("seg", "ops", None),
        P("seg", "ops", None),
    )
    return jax.shard_map(
        body,
        mesh=mesh,
        in_specs=placed,
        out_specs=(P(("seg", "ops"), None), P("seg")),
        check_vma=False,
    )
```

time: 301 us -> 108 us (0.36)
  waiting for transfers between devices: 216 us -> 50.1 us
  starting transfers between devices: 2.56 us -> 37.8 us
  blocking collectives: 19.7 us -> 0 us
  matrix products: 18.6 us -> 0 us
  local copies, waits for them, and re-layouts: 18.7 us -> 0.59 us
  Pallas kernels: 0 us -> 16.1 us
  between operations: 16.3 us -> 0.78 us
  other arithmetic: 8.23 us -> 2.65 us
    reduce_scatter x2 -> x0, waiting for transfers between devices: 134 us -> none  [apply_terms(): lax.psum_scatter(rows_of(0, bond), 'ops', scatter_dimension=0, tiled=True)]
    all_gather x2 -> x0, waiting for transfers between devices: 80.9 us -> none  [apply_terms(): whole = lax.all_gather(vector, 'ops', axis=0, tiled=True)]
    ppermute x0 -> x29, waiting for transfers between devices: none -> 49.1 us  [exchange(): return lax.ppermute(array, 'ops', [(o, o ^ by) for o in range(devices)])]
    ppermute x0 -> x29, starting transfers between devices: none -> 35.4 us  [exchange(): return lax.ppermute(array, 'ops', [(o, o ^ by) for o in range(devices)])]
    psum x1 -> x0, blocking collectives: 19.7 us -> none  [body(): lax.psum((jnp.sum(psi_float * sigma_one), jnp.sum(psi_float * psi_float))...]
    dot_general x2 -> x0, matrix products: 18.6 us -> none  [row_per_term(): jnp.einsum('knrb,kndb->nrd', inner_block, rblock, preferred_element_type=...]
    gather x2 -> x0, local copies, waits for them, and re-layouts: 18.5 us -> none  [row_per_term(): picked = blocks[links]]
    pallas_call x0 -> x10, Pallas kernels: none -> 16.1 us  [the longest x8 10.4 us: on_chip(): pl.pallas_call(kernel, out_shape=out_shape, in_specs=[SMEM] * nscalar + [...]
  transfers between devices with their start and end apart: 5 -> 30, of which waited for: 5 -> 17; matrix products, arithmetic and copies ran while one was open for 1% -> 1% of each run, Pallas kernels for 0% -> 5%
where the time goes in v1:
time: 108 us
  waiting for transfers between devices  50.1 us (46%)
  starting transfers between devices  37.8 us (35%)
  Pallas kernels  16.1 us (15%)
  other arithmetic  2.65 us (2%)
    ppermute x29, waiting for transfers between devices, exchange(): return lax.ppermute(array, 'ops', [(o, o ^ by) for o in range(devices)])  49.1 us
    ppermute x29, starting transfers between devices, exchange(): return lax.ppermute(array, 'ops', [(o, o ^ by) for o in range(devices)])  35.4 us
    pallas_call x8, Pallas kernels, on_chip(): pl.pallas_call(kernel, out_shape=out_shape, in_specs=[SMEM] * nscalar + [...  10.4 us
    pallas_call x2, Pallas kernels, loaded(): pl.pallas_call(load_kernel, out_shape=pltpu.VMEM(operators.shape, operato...  5.71 us
    ppermute x1, starting transfers between devices, shifted(): return lax.ppermute(array, axis, pairs)  2.4 us
  transfers between devices with their start and end apart: 30, of which 17 were waited for; matrix products, arithmetic and copies ran while one was open for 1% of the time, Pallas kernels for 5%

profile of v1, /device:TPU:0, one launch (start us, length us, event | category | flops | bytes accessed | tf_op | source)
XLA Modules:
  0.0 108.0 jit_solution(1735597331476959610)
XLA Ops:
  0.6 2.4 %collective-permute-start = (f32[512]{0:T(512)}, f32[512]{0:T(512)S(1)}, u32[]{:S(2)}, u32[]{:S(2)}) collective-permute-start(f32[512]{0:T(512)} %param.8), channel_id=1, source_target_pairs={{0,8},{8,16},{16,24},{1,9},{9,17},{17,25},{2,10},{10,18},{18,26},{... | collective-permute-start | bytes 6152 | tf_op jit(solution)/shard_map/ppermute | solution.py:14
  5.1 4.5 %collective-permute-start.3 = (bf16[512,128]{1,0:T(8,128)(2,1)S(1)}, bf16[512,128]{1,0:T(8,128)(2,1)S(1)}, u32[]{:S(2)}, u32[]{:S(2)}) collective-permute-start(bf16[512,128]{1,0:T(8,128)(2,1)S(1)} %multiply_convert_fusion.refs_0_.refs_5_), channel_id=1, source_target_pairs={{0,6},{1,7},{2,4},{3,5},{4,2},{5,3},{6,0},{7,1},{8,14},{9,15},{10,... | collective-permute-start | bytes 393224 | tf_op jit(solution)/shard_map/ppermute | solution.py:218
  10.2 1.7 %collective-permute-start.4 = (bf16[512,128]{1,0:T(8,128)(2,1)S(1)}, bf16[512,128]{1,0:T(8,128)(2,1)S(1)}, u32[]{:S(2)}, u32[]{:S(2)}) collective-permute-start(bf16[512,128]{1,0:T(8,128)(2,1)S(1)} %multiply_convert_fusion.refs_0_.refs_5_), channel_id=1, source_target_pairs={{0,1},{1,0},{2,3},{3,2},{4,5},{5,4},{6,7},{7,6},{8,9},{9,8},{10,11... | collective-permute-start | bytes 393224 | tf_op jit(solution)/shard_map/ppermute | solution.py:218
  13.1 2.0 %collective-permute-start.7 = (bf16[512,128]{1,0:T(8,128)(2,1)S(1)}, bf16[512,128]{1,0:T(8,128)(2,1)S(1)}, u32[]{:S(2)}, u32[]{:S(2)}) collective-permute-start(bf16[512,128]{1,0:T(8,128)(2,1)S(1)} %collective-permute-done.3.refs_3_), channel_id=1, source_target_pairs={{0,1},{1,0},{2,3},{3,2},{4,5},{5,4},{6,7},{7,6},{8,9},{9,8},{10,11... | collective-permute-start | bytes 393224 | tf_op jit(solution)/shard_map/ppermute | solution.py:218
  15.0 6.1 %collective-permute-done.2.refs_2_ = bf16[512,128]{1,0:T(8,128)(2,1)S(1)} collective-permute-done((bf16[512,128]{1,0:T(8,128)(2,1)S(1)}, bf16[512,128]{1,0:T(8,128)(2,1)S(1)}, u32[]{:S(2)}, u32[]{:S(2)}) %collective-permute-start.2) | collective-permute-done | bytes 131104 | tf_op jit(solution)/shard_map/ppermute | solution.py:218
  23.9 2.9 %shard_map.86.left = bf16[1,6,4096,128]{3,2,1,0:T(8,128)(2,1)S(1)} custom-call(bf16[1,6,4096,128]{3,2,1,0:T(8,128)(2,1)} %source), custom_call_target="tpu_custom_call" | custom-call | tf_op jit(solution)/shard_map/pallas_call | solution.py:192
  26.8 2.9 %shard_map.87.right = bf16[1,6,4096,128]{3,2,1,0:T(8,128)(2,1)S(1)} custom-call(bf16[1,6,4096,128]{3,2,1,0:T(8,128)(2,1)} %source.1), custom_call_target="tpu_custom_call" | custom-call | tf_op jit(solution)/shard_map/pallas_call | solution.py:192
  31.1 3.8 %shard_map.89 = (bf16[512,128]{1,0:T(8,128)(2,1)S(1)}, bf16[512,128]{1,0:T(8,128)(2,1)S(1)}, bf16[512,128]{1,0:T(8,128)(2,1)S(1)}, f32[512,128]{1,0:T(8,128)S(1)...) custom-call(s32[1]{0:T(128)} %bitcast.place, ...), custom_call_target="tpu_custom_call" | custom-call | tf_op jit(solution)/shard_map/pallas_call | solution.py:181
  34.9 1.6 %collective-permute-start.14 = (bf16[512,128]{1,0:T(8,128)(2,1)S(1)}, bf16[512,128]{1,0:T(8,128)(2,1)S(1)}, u32[]{:S(2)}, u32[]{:S(2)}) collective-permute-start(bf16[512,128]{1,0:T(8,128)(2,1)S(1)} %get-tuple-element.41), channel_id=1, source_target_pairs={{0,1},{1,0},{2,3},{3,2},{4,5},{5,4},{6,7},{7,6},{8,9},{9,8},{10,11... | collective-permute-start | bytes 393224 | tf_op jit(solution)/shard_map/ppermute | solution.py:218
  37.0 1.5 %collective-permute-start.9 = (bf16[512,128]{1,0:T(8,128)(2,1)S(1)}, bf16[512,128]{1,0:T(8,128)(2,1)S(1)}, u32[]{:S(2)}, u32[]{:S(2)}) collective-permute-start(bf16[512,128]{1,0:T(8,128)(2,1)S(1)} %get-tuple-element.36), channel_id=1, source_target_pairs={{0,1},{1,0},{2,3},{3,2},{4,5},{5,4},{6,7},{7,6},{8,9},{9,8},{10,11... | collective-permute-start | bytes 393224 | tf_op jit(solution)/shard_map/ppermute | solution.py:218
  39.0 6.9 %collective-permute-done.10.other.refs_8_ = f32[8,128]{1,0:T(8,128)S(1)} collective-permute-done((f32[8,128]{1,0:T(8,128)S(1)}, f32[8,128]{1,0:T(8,128)S(1)}, u32[]{:S(2)}, u32[]{:S(2)}) %collective-permute-start.10) | collective-permute-done | bytes 4128 | tf_op jit(solution)/shard_map/ppermute | solution.py:218
  47.1 1.9 %collective-permute-start.13 = (bf16[528,128]{1,0:T(8,128)(2,1)S(1)}, bf16[528,128]{1,0:T(8,128)(2,1)S(1)}, u32[]{:S(2)}, u32[]{:S(2)}) collective-permute-start(bf16[528,128]{1,0:T(8,128)(2,1)S(1)} %shard_map.91), channel_id=1, source_target_pairs={{0,6},{1,7},{2,4},{3,5},{4,2},{5,3},{6,0},{7,1},{8,14},{9,15},{10,... | collective-permute-start | bytes 405512 | tf_op jit(solution)/shard_map/ppermute | solution.py:218
  49.7 1.5 %collective-permute-start.8 = (bf16[512,128]{1,0:T(8,128)(2,1)S(1)}, bf16[512,128]{1,0:T(8,128)(2,1)S(1)}, u32[]{:S(2)}, u32[]{:S(2)}) collective-permute-start(bf16[512,128]{1,0:T(8,128)(2,1)S(1)} %get-tuple-element.34), channel_id=1, source_target_pairs={{0,1},{1,0},{2,3},{3,2},{4,5},{5,4},{6,7},{7,6},{8,9},{9,8},{10,11... | collective-permute-start | bytes 393224 | tf_op jit(solution)/shard_map/ppermute | solution.py:218
  51.2 3.5 %collective-permute-done.8.refs_1_ = bf16[512,128]{1,0:T(8,128)(2,1)S(1)} collective-permute-done((bf16[512,128]{1,0:T(8,128)(2,1)S(1)}, bf16[512,128]{1,0:T(8,128)(2,1)S(1)}, u32[]{:S(2)}, u32[]{:S(2)}) %collective-permute-start.8) | collective-permute-done | bytes 131104 | tf_op jit(solution)/shard_map/ppermute | solution.py:218
  54.7 1.6 %collective-permute-done.13.refs_3_ = bf16[528,128]{1,0:T(8,128)(2,1)S(1)} collective-permute-done((bf16[528,128]{1,0:T(8,128)(2,1)S(1)}, bf16[528,128]{1,0:T(8,128)(2,1)S(1)}, u32[]{:S(2)}, u32[]{:S(2)}) %collective-permute-start.13) | collective-permute-done | bytes 135200 | tf_op jit(solution)/shard_map/ppermute | solution.py:218
  56.3 5.0 %collective-permute-done.11.refs_2_ = bf16[528,128]{1,0:T(8,128)(2,1)S(1)} collective-permute-done((bf16[528,128]{1,0:T(8,128)(2,1)S(1)}, bf16[528,128]{1,0:T(8,128)(2,1)S(1)}, u32[]{:S(2)}, u32[]{:S(2)}) %collective-permute-start.11) | collective-permute-done | bytes 135200 | tf_op jit(solution)/shard_map/ppermute | solution.py:218
  61.5 2.2 %collective-permute-start.18 = (bf16[512,128]{1,0:T(8,128)(2,1)S(1)}, bf16[512,128]{1,0:T(8,128)(2,1)S(1)}, u32[]{:S(2)}, u32[]{:S(2)}) collective-permute-start(bf16[512,128]{1,0:T(8,128)(2,1)S(1)} %get-tuple-element.43.refs_0_), channel_id=1, source_target_pairs={{0,6},{1,7},{2,4},{3,5},{4,2},{5,3},{6,0},{7,1},{8,14},{9,15},{10,... | collective-permute-start | bytes 393224 | tf_op jit(solution)/shard_map/ppermute | solution.py:218
  63.6 2.3 %collective-permute-start.16 = (bf16[512,128]{1,0:T(8,128)(2,1)S(1)}, bf16[512,128]{1,0:T(8,128)(2,1)S(1)}, u32[]{:S(2)}, u32[]{:S(2)}) collective-permute-start(bf16[512,128]{1,0:T(8,128)(2,1)S(1)} %get-tuple-element.43.refs_0_), channel_id=1, source_target_pairs={{0,2},{1,3},{2,0},{3,1},{4,6},{5,7},{6,4},{7,5},{8,10},{9,11},{10,... | collective-permute-start | bytes 393224 | tf_op jit(solution)/shard_map/ppermute | solution.py:218
  65.9 1.5 %collective-permute-start.19 = (bf16[512,128]{1,0:T(8,128)(2,1)S(1)}, bf16[512,128]{1,0:T(8,128)(2,1)S(1)}, u32[]{:S(2)}, u32[]{:S(2)}) collective-permute-start(bf16[512,128]{1,0:T(8,128)(2,1)S(1)} %get-tuple-element.43.refs_0_), channel_id=1, source_target_pairs={{0,1},{1,0},{2,3},{3,2},{4,5},{5,4},{6,7},{7,6},{8,9},{9,8},{10,11... | collective-permute-start | bytes 393224 | tf_op jit(solution)/shard_map/ppermute | solution.py:218
  67.4 2.3 %collective-permute-done.18.refs_3_ = bf16[512,128]{1,0:T(8,128)(2,1)S(1)} collective-permute-done((bf16[512,128]{1,0:T(8,128)(2,1)S(1)}, bf16[512,128]{1,0:T(8,128)(2,1)S(1)}, u32[]{:S(2)}, u32[]{:S(2)}) %collective-permute-start.18) | collective-permute-done | bytes 131104 | tf_op jit(solution)/shard_map/ppermute | solution.py:218
  69.7 1.5 %collective-permute-start.22 = (bf16[512,128]{1,0:T(8,128)(2,1)S(1)}, bf16[512,128]{1,0:T(8,128)(2,1)S(1)}, u32[]{:S(2)}, u32[]{:S(2)}) collective-permute-start(bf16[512,128]{1,0:T(8,128)(2,1)S(1)} %collective-permute-done.18.refs_3_), channel_id=1, source_target_pairs={{0,1},{1,0},{2,3},{3,2},{4,5},{5,4},{6,7},{7,6},{8,9},{9,8},{10,11... | collective-permute-start | bytes 393224 | tf_op jit(solution)/shard_map/ppermute | solution.py:218
  71.2 2.4 %collective-permute-done.17.refs_2_ = bf16[512,128]{1,0:T(8,128)(2,1)S(1)} collective-permute-done((bf16[512,128]{1,0:T(8,128)(2,1)S(1)}, bf16[512,128]{1,0:T(8,128)(2,1)S(1)}, u32[]{:S(2)}, u32[]{:S(2)}) %collective-permute-start.17) | collective-permute-done | bytes 131104 | tf_op jit(solution)/shard_map/ppermute | solution.py:218
  73.6 1.5 %collective-permute-start.21 = (bf16[512,128]{1,0:T(8,128)(2,1)S(1)}, bf16[512,128]{1,0:T(8,128)(2,1)S(1)}, u32[]{:S(2)}, u32[]{:S(2)}) collective-permute-start(bf16[512,128]{1,0:T(8,128)(2,1)S(1)} %collective-permute-done.17.refs_2_), channel_id=1, source_target_pairs={{0,1},{1,0},{2,3},{3,2},{4,5},{5,4},{6,7},{7,6},{8,9},{9,8},{10,11... | collective-permute-start | bytes 393224 | tf_op jit(solution)/shard_map/ppermute | solution.py:218
  75.7 4.3 %collective-permute-done.21.refs_6_ = bf16[512,128]{1,0:T(8,128)(2,1)S(1)} collective-permute-done((bf16[512,128]{1,0:T(8,128)(2,1)S(1)}, bf16[512,128]{1,0:T(8,128)(2,1)S(1)}, u32[]{:S(2)}, u32[]{:S(2)}) %collective-permute-start.21) | collective-permute-done | bytes 131104 | tf_op jit(solution)/shard_map/ppermute | solution.py:218
  80.0 1.8 %collective-permute-done.20.refs_5_ = bf16[512,128]{1,0:T(8,128)(2,1)S(1)} collective-permute-done((bf16[512,128]{1,0:T(8,128)(2,1)S(1)}, bf16[512,128]{1,0:T(8,128)(2,1)S(1)}, u32[]{:S(2)}, u32[]{:S(2)}) %collective-permute-start.20) | collective-permute-done | bytes 131104 | tf_op jit(solution)/shard_map/ppermute | solution.py:218
  83.0 3.8 %shard_map.95 = (bf16[512,128]{1,0:T(8,128)(2,1)S(1)}, bf16[512,128]{1,0:T(8,128)(2,1)S(1)}, bf16[512,128]{1,0:T(8,128)(2,1)S(1)}, f32[512,128]{1,0:T(8,128)S(1)...) custom-call(s32[1]{0:T(128)} %bitcast.place, s32[192]{0:T(256)S(1)} %select_n.17.links, ...), custom_call_target="tpu_custom_call" | custom-call | tf_op jit(solution)/shard_map/pallas_call | solution.py:181
  86.8 1.6 %collective-permute-start.26 = (bf16[512,128]{1,0:T(8,128)(2,1)S(1)}, bf16[512,128]{1,0:T(8,128)(2,1)S(1)}, u32[]{:S(2)}, u32[]{:S(2)}) collective-permute-start(bf16[512,128]{1,0:T(8,128)(2,1)S(1)} %get-tuple-element.50), channel_id=1, source_target_pairs={{0,1},{1,0},{2,3},{3,2},{4,5},{5,4},{6,7},{7,6},{8,9},{9,8},{10,11... | collective-permute-start | bytes 393224 | tf_op jit(solution)/shard_map/ppermute | solution.py:218
  88.9 1.5 %collective-permute-start.28 = (bf16[512,128]{1,0:T(8,128)(2,1)S(1)}, bf16[512,128]{1,0:T(8,128)(2,1)S(1)}, u32[]{:S(2)}, u32[]{:S(2)}) collective-permute-start(bf16[512,128]{1,0:T(8,128)(2,1)S(1)} %get-tuple-element.52), channel_id=1, source_target_pairs={{0,1},{1,0},{2,3},{3,2},{4,5},{5,4},{6,7},{7,6},{8,9},{9,8},{10,11... | collective-permute-start | bytes 393224 | tf_op jit(solution)/shard_map/ppermute | solution.py:218
  90.9 2.3 %collective-permute-done.26 = bf16[512,128]{1,0:T(8,128)(2,1)S(1)} collective-permute-done((bf16[512,128]{1,0:T(8,128)(2,1)S(1)}, bf16[512,128]{1,0:T(8,128)(2,1)S(1)}, u32[]{:S(2)}, u32[]{:S(2)}) %collective-permute-start.26) | collective-permute-done | bytes 131104 | tf_op jit(solution)/shard_map/ppermute | solution.py:218
  94.7 3.7 %collective-permute-done.28 = bf16[512,128]{1,0:T(8,128)(2,1)S(1)} collective-permute-done((bf16[512,128]{1,0:T(8,128)(2,1)S(1)}, bf16[512,128]{1,0:T(8,128)(2,1)S(1)}, u32[]{:S(2)}, u32[]{:S(2)}) %collective-permute-start.28) | collective-permute-done | bytes 131104 | tf_op jit(solution)/shard_map/ppermute | solution.py:218
  100.5 3.9 %collective-permute-done.29 = bf16[512,128]{1,0:T(8,128)(2,1)S(1)} collective-permute-done((bf16[512,128]{1,0:T(8,128)(2,1)S(1)}, bf16[512,128]{1,0:T(8,128)(2,1)S(1)}, u32[]{:S(2)}, u32[]{:S(2)}) %collective-permute-start.29) | collective-permute-done | bytes 131104 | tf_op jit(solution)/shard_map/ppermute | solution.py:218
  104.4 2.7 %collective-permute-done.25 = bf16[512,128]{1,0:T(8,128)(2,1)S(1)} collective-permute-done((bf16[512,128]{1,0:T(8,128)(2,1)S(1)}, bf16[512,128]{1,0:T(8,128)(2,1)S(1)}, u32[]{:S(2)}, u32[]{:S(2)}) %collective-permute-start.25) | collective-permute-done | bytes 131104 | tf_op jit(solution)/shard_map/ppermute | solution.py:218
  (49 shorter events, 18.3 us)
Async XLA Ops:
  0.6 3.4 %collective-permute-start = (f32[512]{0:T(512)}, f32[512]{0:T(512)S(1)}, u32[]{:S(2)}, u32[]{:S(2)}) collective-permute-start(f32[512]{0:T(512)} %param.8), channel_id=1, source_target_pairs={{0,8},{8,16},{16,24},{1,9},{9,17},{17,25},{2,10},{10,18},{18,26},{... | collective-permute-start | bytes 6152 | tf_op jit(solution)/shard_map/ppermute | solution.py:14
  5.1 8.0 %collective-permute-start.3 = (bf16[512,128]{1,0:T(8,128)(2,1)S(1)}, bf16[512,128]{1,0:T(8,128)(2,1)S(1)}, u32[]{:S(2)}, u32[]{:S(2)}) collective-permute-start(bf16[512,128]{1,0:T(8,128)(2,1)S(1)} %multiply_convert_fusion.refs_0_.refs_5_), channel_id=1, source_target_pairs={{0,6},{1,7},{2,4},{3,5},{4,2},{5,3},{6,0},{7,1},{8,14},{9,15},{10,... | collective-permute-start | bytes 393224 | tf_op jit(solution)/shard_map/ppermute | solution.py:218
  9.6 11.5 %collective-permute-start.2 = (bf16[512,128]{1,0:T(8,128)(2,1)S(1)}, bf16[512,128]{1,0:T(8,128)(2,1)S(1)}, u32[]{:S(2)}, u32[]{:S(2)}) collective-permute-start(bf16[512,128]{1,0:T(8,128)(2,1)S(1)} %multiply_convert_fusion.refs_0_.refs_5_), channel_id=1, source_target_pairs={{0,4},{1,5},{2,6},{3,7},{4,0},{5,1},{6,2},{7,3},{8,12},{9,13},{10,... | collective-permute-start | bytes 393224 | tf_op jit(solution)/shard_map/ppermute | solution.py:218
  9.6 13.0 %collective-permute-start.1 = (bf16[512,128]{1,0:T(8,128)(2,1)S(1)}, bf16[512,128]{1,0:T(8,128)(2,1)S(1)}, u32[]{:S(2)}, u32[]{:S(2)}) collective-permute-start(bf16[512,128]{1,0:T(8,128)(2,1)S(1)} %multiply_convert_fusion.refs_0_.refs_5_), channel_id=1, source_target_pairs={{0,2},{1,3},{2,0},{3,1},{4,6},{5,7},{6,4},{7,5},{8,10},{9,11},{10,... | collective-permute-start | bytes 393224 | tf_op jit(solution)/shard_map/ppermute | solution.py:218
  10.2 19.5 %collective-permute-start.4 = (bf16[512,128]{1,0:T(8,128)(2,1)S(1)}, bf16[512,128]{1,0:T(8,128)(2,1)S(1)}, u32[]{:S(2)}, u32[]{:S(2)}) collective-permute-start(bf16[512,128]{1,0:T(8,128)(2,1)S(1)} %multiply_convert_fusion.refs_0_.refs_5_), channel_id=1, source_target_pairs={{0,1},{1,0},{2,3},{3,2},{4,5},{5,4},{6,7},{7,6},{8,9},{9,8},{10,11... | collective-permute-start | bytes 393224 | tf_op jit(solution)/shard_map/ppermute | solution.py:218
  13.1 16.6 %collective-permute-start.7 = (bf16[512,128]{1,0:T(8,128)(2,1)S(1)}, bf16[512,128]{1,0:T(8,128)(2,1)S(1)}, u32[]{:S(2)}, u32[]{:S(2)}) collective-permute-start(bf16[512,128]{1,0:T(8,128)(2,1)S(1)} %collective-permute-done.3.refs_3_), channel_id=1, source_target_pairs={{0,1},{1,0},{2,3},{3,2},{4,5},{5,4},{6,7},{7,6},{8,9},{9,8},{10,11... | collective-permute-start | bytes 393224 | tf_op jit(solution)/shard_map/ppermute | solution.py:218
  21.1 8.6 %collective-permute-start.6 = (bf16[512,128]{1,0:T(8,128)(2,1)S(1)}, bf16[512,128]{1,0:T(8,128)(2,1)S(1)}, u32[]{:S(2)}, u32[]{:S(2)}) collective-permute-start(bf16[512,128]{1,0:T(8,128)(2,1)S(1)} %collective-permute-done.2.refs_2_), channel_id=1, source_target_pairs={{0,1},{1,0},{2,3},{3,2},{4,5},{5,4},{6,7},{7,6},{8,9},{9,8},{10,11... | collective-permute-start | bytes 393224 | tf_op jit(solution)/shard_map/ppermute | solution.py:218
  22.6 7.2 %collective-permute-start.5 = (bf16[512,128]{1,0:T(8,128)(2,1)S(1)}, bf16[512,128]{1,0:T(8,128)(2,1)S(1)}, u32[]{:S(2)}, u32[]{:S(2)}) collective-permute-start(bf16[512,128]{1,0:T(8,128)(2,1)S(1)} %collective-permute-done.1.refs_1_), channel_id=1, source_target_pairs={{0,1},{1,0},{2,3},{3,2},{4,5},{5,4},{6,7},{7,6},{8,9},{9,8},{10,11... | collective-permute-start | bytes 393224 | tf_op jit(solution)/shard_map/ppermute | solution.py:218
  29.8 1.2 %copy-start = (f32[512,128]{1,0:T(8,128)S(1)}, f32[512,128]{1,0:T(8,128)}, u32[]{:S(2)}) copy-start(f32[512,128]{1,0:T(8,128)} %refs_6_.1) | copy-start | bytes 786436
  34.9 11.0 %collective-permute-start.14 = (bf16[512,128]{1,0:T(8,128)(2,1)S(1)}, bf16[512,128]{1,0:T(8,128)(2,1)S(1)}, u32[]{:S(2)}, u32[]{:S(2)}) collective-permute-start(bf16[512,128]{1,0:T(8,128)(2,1)S(1)} %get-tuple-element.41), channel_id=1, source_target_pairs={{0,1},{1,0},{2,3},{3,2},{4,5},{5,4},{6,7},{7,6},{8,9},{9,8},{10,11... | collective-permute-start | bytes 393224 | tf_op jit(solution)/shard_map/ppermute | solution.py:218
  36.5 10.6 %collective-permute-start.12 = (bf16[512,128]{1,0:T(8,128)(2,1)S(1)}, bf16[512,128]{1,0:T(8,128)(2,1)S(1)}, u32[]{:S(2)}, u32[]{:S(2)}) collective-permute-start(bf16[512,128]{1,0:T(8,128)(2,1)S(1)} %get-tuple-element.39), channel_id=1, source_target_pairs={{0,1},{1,0},{2,3},{3,2},{4,5},{5,4},{6,7},{7,6},{8,9},{9,8},{10,11... | collective-permute-start | bytes 393224 | tf_op jit(solution)/shard_map/ppermute | solution.py:218
  37.0 12.0 %collective-permute-start.9 = (bf16[512,128]{1,0:T(8,128)(2,1)S(1)}, bf16[512,128]{1,0:T(8,128)(2,1)S(1)}, u32[]{:S(2)}, u32[]{:S(2)}) collective-permute-start(bf16[512,128]{1,0:T(8,128)(2,1)S(1)} %get-tuple-element.36), channel_id=1, source_target_pairs={{0,1},{1,0},{2,3},{3,2},{4,5},{5,4},{6,7},{7,6},{8,9},{9,8},{10,11... | collective-permute-start | bytes 393224 | tf_op jit(solution)/shard_map/ppermute | solution.py:218
  38.5 7.4 %collective-permute-start.10 = (f32[8,128]{1,0:T(8,128)S(1)}, f32[8,128]{1,0:T(8,128)S(1)}, u32[]{:S(2)}, u32[]{:S(2)}) collective-permute-start(f32[8,128]{1,0:T(8,128)S(1)} %get-tuple-element.37.mine.refs_7_), channel_id=1, source_target_pairs={{0,1},{1,0},{2,3},{3,2},{4,5},{5,4},{6,7},{7,6},{8,9},{9,8},{10,11... | collective-permute-start | bytes 12296 | tf_op jit(solution)/shard_map/ppermute | solution.py:218
  45.9 8.7 %collective-permute-start.15 = (bf16[528,128]{1,0:T(8,128)(2,1)S(1)}, bf16[528,128]{1,0:T(8,128)(2,1)S(1)}, u32[]{:S(2)}, u32[]{:S(2)}) collective-permute-start(bf16[528,128]{1,0:T(8,128)(2,1)S(1)} %shard_map.92), channel_id=1, source_target_pairs={{0,2},{1,3},{2,0},{3,1},{4,6},{5,7},{6,4},{7,5},{8,10},{9,11},{10,... | collective-permute-start | bytes 405512 | tf_op jit(solution)/shard_map/ppermute | solution.py:218
  47.1 9.2 %collective-permute-start.13 = (bf16[528,128]{1,0:T(8,128)(2,1)S(1)}, bf16[528,128]{1,0:T(8,128)(2,1)S(1)}, u32[]{:S(2)}, u32[]{:S(2)}) collective-permute-start(bf16[528,128]{1,0:T(8,128)(2,1)S(1)} %shard_map.91), channel_id=1, source_target_pairs={{0,6},{1,7},{2,4},{3,5},{4,2},{5,3},{6,0},{7,1},{8,14},{9,15},{10,... | collective-permute-start | bytes 405512 | tf_op jit(solution)/shard_map/ppermute | solution.py:218
  49.0 12.2 %collective-permute-start.11 = (bf16[528,128]{1,0:T(8,128)(2,1)S(1)}, bf16[528,128]{1,0:T(8,128)(2,1)S(1)}, u32[]{:S(2)}, u32[]{:S(2)}) collective-permute-start(bf16[528,128]{1,0:T(8,128)(2,1)S(1)} %shard_map.90), channel_id=1, source_target_pairs={{0,4},{1,5},{2,6},{3,7},{4,0},{5,1},{6,2},{7,3},{8,12},{9,13},{10,... | collective-permute-start | bytes 405512 | tf_op jit(solution)/shard_map/ppermute | solution.py:218
  49.7 5.0 %collective-permute-start.8 = (bf16[512,128]{1,0:T(8,128)(2,1)S(1)}, bf16[512,128]{1,0:T(8,128)(2,1)S(1)}, u32[]{:S(2)}, u32[]{:S(2)}) collective-permute-start(bf16[512,128]{1,0:T(8,128)(2,1)S(1)} %get-tuple-element.34), channel_id=1, source_target_pairs={{0,1},{1,0},{2,3},{3,2},{4,5},{5,4},{6,7},{7,6},{8,9},{9,8},{10,11... | collective-permute-start | bytes 393224 | tf_op jit(solution)/shard_map/ppermute | solution.py:218
  61.5 8.2 %collective-permute-start.18 = (bf16[512,128]{1,0:T(8,128)(2,1)S(1)}, bf16[512,128]{1,0:T(8,128)(2,1)S(1)}, u32[]{:S(2)}, u32[]{:S(2)}) collective-permute-start(bf16[512,128]{1,0:T(8,128)(2,1)S(1)} %get-tuple-element.43.refs_0_), channel_id=1, source_target_pairs={{0,6},{1,7},{2,4},{3,5},{4,2},{5,3},{6,0},{7,1},{8,14},{9,15},{10,... | collective-permute-start | bytes 393224 | tf_op jit(solution)/shard_map/ppermute | solution.py:218
  63.6 10.0 %collective-permute-start.17 = (bf16[512,128]{1,0:T(8,128)(2,1)S(1)}, bf16[512,128]{1,0:T(8,128)(2,1)S(1)}, u32[]{:S(2)}, u32[]{:S(2)}) collective-permute-start(bf16[512,128]{1,0:T(8,128)(2,1)S(1)} %get-tuple-element.43.refs_0_), channel_id=1, source_target_pairs={{0,4},{1,5},{2,6},{3,7},{4,0},{5,1},{6,2},{7,3},{8,12},{9,13},{10,... | collective-permute-start | bytes 393224 | tf_op jit(solution)/shard_map/ppermute | solution.py:218
  63.6 11.6 %collective-permute-start.16 = (bf16[512,128]{1,0:T(8,128)(2,1)S(1)}, bf16[512,128]{1,0:T(8,128)(2,1)S(1)}, u32[]{:S(2)}, u32[]{:S(2)}) collective-permute-start(bf16[512,128]{1,0:T(8,128)(2,1)S(1)} %get-tuple-element.43.refs_0_), channel_id=1, source_target_pairs={{0,2},{1,3},{2,0},{3,1},{4,6},{5,7},{6,4},{7,5},{8,10},{9,11},{10,... | collective-permute-start | bytes 393224 | tf_op jit(solution)/shard_map/ppermute | solution.py:218
  65.9 9.8 %collective-permute-start.19 = (bf16[512,128]{1,0:T(8,128)(2,1)S(1)}, bf16[512,128]{1,0:T(8,128)(2,1)S(1)}, u32[]{:S(2)}, u32[]{:S(2)}) collective-permute-start(bf16[512,128]{1,0:T(8,128)(2,1)S(1)} %get-tuple-element.43.refs_0_), channel_id=1, source_target_pairs={{0,1},{1,0},{2,3},{3,2},{4,5},{5,4},{6,7},{7,6},{8,9},{9,8},{10,11... | collective-permute-start | bytes 393224 | tf_op jit(solution)/shard_map/ppermute | solution.py:218
  69.7 6.0 %collective-permute-start.22 = (bf16[512,128]{1,0:T(8,128)(2,1)S(1)}, bf16[512,128]{1,0:T(8,128)(2,1)S(1)}, u32[]{:S(2)}, u32[]{:S(2)}) collective-permute-start(bf16[512,128]{1,0:T(8,128)(2,1)S(1)} %collective-permute-done.18.refs_3_), channel_id=1, source_target_pairs={{0,1},{1,0},{2,3},{3,2},{4,5},{5,4},{6,7},{7,6},{8,9},{9,8},{10,11... | collective-permute-start | bytes 393224 | tf_op jit(solution)/shard_map/ppermute | solution.py:218
  73.6 6.4 %collective-permute-start.21 = (bf16[512,128]{1,0:T(8,128)(2,1)S(1)}, bf16[512,128]{1,0:T(8,128)(2,1)S(1)}, u32[]{:S(2)}, u32[]{:S(2)}) collective-permute-start(bf16[512,128]{1,0:T(8,128)(2,1)S(1)} %collective-permute-done.17.refs_2_), channel_id=1, source_target_pairs={{0,1},{1,0},{2,3},{3,2},{4,5},{5,4},{6,7},{7,6},{8,9},{9,8},{10,11... | collective-permute-start | bytes 393224 | tf_op jit(solution)/shard_map/ppermute | solution.py:218
  75.2 6.6 %collective-permute-start.20 = (bf16[512,128]{1,0:T(8,128)(2,1)S(1)}, bf16[512,128]{1,0:T(8,128)(2,1)S(1)}, u32[]{:S(2)}, u32[]{:S(2)}) collective-permute-start(bf16[512,128]{1,0:T(8,128)(2,1)S(1)} %collective-permute-done.16.refs_1_), channel_id=1, source_target_pairs={{0,1},{1,0},{2,3},{3,2},{4,5},{5,4},{6,7},{7,6},{8,9},{9,8},{10,11... | collective-permute-start | bytes 393224 | tf_op jit(solution)/shard_map/ppermute | solution.py:218
  86.8 6.4 %collective-permute-start.26 = (bf16[512,128]{1,0:T(8,128)(2,1)S(1)}, bf16[512,128]{1,0:T(8,128)(2,1)S(1)}, u32[]{:S(2)}, u32[]{:S(2)}) collective-permute-start(bf16[512,128]{1,0:T(8,128)(2,1)S(1)} %get-tuple-element.50), channel_id=1, source_target_pairs={{0,1},{1,0},{2,3},{3,2},{4,5},{5,4},{6,7},{7,6},{8,9},{9,8},{10,11... | collective-permute-start | bytes 393224 | tf_op jit(solution)/shard_map/ppermute | solution.py:218
  88.4 12.1 %collective-permute-start.23 = (bf16[512,128]{1,0:T(8,128)(2,1)S(1)}, bf16[512,128]{1,0:T(8,128)(2,1)S(1)}, u32[]{:S(2)}, u32[]{:S(2)}) collective-permute-start(bf16[512,128]{1,0:T(8,128)(2,1)S(1)} %get-tuple-element.46), channel_id=1, source_target_pairs={{0,1},{1,0},{2,3},{3,2},{4,5},{5,4},{6,7},{7,6},{8,9},{9,8},{10,11... | collective-permute-start | bytes 393224 | tf_op jit(solution)/shard_map/ppermute | solution.py:218
  88.9 9.5 %collective-permute-start.28 = (bf16[512,128]{1,0:T(8,128)(2,1)S(1)}, bf16[512,128]{1,0:T(8,128)(2,1)S(1)}, u32[]{:S(2)}, u32[]{:S(2)}) collective-permute-start(bf16[512,128]{1,0:T(8,128)(2,1)S(1)} %get-tuple-element.52), channel_id=1, source_target_pairs={{0,1},{1,0},{2,3},{3,2},{4,5},{5,4},{6,7},{7,6},{8,9},{9,8},{10,11... | collective-permute-start | bytes 393224 | tf_op jit(solution)/shard_map/ppermute | solution.py:218
  90.4 9.4 %collective-permute-start.24 = (bf16[512,128]{1,0:T(8,128)(2,1)S(1)}, bf16[512,128]{1,0:T(8,128)(2,1)S(1)}, u32[]{:S(2)}, u32[]{:S(2)}) collective-permute-start(bf16[512,128]{1,0:T(8,128)(2,1)S(1)} %get-tuple-element.48), channel_id=1, source_target_pairs={{0,1},{1,0},{2,3},{3,2},{4,5},{5,4},{6,7},{7,6},{8,9},{9,8},{10,11... | collective-permute-start | bytes 393224 | tf_op jit(solution)/shard_map/ppermute | solution.py:218
  93.3 7.3 %collective-permute-start.27 = (bf16[512,128]{1,0:T(8,128)(2,1)S(1)}, bf16[512,128]{1,0:T(8,128)(2,1)S(1)}, u32[]{:S(2)}, u32[]{:S(2)}) collective-permute-start(bf16[512,128]{1,0:T(8,128)(2,1)S(1)} %add_convert_fusion.1), channel_id=1, source_target_pairs={{0,6},{1,7},{2,4},{3,5},{4,2},{5,3},{6,0},{7,1},{8,14},{9,15},{10,... | collective-permute-start | bytes 393224 | tf_op jit(solution)/shard_map/ppermute | solution.py:218
  98.4 6.0 %collective-permute-start.29 = (bf16[512,128]{1,0:T(8,128)(2,1)S(1)}, bf16[512,128]{1,0:T(8,128)(2,1)S(1)}, u32[]{:S(2)}, u32[]{:S(2)}) collective-permute-start(bf16[512,128]{1,0:T(8,128)(2,1)S(1)} %add_convert_fusion), channel_id=1, source_target_pairs={{0,2},{1,3},{2,0},{3,1},{4,6},{5,7},{6,4},{7,5},{8,10},{9,11},{10,... | collective-permute-start | bytes 393224 | tf_op jit(solution)/shard_map/ppermute | solution.py:218
  99.8 7.3 %collective-permute-start.25 = (bf16[512,128]{1,0:T(8,128)(2,1)S(1)}, bf16[512,128]{1,0:T(8,128)(2,1)S(1)}, u32[]{:S(2)}, u32[]{:S(2)}) collective-permute-start(bf16[512,128]{1,0:T(8,128)(2,1)S(1)} %add_convert_fusion.2), channel_id=1, source_target_pairs={{0,4},{1,5},{2,6},{3,7},{4,0},{5,1},{6,2},{7,3},{8,12},{9,13},{10,... | collective-permute-start | bytes 393224 | tf_op jit(solution)/shard_map/ppermute | solution.py:218

commit v2 on v1

--- a/solution.py
+++ b/solution.py
@@ -87,15 +87,17 @@
     return jnp.sum((total * own).reshape(-1, 8, total.shape[1]), axis=0)
 
 
-def first_kernel(line, first, dots, place, links, left, right, *refs):
-    npiece = 2 * line
+TAIL = 16
+
+
+def first_kernel(offsets, first, dots, place, links, left, right, *refs):
+    npiece = len(offsets)
     pieces, vector, outs = refs[:npiece], refs[npiece], refs[npiece + 1 :]
     rows, width = pieces[0].shape
-    for p in range(npiece):
-        chunk = place[0] ^ (2 * (p % line)) ^ (p // line)
-        vector[rows_at(chunk, rows), :] = pieces[p][...]
+    for piece, offset in zip(pieces, offsets):
+        vector[rows_at(place[0] ^ offset, rows), :] = piece[...]
     vector[npiece * rows :, :] = jnp.zeros((width, width), vector.dtype)
-    chunks = [place[0] ^ (2 * d) ^ 1 for d in first]
+    chunks = [place[0] ^ offset for offset in first]
     if dots:
         outs[-1][...] = jnp.zeros_like(outs[-1])
 
@@ -109,19 +111,29 @@
     scaled_products(vector, links, left, right, chunks, rows // width, store)
 
 
-def second_kernel(line, rest, dots, place, links, left, right, vector, *refs):
+def three_roundings(part):
+    row = lax.broadcasted_iota(jnp.int32, (TAIL, part.shape[1]), 0)
+    tail = jnp.zeros((TAIL, part.shape[1]), jnp.float32)
+    for r in range(3):
+        rounded = part.astype(jnp.bfloat16).astype(jnp.float32)
+        tail = jnp.where(row == r, rounded, tail)
+        part = part - rounded
+    return tail.astype(jnp.bfloat16)
+
+
+def second_kernel(rest, dots, place, links, left, right, vector, *refs):
     width = vector.shape[1]
     if dots:
         hdiag, before, *outs, numer, denom = refs
         rows = hdiag.shape[0]
         own = vector[rows_at(place[0], rows), :].astype(jnp.float32)
         numer[...] = before[...] + squares(hdiag[...] * own, own)
-        whole = vector[: 2 * line * rows, :].astype(jnp.float32)
+        whole = vector[: vector.shape[0] - width, :].astype(jnp.float32)
         denom[...] = squares(whole, whole)
     else:
         outs = refs
         rows = outs[0].shape[0]
-    chunks = [place[0] ^ (2 * d) ^ 1 for d in rest] + [place[0] ^ (2 * d) for d in range(line)]
+    chunks = [place[0] ^ offset for offset in rest]
 
     def store(t, i, sums):
         at = slice(i * width, (i + 1) * width)
@@ -131,33 +143,38 @@
             numer[...] += squares(sums, vector[pl.ds(start, width), :].astype(jnp.float32))
 
     scaled_products(vector, links, left, right, chunks, rows // width, store)
-
-
-TAIL = 16
-
-
-def pass_kernel(kept, came, mine, other, out):
-    rows, width = kept.shape
-    out[:rows, :] = (kept[...] + came[...].astype(jnp.float32)).astype(out.dtype)
-    part = jnp.sum(mine[...] + other[...], axis=0, keepdims=True)
-    row = lax.broadcasted_iota(jnp.int32, (TAIL, width), 0)
-    tail = jnp.zeros((TAIL, width), jnp.float32)
-    for r in range(3):
-        rounded = part.astype(out.dtype).astype(jnp.float32)
-        tail = jnp.where(row == r, rounded, tail)
-        part = part - rounded
-    out[rows:, :] = tail.astype(out.dtype)
+    if dots:
+        tail = three_roundings(jnp.sum(numer[...], axis=0, keepdims=True))
+        for out in outs:
+            if out.shape[0] > rows:
+                out[rows:, :] = tail
+
+
+def added_kernel(kept, *refs):
+    out = refs[-1]
+    total = kept[...]
+    for came in refs[:-1]:
+        total = total + came[...].astype(jnp.float32)
+    out[...] = total.astype(out.dtype)
+
+
+def half_kernel(numer, *refs):
+    out = refs[-1]
+    total = jnp.sum(numer[...], axis=0, keepdims=True)
+    for came in refs[:-1]:
+        rows = came.shape[0] - TAIL
+        total = total + jnp.sum(came[rows:, :].astype(jnp.float32), axis=0, keepdims=True)
+    out[...] = jnp.broadcast_to(total, out.shape)
 
 
 def correct_kernel(nmore, *refs):
-    kept, came, more, refs = refs[0], refs[1], refs[2 : 2 + nmore], refs[2 + nmore :]
+    kept, more, refs = refs[0], refs[1 : 1 + nmore], refs[1 + nmore :]
     psi, hdiag, mine, other, denom, correction, theta = refs
     rows = psi.shape[0]
-    total = kept[...] + came[...].astype(jnp.float32)
-    numer = jnp.sum(mine[...] + other[...], keepdims=True)
+    total = kept[...]
     for m in more:
         total = total + m[:rows, :].astype(jnp.float32)
-        numer = numer + jnp.sum(m[rows:, :].astype(jnp.float32), keepdims=True)
+    numer = jnp.sum(mine[:1, :] + other[:1, :], keepdims=True)
     quotient = numer / jnp.sum(denom[...], keepdims=True)
     vector = psi[...].astype(jnp.float32)
     sigma = total + hdiag[...] * vector
@@ -199,84 +216,77 @@
     )(pltpu.with_memory_space_constraint(operators, pltpu.HBM))
 
 
-def far_first(line):
-    return sorted(range(line), key=lambda d: -d.bit_length())
+def within(half):
+    return sorted(range(1, half), key=lambda r: (-r.bit_count(), r))
 
 
 def paired_body(amat, lam, hdiag, left_ops, right_operators, couple, blockmask):
     rows, width = amat.shape
     nsector = couple.shape[2]
     devices = lax.axis_size("ops")
-    line = devices // 2
+    half = devices // 2
+    inside = within(half)
     place = lax.axis_index("ops").astype(jnp.int32).reshape(1)
     links = jnp.where(blockmask[0] != 0, couple[0], nsector).reshape(-1)
     shape = jax.ShapeDtypeStruct
     tile = shape((8, width), jnp.float32)
     sent, kept = shape((rows, width), jnp.bfloat16), shape((rows, width), jnp.float32)
+    tailed = shape((rows + TAIL, width), jnp.bfloat16)
 
     def exchange(array, by):
         return lax.ppermute(array, "ops", [(o, o ^ by) for o in range(devices)])
 
-    far = far_first(line)
-    first, rest = far[:1], far[1:]
-
     def gather(piece):
-        column = {0: piece}
-        for d in far:
-            if d:
-                column[d] = exchange(piece, 2 * d)
-        other = {d: exchange(column[d], 1) for d in range(line)}
-        return [column[d] for d in range(line)] + [other[d] for d in range(line)]
+        pieces = {0: piece, half: exchange(piece, half)}
+        for r in inside:
+            pieces[r] = exchange(piece, r)
+        for r in inside:
+            pieces[half ^ r] = exchange(pieces[half], r)
+        return pieces
 
     def apply_terms(piece, left, right, dots):
         left = pltpu.with_memory_space_constraint(left, pltpu.VMEM)
         right = pltpu.with_memory_space_constraint(right, pltpu.VMEM)
         pieces = gather(piece)
+        first = [half ^ r for r in inside]
+        rest = inside + [half, 0]
         whole = shape((devices * rows + width, width), jnp.bfloat16)
         vector, *lead = on_chip(
-            partial(first_kernel, line, first, dots),
+            partial(first_kernel, list(pieces), first, dots),
             [whole] + [sent] * len(first) + [tile] * dots,
-            2, place, links, left, right, *pieces,
+            2, place, links, left, right, *pieces.values(),
         )
         extra = (hdiag, lead[-1]) if dots else ()
         outs = on_chip(
-            partial(second_kernel, line, rest, dots),
-            [sent] * len(rest) + [kept] * line + [tile] * (2 * dots),
+            partial(second_kernel, rest, dots),
+            [tailed if dots else sent] * len(inside) + [kept] * 2 + [tile] * (2 * dots),
             2, place, links, left, right, vector, *extra,
         )
-        leave = dict(zip(first + rest, lead[: len(first)] + outs[: len(rest)]))
-        stay = outs[len(rest) : len(rest) + line]
-        sums = ()
+        crossing, own, *sums = outs[len(inside) :]
+        came = [exchange(chunk, r) for r, chunk in zip(inside, lead)]
+        ours = [exchange(chunk, r) for r, chunk in zip(inside, outs)]
+        theirs = exchange(on_chip(added_kernel, [sent], 0, crossing, *came)[0], half)
         if dots:
-            mine, denom = outs[len(rest) + line :]
-            other = exchange(mine, 1)
-            sums = (mine, other, denom)
-        came = {d: exchange(leave[d], 1) for d in far}
-        more = []
-        for d in far:
-            if d and dots:
-                message = on_chip(pass_kernel, [shape((rows + TAIL, width), jnp.bfloat16)], 0, stay[d], came[d], mine, other)[0]
-            elif d:
-                message = (stay[d] + came[d].astype(jnp.float32)).astype(jnp.bfloat16)
-            if d:
-                more.append(exchange(message, 2 * d))
-        return [stay[0], came[0]] + more, sums
-
-    links, left_ops, right_operators = lax.optimization_barrier((links, left_ops, right_operators))
+            numer, denom = sums
+            mine = on_chip(half_kernel, [tile], 0, numer, *ours)[0]
+            sums = [mine, exchange(mine, half), denom]
+        return [own, *ours, theirs], sums
+
+    place, links, left_ops, right_operators = lax.optimization_barrier((place, links, left_ops, right_operators))
     left = loaded(left_ops)
     right = loaded(right_operators)
     earlier = shifted(lam, "seg", 1)
     weights = jnp.where(lax.axis_index("seg") == 0, jnp.ones_like(earlier), earlier)
     psi = (weights[:, None] * amat.astype(jnp.float32)).astype(jnp.bfloat16)
     terms, sums = apply_terms(psi, left, right, True)
-    correction, theta = on_chip(partial(correct_kernel, line - 1), [sent, tile], 0, *terms, psi, hdiag, *sums)
+    correction, theta = on_chip(partial(correct_kernel, half), [sent, tile], 0, *terms, psi, hdiag, *sums)
     terms, _ = apply_terms(correction, left, right, False)
     sigma_two = sum(t.astype(jnp.float32) for t in terms) + hdiag * correction.astype(jnp.float32)
     return (sigma_two, theta[0, :1])
 
 
 def is_paired(devices, nsector):
-    return devices >= 2 and devices & (devices - 1) == 0 and nsector % devices == 0
+    return devices >= 4 and devices & (devices - 1) == 0 and nsector % devices == 0
 
 
 def body(amat, lam, hdiag, left_ops, right_operators, couple, blockmask):

time: 108 us -> 86.4 us (0.80)
  waiting for transfers between devices: 50.1 us -> 25.7 us
  starting transfers between devices: 37.8 us -> 40.4 us
    ppermute x29, waiting for transfers between devices: 49.1 us -> 24.7 us  [exchange(): return lax.ppermute(array, 'ops', [(o, o ^ by) for o in range(devices)])]
    ppermute x29, starting transfers between devices: 35.4 us -> 38 us  [exchange(): return lax.ppermute(array, 'ops', [(o, o ^ by) for o in range(devices)])]
  transfers between devices with their start and end apart: 30 -> 30, of which waited for: 17 -> 16; matrix products, arithmetic and copies ran while one was open for 1% -> 2% of each run, Pallas kernels for 5% -> 14%
where the time goes in v2:
time: 86.4 us; the launch traced here: 86.2 us
  starting transfers between devices  40.4 us (47%)
  waiting for transfers between devices  25.7 us (30%)
  Pallas kernels  16.1 us (19%)
  other arithmetic  2.55 us (3%)
    ppermute x29, starting transfers between devices, exchange(): return lax.ppermute(array, 'ops', [(o, o ^ by) for o in range(devices)])  38 us
    ppermute x29, waiting for transfers between devices, exchange(): return lax.ppermute(array, 'ops', [(o, o ^ by) for o in range(devices)])  24.7 us
    pallas_call x8, Pallas kernels, on_chip(): pl.pallas_call(kernel, out_shape=out_shape, in_specs=[SMEM] * nscalar + [...  10.4 us
    pallas_call x2, Pallas kernels, loaded(): pl.pallas_call(load_kernel, out_shape=pltpu.VMEM(operators.shape, operato...  5.71 us
    ppermute x1, starting transfers between devices, shifted(): return lax.ppermute(array, axis, pairs)  2.4 us
  transfers between devices with their start and end apart: 30, of which 16 were waited for; matrix products, arithmetic and copies ran while one was open for 2% of the time, Pallas kernels for 14%

profile of v2, /device:TPU:0, one launch (start us, length us, event | category | flops | bytes accessed | tf_op | source)
XLA Modules:
  0.0 86.2 jit_solution(6356085102203418405)
XLA Ops:
  0.6 2.4 %collective-permute-start = (f32[512]{0:T(512)}, f32[512]{0:T(512)S(1)}, u32[]{:S(2)}, u32[]{:S(2)}) collective-permute-start(f32[512]{0:T(512)} %param.8), channel_id=1, source_target_pairs={{0,8},{8,16},{16,24},{1,9},{9,17},{17,25},{2,10},{10,18},{18,26},{... | collective-permute-start | bytes 6152 | tf_op jit(solution)/shard_map/ppermute | solution.py:14
  5.1 3.5 %collective-permute-start.1 = (bf16[512,128]{1,0:T(8,128)(2,1)S(1)}, bf16[512,128]{1,0:T(8,128)(2,1)S(1)}, u32[]{:S(2)}, u32[]{:S(2)}) collective-permute-start(bf16[512,128]{1,0:T(8,128)(2,1)S(1)} %multiply_convert_fusion.refs_0_.refs_5_), channel_id=1, source_target_pairs={{0,4},{1,5},{2,6},{3,7},{4,0},{5,1},{6,2},{7,3},{8,12},{9,13},{10,... | collective-permute-start | bytes 393224 | tf_op jit(solution)/shard_map/ppermute | solution.py:237
  8.6 1.6 %collective-permute-start.4 = (bf16[512,128]{1,0:T(8,128)(2,1)S(1)}, bf16[512,128]{1,0:T(8,128)(2,1)S(1)}, u32[]{:S(2)}, u32[]{:S(2)}) collective-permute-start(bf16[512,128]{1,0:T(8,128)(2,1)S(1)} %multiply_convert_fusion.refs_0_.refs_5_), channel_id=1, source_target_pairs={{0,2},{1,3},{2,0},{3,1},{4,6},{5,7},{6,4},{7,5},{8,10},{9,11},{10,... | collective-permute-start | bytes 393224 | tf_op jit(solution)/shard_map/ppermute | solution.py:237
  10.1 1.5 %collective-permute-start.3 = (bf16[512,128]{1,0:T(8,128)(2,1)S(1)}, bf16[512,128]{1,0:T(8,128)(2,1)S(1)}, u32[]{:S(2)}, u32[]{:S(2)}) collective-permute-start(bf16[512,128]{1,0:T(8,128)(2,1)S(1)} %multiply_convert_fusion.refs_0_.refs_5_), channel_id=1, source_target_pairs={{0,1},{1,0},{2,3},{3,2},{4,5},{5,4},{6,7},{7,6},{8,9},{9,8},{10,11... | collective-permute-start | bytes 393224 | tf_op jit(solution)/shard_map/ppermute | solution.py:237
  12.1 2.3 %collective-permute-done.1.refs_1_ = bf16[512,128]{1,0:T(8,128)(2,1)S(1)} collective-permute-done((bf16[512,128]{1,0:T(8,128)(2,1)S(1)}, bf16[512,128]{1,0:T(8,128)(2,1)S(1)}, u32[]{:S(2)}, u32[]{:S(2)}) %collective-permute-start.1) | collective-permute-done | bytes 131104 | tf_op jit(solution)/shard_map/ppermute | solution.py:237
  14.3 2.4 %collective-permute-start.7 = (bf16[512,128]{1,0:T(8,128)(2,1)S(1)}, bf16[512,128]{1,0:T(8,128)(2,1)S(1)}, u32[]{:S(2)}, u32[]{:S(2)}) collective-permute-start(bf16[512,128]{1,0:T(8,128)(2,1)S(1)} %collective-permute-done.1.refs_1_), channel_id=1, source_target_pairs={{0,2},{1,3},{2,0},{3,1},{4,6},{5,7},{6,4},{7,5},{8,10},{9,11},{10,... | collective-permute-start | bytes 393224 | tf_op jit(solution)/shard_map/ppermute | solution.py:237
  16.7 1.5 %collective-permute-start.6 = (bf16[512,128]{1,0:T(8,128)(2,1)S(1)}, bf16[512,128]{1,0:T(8,128)(2,1)S(1)}, u32[]{:S(2)}, u32[]{:S(2)}) collective-permute-start(bf16[512,128]{1,0:T(8,128)(2,1)S(1)} %collective-permute-done.1.refs_1_), channel_id=1, source_target_pairs={{0,1},{1,0},{2,3},{3,2},{4,5},{5,4},{6,7},{7,6},{8,9},{9,8},{10,11... | collective-permute-start | bytes 393224 | tf_op jit(solution)/shard_map/ppermute | solution.py:237
  19.2 2.9 %shard_map.86.left = bf16[1,6,4096,128]{3,2,1,0:T(8,128)(2,1)S(1)} custom-call(bf16[1,6,4096,128]{3,2,1,0:T(8,128)(2,1)} %source), custom_call_target="tpu_custom_call" | custom-call | tf_op jit(solution)/shard_map/pallas_call | solution.py:209
  22.1 2.9 %shard_map.87.right = bf16[1,6,4096,128]{3,2,1,0:T(8,128)(2,1)S(1)} custom-call(bf16[1,6,4096,128]{3,2,1,0:T(8,128)(2,1)} %source.1), custom_call_target="tpu_custom_call" | custom-call | tf_op jit(solution)/shard_map/pallas_call | solution.py:209
  25.6 2.1 %shard_map.88 = (bf16[4224,128]{1,0:T(8,128)(2,1)S(1)}, bf16[512,128]{1,0:T(8,128)(2,1)S(1)}, bf16[512,128]{1,0:T(8,128)(2,1)S(1)}, bf16[512,128]{1,0:T(8,128)(2,1)S(1)}, f32[8,128]{1,0:T(8,128)S(1)}) custom-call(s32[1]{0:T(128)} %bitcast.place, s32[192]{0:T(256)S(1)} %select_n.17.links, bf16[1,6,4096,128]{3,2,1,0:T(8,128)(2,1)S(1)} %shard_map.86.left, ...), custom_call_target="tpu_custom_call" | custom-call | tf_op jit(solution)/shard_map/pallas_call | solution.py:198
  27.7 2.2 %collective-permute-start.11 = (bf16[512,128]{1,0:T(8,128)(2,1)S(1)}, bf16[512,128]{1,0:T(8,128)(2,1)S(1)}, u32[]{:S(2)}, u32[]{:S(2)}) collective-permute-start(bf16[512,128]{1,0:T(8,128)(2,1)S(1)} %get-tuple-element.40), channel_id=1, source_target_pairs={{0,3},{1,2},{2,1},{3,0},{4,7},{5,6},{6,5},{7,4},{8,11},{9,10},{10,... | collective-permute-start | bytes 393224 | tf_op jit(solution)/shard_map/ppermute | solution.py:237
  31.2 3.0 %shard_map.89 = (bf16[528,128]{1,0:T(8,128)(2,1)S(1)}, bf16[528,128]{1,0:T(8,128)(2,1)S(1)}, bf16[528,128]{1,0:T(8,128)(2,1)S(1)}, f32[512,128]{1,0:T(8,128)S(1)...) custom-call(s32[1]{0:T(128)} %bitcast.place, s32[192]{0:T(256)S(1)} %select_n.17.links, ...), custom_call_target="tpu_custom_call" | custom-call | tf_op jit(solution)/shard_map/pallas_call | solution.py:198
  34.2 2.2 %collective-permute-start.8 = (bf16[528,128]{1,0:T(8,128)(2,1)S(1)}, bf16[528,128]{1,0:T(8,128)(2,1)S(1)}, u32[]{:S(2)}, u32[]{:S(2)}) collective-permute-start(bf16[528,128]{1,0:T(8,128)(2,1)S(1)} %get-tuple-element.36), channel_id=1, source_target_pairs={{0,3},{1,2},{2,1},{3,0},{4,7},{5,6},{6,5},{7,4},{8,11},{9,10},{10,... | collective-permute-start | bytes 405512 | tf_op jit(solution)/shard_map/ppermute | solution.py:237
  37.8 2.8 %collective-permute-start.14 = (bf16[512,128]{1,0:T(8,128)(2,1)S(1)}, bf16[512,128]{1,0:T(8,128)(2,1)S(1)}, u32[]{:S(2)}, u32[]{:S(2)}) collective-permute-start(bf16[512,128]{1,0:T(8,128)(2,1)S(1)} %shard_map.90), channel_id=1, source_target_pairs={{0,4},{1,5},{2,6},{3,7},{4,0},{5,1},{6,2},{7,3},{8,12},{9,13},{10,... | collective-permute-start | bytes 393224 | tf_op jit(solution)/shard_map/ppermute | solution.py:237
  40.7 2.4 %collective-permute-done.8.refs_0_.refs_1_ = bf16[528,128]{1,0:T(8,128)(2,1)S(1)} collective-permute-done((bf16[528,128]{1,0:T(8,128)(2,1)S(1)}, bf16[528,128]{1,0:T(8,128)(2,1)S(1)}, u32[]{:S(2)}, u32[]{:S(2)}) %collective-permute-start.8) | collective-permute-done | bytes 135200 | tf_op jit(solution)/shard_map/ppermute | solution.py:237
  43.0 2.5 %collective-permute-done.10.refs_2_.refs_3_ = bf16[528,128]{1,0:T(8,128)(2,1)S(1)} collective-permute-done((bf16[528,128]{1,0:T(8,128)(2,1)S(1)}, bf16[528,128]{1,0:T(8,128)(2,1)S(1)}, u32[]{:S(2)}, u32[]{:S(2)}) %collective-permute-start.10) | collective-permute-done | bytes 135200 | tf_op jit(solution)/shard_map/ppermute | solution.py:237
  45.5 1.2 %collective-permute-start.15 = (f32[8,128]{1,0:T(8,128)S(1)}, f32[8,128]{1,0:T(8,128)S(1)}, u32[]{:S(2)}, u32[]{:S(2)}) collective-permute-start(f32[8,128]{1,0:T(8,128)S(1)} %shard_map.91.refs_7_), channel_id=1, source_target_pairs={{0,4},{1,5},{2,6},{3,7},{4,0},{5,1},{6,2},{7,3},{8,12},{9,13},{10,... | collective-permute-start | bytes 12296 | tf_op jit(solution)/shard_map/ppermute | solution.py:237
  46.7 3.4 %collective-permute-done.15.refs_8_ = f32[8,128]{1,0:T(8,128)S(1)} collective-permute-done((f32[8,128]{1,0:T(8,128)S(1)}, f32[8,128]{1,0:T(8,128)S(1)}, u32[]{:S(2)}, u32[]{:S(2)}) %collective-permute-start.15) | collective-permute-done | bytes 4128 | tf_op jit(solution)/shard_map/ppermute | solution.py:237
  50.3 1.2 %collective-permute-start.16 = (bf16[512,128]{1,0:T(8,128)(2,1)S(1)}, bf16[512,128]{1,0:T(8,128)(2,1)S(1)}, u32[]{:S(2)}, u32[]{:S(2)}) collective-permute-start(bf16[512,128]{1,0:T(8,128)(2,1)S(1)} %get-tuple-element.45.refs_0_), channel_id=1, source_target_pairs={{0,4},{1,5},{2,6},{3,7},{4,0},{5,1},{6,2},{7,3},{8,12},{9,13},{10,... | collective-permute-start | bytes 393224 | tf_op jit(solution)/shard_map/ppermute | solution.py:237
  51.5 2.1 %collective-permute-start.19 = (bf16[512,128]{1,0:T(8,128)(2,1)S(1)}, bf16[512,128]{1,0:T(8,128)(2,1)S(1)}, u32[]{:S(2)}, u32[]{:S(2)}) collective-permute-start(bf16[512,128]{1,0:T(8,128)(2,1)S(1)} %get-tuple-element.45.refs_0_), channel_id=1, source_target_pairs={{0,2},{1,3},{2,0},{3,1},{4,6},{5,7},{6,4},{7,5},{8,10},{9,11},{10,... | collective-permute-start | bytes 393224 | tf_op jit(solution)/shard_map/ppermute | solution.py:237
  53.6 1.5 %collective-permute-start.17 = (bf16[512,128]{1,0:T(8,128)(2,1)S(1)}, bf16[512,128]{1,0:T(8,128)(2,1)S(1)}, u32[]{:S(2)}, u32[]{:S(2)}) collective-permute-start(bf16[512,128]{1,0:T(8,128)(2,1)S(1)} %get-tuple-element.45.refs_0_), channel_id=1, source_target_pairs={{0,3},{1,2},{2,1},{3,0},{4,7},{5,6},{6,5},{7,4},{8,11},{9,10},{10,... | collective-permute-start | bytes 393224 | tf_op jit(solution)/shard_map/ppermute | solution.py:237
  55.0 2.6 %collective-permute-done.16.refs_1_ = bf16[512,128]{1,0:T(8,128)(2,1)S(1)} collective-permute-done((bf16[512,128]{1,0:T(8,128)(2,1)S(1)}, bf16[512,128]{1,0:T(8,128)(2,1)S(1)}, u32[]{:S(2)}, u32[]{:S(2)}) %collective-permute-start.16) | collective-permute-done | bytes 131104 | tf_op jit(solution)/shard_map/ppermute | solution.py:237
  58.0 1.2 %collective-permute-done.19.refs_4_ = bf16[512,128]{1,0:T(8,128)(2,1)S(1)} collective-permute-done((bf16[512,128]{1,0:T(8,128)(2,1)S(1)}, bf16[512,128]{1,0:T(8,128)(2,1)S(1)}, u32[]{:S(2)}, u32[]{:S(2)}) %collective-permute-start.19) | collective-permute-done | bytes 131104 | tf_op jit(solution)/shard_map/ppermute | solution.py:237
  59.2 2.2 %collective-permute-start.20 = (bf16[512,128]{1,0:T(8,128)(2,1)S(1)}, bf16[512,128]{1,0:T(8,128)(2,1)S(1)}, u32[]{:S(2)}, u32[]{:S(2)}) collective-permute-start(bf16[512,128]{1,0:T(8,128)(2,1)S(1)} %collective-permute-done.16.refs_1_), channel_id=1, source_target_pairs={{0,3},{1,2},{2,1},{3,0},{4,7},{5,6},{6,5},{7,4},{8,11},{9,10},{10,... | collective-permute-start | bytes 393224 | tf_op jit(solution)/shard_map/ppermute | solution.py:237
  63.7 1.4 %collective-permute-done.20.refs_5_ = bf16[512,128]{1,0:T(8,128)(2,1)S(1)} collective-permute-done((bf16[512,128]{1,0:T(8,128)(2,1)S(1)}, bf16[512,128]{1,0:T(8,128)(2,1)S(1)}, u32[]{:S(2)}, u32[]{:S(2)}) %collective-permute-start.20) | collective-permute-done | bytes 131104 | tf_op jit(solution)/shard_map/ppermute | solution.py:237
  65.1 2.1 %shard_map.93 = (bf16[4224,128]{1,0:T(8,128)(2,1)S(1)}, bf16[512,128]{1,0:T(8,128)(2,1)S(1)}, bf16[512,128]{1,0:T(8,128)(2,1)S(1)}, bf16[512,128]{1,0:T(8,128)(2,1)S(1)}) custom-call(s32[1]{0:T(128)} %bitcast.place, s32[192]{0:T(256)S(1)} %select_n.17.links, bf16[1,6,4096,128]{3,2,1,0:T(8,128)(2,1)S(1)} %shard_map.86.left, ...), custom_call_target="tpu_custom_call" | custom-call | tf_op jit(solution)/shard_map/pallas_call | solution.py:198
  67.2 2.3 %collective-permute-start.26 = (bf16[512,128]{1,0:T(8,128)(2,1)S(1)}, bf16[512,128]{1,0:T(8,128)(2,1)S(1)}, u32[]{:S(2)}, u32[]{:S(2)}) collective-permute-start(bf16[512,128]{1,0:T(8,128)(2,1)S(1)} %get-tuple-element.52), channel_id=1, source_target_pairs={{0,3},{1,2},{2,1},{3,0},{4,7},{5,6},{6,5},{7,4},{8,11},{9,10},{10,... | collective-permute-start | bytes 393224 | tf_op jit(solution)/shard_map/ppermute | solution.py:237
  70.7 2.9 %shard_map.94 = (bf16[512,128]{1,0:T(8,128)(2,1)S(1)}, bf16[512,128]{1,0:T(8,128)(2,1)S(1)}, bf16[512,128]{1,0:T(8,128)(2,1)S(1)}, f32[512,128]{1,0:T(8,128)S(1)}, f32[512,128]{1,0:T(8,128)S(1)}) custom-call(s32[1]{0:T(128)} %bitcast.place, s32[192]{0:T(256)S(1)} %select_n.17.links, bf16[1,6,4096,128]{3,2,1,0:T(8,128)(2,1)S(1)} %shard_map.86.left, ...), custom_call_target="tpu_custom_call" | custom-call | tf_op jit(solution)/shard_map/pallas_call | solution.py:198
  73.6 2.3 %collective-permute-start.23 = (bf16[512,128]{1,0:T(8,128)(2,1)S(1)}, bf16[512,128]{1,0:T(8,128)(2,1)S(1)}, u32[]{:S(2)}, u32[]{:S(2)}) collective-permute-start(bf16[512,128]{1,0:T(8,128)(2,1)S(1)} %get-tuple-element.48), channel_id=1, source_target_pairs={{0,3},{1,2},{2,1},{3,0},{4,7},{5,6},{6,5},{7,4},{8,11},{9,10},{10,... | collective-permute-start | bytes 393224 | tf_op jit(solution)/shard_map/ppermute | solution.py:237
  78.0 1.5 %collective-permute-start.29 = (bf16[512,128]{1,0:T(8,128)(2,1)S(1)}, bf16[512,128]{1,0:T(8,128)(2,1)S(1)}, u32[]{:S(2)}, u32[]{:S(2)}) collective-permute-start(bf16[512,128]{1,0:T(8,128)(2,1)S(1)} %shard_map.95), channel_id=1, source_target_pairs={{0,4},{1,5},{2,6},{3,7},{4,0},{5,1},{6,2},{7,3},{8,12},{9,13},{10,... | collective-permute-start | bytes 393224 | tf_op jit(solution)/shard_map/ppermute | solution.py:237
  80.5 1.3 %collective-permute-done.24 = bf16[512,128]{1,0:T(8,128)(2,1)S(1)} collective-permute-done((bf16[512,128]{1,0:T(8,128)(2,1)S(1)}, bf16[512,128]{1,0:T(8,128)(2,1)S(1)}, u32[]{:S(2)}, u32[]{:S(2)}) %collective-permute-start.24) | collective-permute-done | bytes 131104 | tf_op jit(solution)/shard_map/ppermute | solution.py:237
  81.9 3.5 %collective-permute-done.29 = bf16[512,128]{1,0:T(8,128)(2,1)S(1)} collective-permute-done((bf16[512,128]{1,0:T(8,128)(2,1)S(1)}, bf16[512,128]{1,0:T(8,128)(2,1)S(1)}, u32[]{:S(2)}, u32[]{:S(2)}) %collective-permute-start.29) | collective-permute-done | bytes 131104 | tf_op jit(solution)/shard_map/ppermute | solution.py:237
  (46 shorter events, 14.8 us)
Async XLA Ops:
  0.6 3.4 %collective-permute-start = (f32[512]{0:T(512)}, f32[512]{0:T(512)S(1)}, u32[]{:S(2)}, u32[]{:S(2)}) collective-permute-start(f32[512]{0:T(512)} %param.8), channel_id=1, source_target_pairs={{0,8},{8,16},{16,24},{1,9},{9,17},{17,25},{2,10},{10,18},{18,26},{... | collective-permute-start | bytes 6152 | tf_op jit(solution)/shard_map/ppermute | solution.py:14
  5.1 9.2 %collective-permute-start.1 = (bf16[512,128]{1,0:T(8,128)(2,1)S(1)}, bf16[512,128]{1,0:T(8,128)(2,1)S(1)}, u32[]{:S(2)}, u32[]{:S(2)}) collective-permute-start(bf16[512,128]{1,0:T(8,128)(2,1)S(1)} %multiply_convert_fusion.refs_0_.refs_5_), channel_id=1, source_target_pairs={{0,4},{1,5},{2,6},{3,7},{4,0},{5,1},{6,2},{7,3},{8,12},{9,13},{10,... | collective-permute-start | bytes 393224 | tf_op jit(solution)/shard_map/ppermute | solution.py:237
  8.6 9.7 %collective-permute-start.4 = (bf16[512,128]{1,0:T(8,128)(2,1)S(1)}, bf16[512,128]{1,0:T(8,128)(2,1)S(1)}, u32[]{:S(2)}, u32[]{:S(2)}) collective-permute-start(bf16[512,128]{1,0:T(8,128)(2,1)S(1)} %multiply_convert_fusion.refs_0_.refs_5_), channel_id=1, source_target_pairs={{0,2},{1,3},{2,0},{3,1},{4,6},{5,7},{6,4},{7,5},{8,10},{9,11},{10,... | collective-permute-start | bytes 393224 | tf_op jit(solution)/shard_map/ppermute | solution.py:237
  10.1 14.8 %collective-permute-start.3 = (bf16[512,128]{1,0:T(8,128)(2,1)S(1)}, bf16[512,128]{1,0:T(8,128)(2,1)S(1)}, u32[]{:S(2)}, u32[]{:S(2)}) collective-permute-start(bf16[512,128]{1,0:T(8,128)(2,1)S(1)} %multiply_convert_fusion.refs_0_.refs_5_), channel_id=1, source_target_pairs={{0,1},{1,0},{2,3},{3,2},{4,5},{5,4},{6,7},{7,6},{8,9},{9,8},{10,11... | collective-permute-start | bytes 393224 | tf_op jit(solution)/shard_map/ppermute | solution.py:237
  11.7 13.3 %collective-permute-start.2 = (bf16[512,128]{1,0:T(8,128)(2,1)S(1)}, bf16[512,128]{1,0:T(8,128)(2,1)S(1)}, u32[]{:S(2)}, u32[]{:S(2)}) collective-permute-start(bf16[512,128]{1,0:T(8,128)(2,1)S(1)} %multiply_convert_fusion.refs_0_.refs_5_), channel_id=1, source_target_pairs={{0,3},{1,2},{2,1},{3,0},{4,7},{5,6},{6,5},{7,4},{8,11},{9,10},{10,... | collective-permute-start | bytes 393224 | tf_op jit(solution)/shard_map/ppermute | solution.py:237
  14.3 10.7 %collective-permute-start.7 = (bf16[512,128]{1,0:T(8,128)(2,1)S(1)}, bf16[512,128]{1,0:T(8,128)(2,1)S(1)}, u32[]{:S(2)}, u32[]{:S(2)}) collective-permute-start(bf16[512,128]{1,0:T(8,128)(2,1)S(1)} %collective-permute-done.1.refs_1_), channel_id=1, source_target_pairs={{0,2},{1,3},{2,0},{3,1},{4,6},{5,7},{6,4},{7,5},{8,10},{9,11},{10,... | collective-permute-start | bytes 393224 | tf_op jit(solution)/shard_map/ppermute | solution.py:237
  16.7 8.3 %collective-permute-start.6 = (bf16[512,128]{1,0:T(8,128)(2,1)S(1)}, bf16[512,128]{1,0:T(8,128)(2,1)S(1)}, u32[]{:S(2)}, u32[]{:S(2)}) collective-permute-start(bf16[512,128]{1,0:T(8,128)(2,1)S(1)} %collective-permute-done.1.refs_1_), channel_id=1, source_target_pairs={{0,1},{1,0},{2,3},{3,2},{4,5},{5,4},{6,7},{7,6},{8,9},{9,8},{10,11... | collective-permute-start | bytes 393224 | tf_op jit(solution)/shard_map/ppermute | solution.py:237
  18.2 7.4 %collective-permute-start.5 = (bf16[512,128]{1,0:T(8,128)(2,1)S(1)}, bf16[512,128]{1,0:T(8,128)(2,1)S(1)}, u32[]{:S(2)}, u32[]{:S(2)}) collective-permute-start(bf16[512,128]{1,0:T(8,128)(2,1)S(1)} %collective-permute-done.1.refs_1_), channel_id=1, source_target_pairs={{0,3},{1,2},{2,1},{3,0},{4,7},{5,6},{6,5},{7,4},{8,11},{9,10},{10,... | collective-permute-start | bytes 393224 | tf_op jit(solution)/shard_map/ppermute | solution.py:237
  24.9 6.3 %copy-start = (f32[512,128]{1,0:T(8,128)S(1)}, f32[512,128]{1,0:T(8,128)}, u32[]{:S(2)}) copy-start(f32[512,128]{1,0:T(8,128)} %refs_6_.1) | copy-start | bytes 786436
  27.7 9.3 %collective-permute-start.11 = (bf16[512,128]{1,0:T(8,128)(2,1)S(1)}, bf16[512,128]{1,0:T(8,128)(2,1)S(1)}, u32[]{:S(2)}, u32[]{:S(2)}) collective-permute-start(bf16[512,128]{1,0:T(8,128)(2,1)S(1)} %get-tuple-element.40), channel_id=1, source_target_pairs={{0,3},{1,2},{2,1},{3,0},{4,7},{5,6},{6,5},{7,4},{8,11},{9,10},{10,... | collective-permute-start | bytes 393224 | tf_op jit(solution)/shard_map/ppermute | solution.py:237
  29.9 7.8 %collective-permute-start.12 = (bf16[512,128]{1,0:T(8,128)(2,1)S(1)}, bf16[512,128]{1,0:T(8,128)(2,1)S(1)}, u32[]{:S(2)}, u32[]{:S(2)}) collective-permute-start(bf16[512,128]{1,0:T(8,128)(2,1)S(1)} %get-tuple-element.41), channel_id=1, source_target_pairs={{0,1},{1,0},{2,3},{3,2},{4,5},{5,4},{6,7},{7,6},{8,9},{9,8},{10,11... | collective-permute-start | bytes 393224 | tf_op jit(solution)/shard_map/ppermute | solution.py:237
  30.5 7.3 %collective-permute-start.13 = (bf16[512,128]{1,0:T(8,128)(2,1)S(1)}, bf16[512,128]{1,0:T(8,128)(2,1)S(1)}, u32[]{:S(2)}, u32[]{:S(2)}) collective-permute-start(bf16[512,128]{1,0:T(8,128)(2,1)S(1)} %get-tuple-element.42), channel_id=1, source_target_pairs={{0,2},{1,3},{2,0},{3,1},{4,6},{5,7},{6,4},{7,5},{8,10},{9,11},{10,... | collective-permute-start | bytes 393224 | tf_op jit(solution)/shard_map/ppermute | solution.py:237
  34.2 8.8 %collective-permute-start.8 = (bf16[528,128]{1,0:T(8,128)(2,1)S(1)}, bf16[528,128]{1,0:T(8,128)(2,1)S(1)}, u32[]{:S(2)}, u32[]{:S(2)}) collective-permute-start(bf16[528,128]{1,0:T(8,128)(2,1)S(1)} %get-tuple-element.36), channel_id=1, source_target_pairs={{0,3},{1,2},{2,1},{3,0},{4,7},{5,6},{6,5},{7,4},{8,11},{9,10},{10,... | collective-permute-start | bytes 405512 | tf_op jit(solution)/shard_map/ppermute | solution.py:237
  36.4 6.6 %collective-permute-start.9 = (bf16[528,128]{1,0:T(8,128)(2,1)S(1)}, bf16[528,128]{1,0:T(8,128)(2,1)S(1)}, u32[]{:S(2)}, u32[]{:S(2)}) collective-permute-start(bf16[528,128]{1,0:T(8,128)(2,1)S(1)} %get-tuple-element.37), channel_id=1, source_target_pairs={{0,1},{1,0},{2,3},{3,2},{4,5},{5,4},{6,7},{7,6},{8,9},{9,8},{10,11... | collective-permute-start | bytes 405512 | tf_op jit(solution)/shard_map/ppermute | solution.py:237
  37.0 8.5 %collective-permute-start.10 = (bf16[528,128]{1,0:T(8,128)(2,1)S(1)}, bf16[528,128]{1,0:T(8,128)(2,1)S(1)}, u32[]{:S(2)}, u32[]{:S(2)}) collective-permute-start(bf16[528,128]{1,0:T(8,128)(2,1)S(1)} %get-tuple-element.38), channel_id=1, source_target_pairs={{0,2},{1,3},{2,0},{3,1},{4,6},{5,7},{6,4},{7,5},{8,10},{9,11},{10,... | collective-permute-start | bytes 405512 | tf_op jit(solution)/shard_map/ppermute | solution.py:237
  37.8 12.3 %collective-permute-start.14 = (bf16[512,128]{1,0:T(8,128)(2,1)S(1)}, bf16[512,128]{1,0:T(8,128)(2,1)S(1)}, u32[]{:S(2)}, u32[]{:S(2)}) collective-permute-start(bf16[512,128]{1,0:T(8,128)(2,1)S(1)} %shard_map.90), channel_id=1, source_target_pairs={{0,4},{1,5},{2,6},{3,7},{4,0},{5,1},{6,2},{7,3},{8,12},{9,13},{10,... | collective-permute-start | bytes 393224 | tf_op jit(solution)/shard_map/ppermute | solution.py:237
  45.5 4.6 %collective-permute-start.15 = (f32[8,128]{1,0:T(8,128)S(1)}, f32[8,128]{1,0:T(8,128)S(1)}, u32[]{:S(2)}, u32[]{:S(2)}) collective-permute-start(f32[8,128]{1,0:T(8,128)S(1)} %shard_map.91.refs_7_), channel_id=1, source_target_pairs={{0,4},{1,5},{2,6},{3,7},{4,0},{5,1},{6,2},{7,3},{8,12},{9,13},{10,... | collective-permute-start | bytes 12296 | tf_op jit(solution)/shard_map/ppermute | solution.py:237
  50.3 7.3 %collective-permute-start.16 = (bf16[512,128]{1,0:T(8,128)(2,1)S(1)}, bf16[512,128]{1,0:T(8,128)(2,1)S(1)}, u32[]{:S(2)}, u32[]{:S(2)}) collective-permute-start(bf16[512,128]{1,0:T(8,128)(2,1)S(1)} %get-tuple-element.45.refs_0_), channel_id=1, source_target_pairs={{0,4},{1,5},{2,6},{3,7},{4,0},{5,1},{6,2},{7,3},{8,12},{9,13},{10,... | collective-permute-start | bytes 393224 | tf_op jit(solution)/shard_map/ppermute | solution.py:237
  51.5 7.7 %collective-permute-start.19 = (bf16[512,128]{1,0:T(8,128)(2,1)S(1)}, bf16[512,128]{1,0:T(8,128)(2,1)S(1)}, u32[]{:S(2)}, u32[]{:S(2)}) collective-permute-start(bf16[512,128]{1,0:T(8,128)(2,1)S(1)} %get-tuple-element.45.refs_0_), channel_id=1, source_target_pairs={{0,2},{1,3},{2,0},{3,1},{4,6},{5,7},{6,4},{7,5},{8,10},{9,11},{10,... | collective-permute-start | bytes 393224 | tf_op jit(solution)/shard_map/ppermute | solution.py:237
  53.6 7.9 %collective-permute-start.18 = (bf16[512,128]{1,0:T(8,128)(2,1)S(1)}, bf16[512,128]{1,0:T(8,128)(2,1)S(1)}, u32[]{:S(2)}, u32[]{:S(2)}) collective-permute-start(bf16[512,128]{1,0:T(8,128)(2,1)S(1)} %get-tuple-element.45.refs_0_), channel_id=1, source_target_pairs={{0,1},{1,0},{2,3},{3,2},{4,5},{5,4},{6,7},{7,6},{8,9},{9,8},{10,11... | collective-permute-start | bytes 393224 | tf_op jit(solution)/shard_map/ppermute | solution.py:237
  53.6 8.8 %collective-permute-start.17 = (bf16[512,128]{1,0:T(8,128)(2,1)S(1)}, bf16[512,128]{1,0:T(8,128)(2,1)S(1)}, u32[]{:S(2)}, u32[]{:S(2)}) collective-permute-start(bf16[512,128]{1,0:T(8,128)(2,1)S(1)} %get-tuple-element.45.refs_0_), channel_id=1, source_target_pairs={{0,3},{1,2},{2,1},{3,0},{4,7},{5,6},{6,5},{7,4},{8,11},{9,10},{10,... | collective-permute-start | bytes 393224 | tf_op jit(solution)/shard_map/ppermute | solution.py:237
  57.6 5.7 %collective-permute-start.22 = (bf16[512,128]{1,0:T(8,128)(2,1)S(1)}, bf16[512,128]{1,0:T(8,128)(2,1)S(1)}, u32[]{:S(2)}, u32[]{:S(2)}) collective-permute-start(bf16[512,128]{1,0:T(8,128)(2,1)S(1)} %collective-permute-done.16.refs_1_), channel_id=1, source_target_pairs={{0,2},{1,3},{2,0},{3,1},{4,6},{5,7},{6,4},{7,5},{8,10},{9,11},{10,... | collective-permute-start | bytes 393224 | tf_op jit(solution)/shard_map/ppermute | solution.py:237
  57.6 6.0 %collective-permute-start.21 = (bf16[512,128]{1,0:T(8,128)(2,1)S(1)}, bf16[512,128]{1,0:T(8,128)(2,1)S(1)}, u32[]{:S(2)}, u32[]{:S(2)}) collective-permute-start(bf16[512,128]{1,0:T(8,128)(2,1)S(1)} %collective-permute-done.16.refs_1_), channel_id=1, source_target_pairs={{0,1},{1,0},{2,3},{3,2},{4,5},{5,4},{6,7},{7,6},{8,9},{9,8},{10,11... | collective-permute-start | bytes 393224 | tf_op jit(solution)/shard_map/ppermute | solution.py:237
  59.2 5.9 %collective-permute-start.20 = (bf16[512,128]{1,0:T(8,128)(2,1)S(1)}, bf16[512,128]{1,0:T(8,128)(2,1)S(1)}, u32[]{:S(2)}, u32[]{:S(2)}) collective-permute-start(bf16[512,128]{1,0:T(8,128)(2,1)S(1)} %collective-permute-done.16.refs_1_), channel_id=1, source_target_pairs={{0,3},{1,2},{2,1},{3,0},{4,7},{5,6},{6,5},{7,4},{8,11},{9,10},{10,... | collective-permute-start | bytes 393224 | tf_op jit(solution)/shard_map/ppermute | solution.py:237
  67.2 9.4 %collective-permute-start.26 = (bf16[512,128]{1,0:T(8,128)(2,1)S(1)}, bf16[512,128]{1,0:T(8,128)(2,1)S(1)}, u32[]{:S(2)}, u32[]{:S(2)}) collective-permute-start(bf16[512,128]{1,0:T(8,128)(2,1)S(1)} %get-tuple-element.52), channel_id=1, source_target_pairs={{0,3},{1,2},{2,1},{3,0},{4,7},{5,6},{6,5},{7,4},{8,11},{9,10},{10,... | collective-permute-start | bytes 393224 | tf_op jit(solution)/shard_map/ppermute | solution.py:237
  69.5 7.7 %collective-permute-start.27 = (bf16[512,128]{1,0:T(8,128)(2,1)S(1)}, bf16[512,128]{1,0:T(8,128)(2,1)S(1)}, u32[]{:S(2)}, u32[]{:S(2)}) collective-permute-start(bf16[512,128]{1,0:T(8,128)(2,1)S(1)} %get-tuple-element.53), channel_id=1, source_target_pairs={{0,1},{1,0},{2,3},{3,2},{4,5},{5,4},{6,7},{7,6},{8,9},{9,8},{10,11... | collective-permute-start | bytes 393224 | tf_op jit(solution)/shard_map/ppermute | solution.py:237
  70.2 7.8 %collective-permute-start.28 = (bf16[512,128]{1,0:T(8,128)(2,1)S(1)}, bf16[512,128]{1,0:T(8,128)(2,1)S(1)}, u32[]{:S(2)}, u32[]{:S(2)}) collective-permute-start(bf16[512,128]{1,0:T(8,128)(2,1)S(1)} %get-tuple-element.54), channel_id=1, source_target_pairs={{0,2},{1,3},{2,0},{3,1},{4,6},{5,7},{6,4},{7,5},{8,10},{9,11},{10,... | collective-permute-start | bytes 393224 | tf_op jit(solution)/shard_map/ppermute | solution.py:237
  73.6 6.9 %collective-permute-start.23 = (bf16[512,128]{1,0:T(8,128)(2,1)S(1)}, bf16[512,128]{1,0:T(8,128)(2,1)S(1)}, u32[]{:S(2)}, u32[]{:S(2)}) collective-permute-start(bf16[512,128]{1,0:T(8,128)(2,1)S(1)} %get-tuple-element.48), channel_id=1, source_target_pairs={{0,3},{1,2},{2,1},{3,0},{4,7},{5,6},{6,5},{7,4},{8,11},{9,10},{10,... | collective-permute-start | bytes 393224 | tf_op jit(solution)/shard_map/ppermute | solution.py:237
  75.9 6.0 %collective-permute-start.24 = (bf16[512,128]{1,0:T(8,128)(2,1)S(1)}, bf16[512,128]{1,0:T(8,128)(2,1)S(1)}, u32[]{:S(2)}, u32[]{:S(2)}) collective-permute-start(bf16[512,128]{1,0:T(8,128)(2,1)S(1)} %get-tuple-element.49), channel_id=1, source_target_pairs={{0,1},{1,0},{2,3},{3,2},{4,5},{5,4},{6,7},{7,6},{8,9},{9,8},{10,11... | collective-permute-start | bytes 393224 | tf_op jit(solution)/shard_map/ppermute | solution.py:237
  76.6 5.2 %collective-permute-start.25 = (bf16[512,128]{1,0:T(8,128)(2,1)S(1)}, bf16[512,128]{1,0:T(8,128)(2,1)S(1)}, u32[]{:S(2)}, u32[]{:S(2)}) collective-permute-start(bf16[512,128]{1,0:T(8,128)(2,1)S(1)} %get-tuple-element.50), channel_id=1, source_target_pairs={{0,2},{1,3},{2,0},{3,1},{4,6},{5,7},{6,4},{7,5},{8,10},{9,11},{10,... | collective-permute-start | bytes 393224 | tf_op jit(solution)/shard_map/ppermute | solution.py:237
  78.0 7.3 %collective-permute-start.29 = (bf16[512,128]{1,0:T(8,128)(2,1)S(1)}, bf16[512,128]{1,0:T(8,128)(2,1)S(1)}, u32[]{:S(2)}, u32[]{:S(2)}) collective-permute-start(bf16[512,128]{1,0:T(8,128)(2,1)S(1)} %shard_map.95), channel_id=1, source_target_pairs={{0,4},{1,5},{2,6},{3,7},{4,0},{5,1},{6,2},{7,3},{8,12},{9,13},{10,... | collective-permute-start | bytes 393224 | tf_op jit(solution)/shard_map/ppermute | solution.py:237

commit v3 on v2

--- a/solution.py
+++ b/solution.py
@@ -53,20 +53,21 @@
 
 
 def scaled_products(vector, links, left, right, chunks, per, store):
-    nterms, width = left.shape[1], left.shape[3]
+    width = vector.shape[1]
     nsector = vector.shape[0] // width - 1
+    nterms = left.shape[0]
 
     def inner_of(i):
         rows = pl.ds(pl.multiple_of(i * width, width), width)
         blocks = []
         for k in range(nterms):
             at = pl.multiple_of(links[k * nsector + i] * width, width)
-            product = jnp.dot(left[0, k, rows, :], vector[pl.ds(at, width), :], preferred_element_type=jnp.float32)
+            product = jnp.dot(left[k, rows, :], vector[pl.ds(at, width), :], preferred_element_type=jnp.float32)
             blocks.append(product.astype(jnp.bfloat16))
         return jnp.concatenate(blocks, axis=1), rows
 
     def outer_of(inner, rows):
-        factors = jnp.concatenate([right[0, k, rows, :] for k in range(nterms)], axis=1)
+        factors = jnp.concatenate([right[k, rows, :] for k in range(nterms)], axis=1)
         return lax.dot_general(inner, factors, (((1,), (1,)), ((), ())), preferred_element_type=jnp.float32)
 
     waiting = None
@@ -90,6 +91,20 @@
 TAIL = 16
 
 
+def chunk_sums(offsets, rows, place, links, left, right, vector, outs, numer):
+    width = vector.shape[1]
+    chunks = [place[0] ^ offset for offset in offsets]
+
+    def store(t, i, sums):
+        at = slice(i * width, (i + 1) * width)
+        outs[t][at, :] = sums.astype(outs[t].dtype)
+        if numer is not None:
+            start = pl.multiple_of(chunks[t] * rows + i * width, width)
+            numer[...] += squares(sums, vector[pl.ds(start, width), :].astype(jnp.float32))
+
+    scaled_products(vector, links, left, right, chunks, rows // width, store)
+
+
 def first_kernel(offsets, first, dots, place, links, left, right, *refs):
     npiece = len(offsets)
     pieces, vector, outs = refs[:npiece], refs[npiece], refs[npiece + 1 :]
@@ -97,18 +112,24 @@
     for piece, offset in zip(pieces, offsets):
         vector[rows_at(place[0] ^ offset, rows), :] = piece[...]
     vector[npiece * rows :, :] = jnp.zeros((width, width), vector.dtype)
-    chunks = [place[0] ^ offset for offset in first]
+    numer = outs[-1] if dots else None
     if dots:
-        outs[-1][...] = jnp.zeros_like(outs[-1])
-
-    def store(t, i, sums):
-        at = slice(i * width, (i + 1) * width)
-        outs[t][at, :] = sums.astype(outs[t].dtype)
-        if dots:
-            start = pl.multiple_of(chunks[t] * rows + i * width, width)
-            outs[-1][...] += squares(sums, vector[pl.ds(start, width), :].astype(jnp.float32))
-
-    scaled_products(vector, links, left, right, chunks, rows // width, store)
+        numer[...] = jnp.zeros_like(numer)
+    chunk_sums(first, rows, place, links, left, right, vector, outs, numer)
+
+
+def last_kernel(offsets, dots, place, links, left, right, vector, *refs):
+    width = vector.shape[1]
+    numer = None
+    rows = refs[-1].shape[0]
+    if dots:
+        hdiag, before, *refs, numer, denom = refs
+        rows = hdiag.shape[0]
+        own = vector[rows_at(place[0], rows), :].astype(jnp.float32)
+        numer[...] = before[...] + squares(hdiag[...] * own, own)
+        whole = vector[: vector.shape[0] - width, :].astype(jnp.float32)
+        denom[...] = squares(whole, whole)
+    chunk_sums(offsets, rows, place, links, left, right, vector, refs, numer)
 
 
 def three_roundings(part):
@@ -121,33 +142,14 @@
     return tail.astype(jnp.bfloat16)
 
 
-def second_kernel(rest, dots, place, links, left, right, vector, *refs):
-    width = vector.shape[1]
-    if dots:
-        hdiag, before, *outs, numer, denom = refs
-        rows = hdiag.shape[0]
-        own = vector[rows_at(place[0], rows), :].astype(jnp.float32)
-        numer[...] = before[...] + squares(hdiag[...] * own, own)
-        whole = vector[: vector.shape[0] - width, :].astype(jnp.float32)
-        denom[...] = squares(whole, whole)
-    else:
-        outs = refs
-        rows = outs[0].shape[0]
-    chunks = [place[0] ^ offset for offset in rest]
-
-    def store(t, i, sums):
-        at = slice(i * width, (i + 1) * width)
-        outs[t][at, :] = sums.astype(outs[t].dtype)
-        if dots:
-            start = pl.multiple_of(chunks[t] * rows + i * width, width)
-            numer[...] += squares(sums, vector[pl.ds(start, width), :].astype(jnp.float32))
-
-    scaled_products(vector, links, left, right, chunks, rows // width, store)
-    if dots:
-        tail = three_roundings(jnp.sum(numer[...], axis=0, keepdims=True))
-        for out in outs:
-            if out.shape[0] > rows:
-                out[rows:, :] = tail
+def tail_kernel(nlate, mine, other, *refs):
+    chunks, both, outs = refs[:nlate], refs[nlate], refs[nlate + 1 :]
+    both[...] = mine[...] + other[...]
+    tail = three_roundings(jnp.sum(both[...], axis=0, keepdims=True))
+    for chunk, out in zip(chunks, outs):
+        rows = chunk.shape[0]
+        out[:rows, :] = chunk[...]
+        out[rows:, :] = tail
 
 
 def added_kernel(kept, *refs):
@@ -158,13 +160,12 @@
     out[...] = total.astype(out.dtype)
 
 
-def half_kernel(numer, *refs):
+def final_kernel(kept, vector, hdiag, *refs):
     out = refs[-1]
-    total = jnp.sum(numer[...], axis=0, keepdims=True)
+    total = kept[...] + hdiag[...] * vector[...].astype(jnp.float32)
     for came in refs[:-1]:
-        rows = came.shape[0] - TAIL
-        total = total + jnp.sum(came[rows:, :].astype(jnp.float32), axis=0, keepdims=True)
-    out[...] = jnp.broadcast_to(total, out.shape)
+        total = total + came[...].astype(jnp.float32)
+    out[...] = total
 
 
 def correct_kernel(nmore, *refs):
@@ -172,9 +173,11 @@
     psi, hdiag, mine, other, denom, correction, theta = refs
     rows = psi.shape[0]
     total = kept[...]
+    numer = jnp.sum(mine[...] + other[...], keepdims=True)
     for m in more:
         total = total + m[:rows, :].astype(jnp.float32)
-    numer = jnp.sum(mine[:1, :] + other[:1, :], keepdims=True)
+        if m.shape[0] > rows:
+            numer = numer + jnp.sum(m[rows:, :].astype(jnp.float32), keepdims=True)
     quotient = numer / jnp.sum(denom[...], keepdims=True)
     vector = psi[...].astype(jnp.float32)
     sigma = total + hdiag[...] * vector
@@ -182,8 +185,18 @@
     theta[...] = jnp.broadcast_to(quotient, theta.shape)
 
 
+def weigh_kernel(weights, piece, out):
+    width = out.shape[1]
+    columns = weights[...].T
+    for i in range(weights.shape[0]):
+        at = slice(i * width, (i + 1) * width)
+        out[at, :] = (columns[:, i : i + 1] * piece[at, :].astype(jnp.float32)).astype(out.dtype)
+
+
 def load_kernel(source, target, sems):
-    copies = [pltpu.make_async_copy(source.at[:, k], target.at[:, k], sems.at[k]) for k in range(source.shape[1])]
+    count = sems.shape[0]
+    step = source.shape[0] // count
+    copies = [pltpu.make_async_copy(source.at[at], target.at[at], sems.at[k]) for k in range(count) for at in [pl.ds(k * step, step)]]
     for copy in copies:
         copy.start()
     for copy in copies:
@@ -205,15 +218,16 @@
     return list(outs)
 
 
-def loaded(operators):
-    return pl.pallas_call(
+def loaded(array, count):
+    held = pl.pallas_call(
         load_kernel,
-        out_shape=pltpu.VMEM(operators.shape, operators.dtype),
+        out_shape=pltpu.VMEM(array.shape, array.dtype),
         in_specs=[pl.BlockSpec(memory_space=pltpu.HBM)],
         out_specs=VMEM,
-        scratch_shapes=[pltpu.SemaphoreType.DMA((operators.shape[1],))],
+        scratch_shapes=[pltpu.SemaphoreType.DMA((count,))],
         compiler_params=pltpu.CompilerParams(vmem_limit_bytes=1 << 20),
-    )(pltpu.with_memory_space_constraint(operators, pltpu.HBM))
+    )(pltpu.with_memory_space_constraint(array, pltpu.HBM))
+    return pltpu.with_memory_space_constraint(held, pltpu.VMEM)
 
 
 def within(half):
@@ -227,7 +241,6 @@
     half = devices // 2
     inside = within(half)
     place = lax.axis_index("ops").astype(jnp.int32).reshape(1)
-    links = jnp.where(blockmask[0] != 0, couple[0], nsector).reshape(-1)
     shape = jax.ShapeDtypeStruct
     tile = shape((8, width), jnp.float32)
     sent, kept = shape((rows, width), jnp.bfloat16), shape((rows, width), jnp.float32)
@@ -244,44 +257,53 @@
             pieces[half ^ r] = exchange(pieces[half], r)
         return pieces
 
-    def apply_terms(piece, left, right, dots):
-        left = pltpu.with_memory_space_constraint(left, pltpu.VMEM)
-        right = pltpu.with_memory_space_constraint(right, pltpu.VMEM)
-        pieces = gather(piece)
-        first = [half ^ r for r in inside]
-        rest = inside + [half, 0]
+    def apply_terms(pieces, left, right, dots):
+        across = [half ^ r for r in inside]
+        soon = inside.index(1)
+        late = [t for t in range(len(inside)) if t != soon]
         whole = shape((devices * rows + width, width), jnp.bfloat16)
+        fixed = (place, links, left, right)
         vector, *lead = on_chip(
-            partial(first_kernel, list(pieces), first, dots),
-            [whole] + [sent] * len(first) + [tile] * dots,
-            2, place, links, left, right, *pieces.values(),
+            partial(first_kernel, list(pieces), across, dots),
+            [whole] + [sent] * len(across) + [tile] * dots,
+            2, *fixed, *pieces.values(),
         )
-        extra = (hdiag, lead[-1]) if dots else ()
         outs = on_chip(
-            partial(second_kernel, rest, dots),
-            [tailed if dots else sent] * len(inside) + [kept] * 2 + [tile] * (2 * dots),
-            2, place, links, left, right, vector, *extra,
+            partial(last_kernel, inside + [half, 0], dots),
+            [sent] * len(inside) + [kept] * 2 + [tile] * (2 * dots),
+            2, *fixed, vector, *((hdiag, lead[-1]) if dots else ()),
         )
-        crossing, own, *sums = outs[len(inside) :]
-        came = [exchange(chunk, r) for r, chunk in zip(inside, lead)]
-        ours = [exchange(chunk, r) for r, chunk in zip(inside, outs)]
-        theirs = exchange(on_chip(added_kernel, [sent], 0, crossing, *came)[0], half)
+        ours, (crossing, own, *sums) = outs[: len(inside)], outs[len(inside) :]
         if dots:
             numer, denom = sums
-            mine = on_chip(half_kernel, [tile], 0, numer, *ours)[0]
-            sums = [mine, exchange(mine, half), denom]
+            other = exchange(numer, half)
+        came = [exchange(chunk, r) for r, chunk in zip(inside, lead)]
+        crossing = on_chip(added_kernel, [sent], 0, crossing, *came)[0]
+        theirs = exchange(crossing, half)
+        if dots:
+            both, *tails = on_chip(
+                partial(tail_kernel, len(ours) - 1), [tile] + [tailed] * (len(ours) - 1), 0, numer, other, *(ours[t] for t in late)
+            )
+            beside = exchange(both, inside[soon])
+            for t, message in zip(late, tails):
+                ours[t] = message
+            sums = [both, beside, denom]
+        ours = [exchange(chunk, r) for r, chunk in zip(inside, ours)]
         return [own, *ours, theirs], sums
 
+    nterms = left_ops.shape[1]
+    links = jnp.where(blockmask[0] != 0, couple[0], nsector).reshape(-1)
     place, links, left_ops, right_operators = lax.optimization_barrier((place, links, left_ops, right_operators))
-    left = loaded(left_ops)
-    right = loaded(right_operators)
+    left = loaded(left_ops[0], nterms)
+    right = loaded(right_operators[0], nterms)
     earlier = shifted(lam, "seg", 1)
-    weights = jnp.where(lax.axis_index("seg") == 0, jnp.ones_like(earlier), earlier)
-    psi = (weights[:, None] * amat.astype(jnp.float32)).astype(jnp.bfloat16)
-    terms, sums = apply_terms(psi, left, right, True)
+    weights = jnp.where(lax.axis_index("seg") == 0, jnp.ones_like(earlier), earlier).reshape(-1, width)
+    held = loaded(amat, 1)
+    psi = on_chip(weigh_kernel, [sent], 0, weights, held)[0]
+    terms, sums = apply_terms(gather(psi), left, right, True)
     correction, theta = on_chip(partial(correct_kernel, half), [sent, tile], 0, *terms, psi, hdiag, *sums)
-    terms, _ = apply_terms(correction, left, right, False)
-    sigma_two = sum(t.astype(jnp.float32) for t in terms) + hdiag * correction.astype(jnp.float32)
+    terms, _ = apply_terms(gather(correction), left, right, False)
+    sigma_two = on_chip(final_kernel, [kept], 0, terms[0], correction, hdiag, *terms[1:])[0]
     return (sigma_two, theta[0, :1])
 
 

time: 86.4 us -> 87.9 us (1.017)
  starting transfers between devices: 40.4 us -> 48.8 us
  waiting for transfers between devices: 25.7 us -> 18.9 us
  Pallas kernels: 16.1 us -> 18 us
  other arithmetic: 2.55 us -> 0.72 us
    ppermute x29 -> x30, starting transfers between devices: 38 us -> 46.4 us  [exchange(): return lax.ppermute(array, 'ops', [(o, o ^ by) for o in range(devices)])]
    ppermute x29 -> x30, waiting for transfers between devices: 24.7 us -> 18.8 us  [exchange(): return lax.ppermute(array, 'ops', [(o, o ^ by) for o in range(devices)])]
    convert_element_type x1 -> x0, other arithmetic: 1.03 us -> none  [paired_body(): psi = (weights[:, None] * amat.astype(jnp.float32)).astype(jnp.bfloat16)]
    pallas_call x8 -> x10, Pallas kernels: 10.4 us -> 11.4 us  [on_chip(): pl.pallas_call(kernel, out_shape=out_shape, in_specs=[SMEM] * nscalar + [...]
    ppermute x1, waiting for transfers between devices: 1.01 us -> 0.08 us  [shifted(): return lax.ppermute(array, axis, pairs)]
    pallas_call x2 -> x3, Pallas kernels: 5.71 us -> 6.62 us  [loaded(): pl.pallas_call(load_kernel, out_shape=pltpu.VMEM(array.shape, array.dtype...]
  transfers between devices with their start and end apart: 30 -> 31, of which waited for: 16 -> 14; matrix products, arithmetic and copies ran while one was open for 2% -> 1% of each run, Pallas kernels for 14% -> 14%
where the time goes in v3:
time: 87.9 us; the launch traced here: 87.7 us
  starting transfers between devices  48.8 us (56%)
  waiting for transfers between devices  18.9 us (22%)
  Pallas kernels  18 us (20%)
    ppermute x30, starting transfers between devices, exchange(): return lax.ppermute(array, 'ops', [(o, o ^ by) for o in range(devices)])  46.4 us
    ppermute x30, waiting for transfers between devices, exchange(): return lax.ppermute(array, 'ops', [(o, o ^ by) for o in range(devices)])  18.8 us
    pallas_call x10, Pallas kernels, on_chip(): pl.pallas_call(kernel, out_shape=out_shape, in_specs=[SMEM] * nscalar + [...  11.4 us
    pallas_call x3, Pallas kernels, loaded(): pl.pallas_call(load_kernel, out_shape=pltpu.VMEM(array.shape, array.dtype...  6.62 us
    ppermute x1, starting transfers between devices, shifted(): return lax.ppermute(array, axis, pairs)  2.4 us
  transfers between devices with their start and end apart: 31, of which 14 were waited for; matrix products, arithmetic and copies ran while one was open for 1% of the time, Pallas kernels for 14%

profile of v3, /device:TPU:0, one launch (start us, length us, event | category | flops | bytes accessed | tf_op | source)
XLA Modules:
  0.0 87.7 jit_solution(15401100226311780971)
XLA Ops:
  0.6 2.4 %collective-permute-start = (f32[512]{0:T(512)}, f32[512]{0:T(512)S(1)}, u32[]{:S(2)}, u32[]{:S(2)}) collective-permute-start(f32[512]{0:T(512)} %param.8), channel_id=1, source_target_pairs={{0,8},{8,16},{16,24},{1,9},{9,17},{17,25},{2,10},{10,18},{18,26},{... | collective-permute-start | bytes 6152 | tf_op jit(solution)/shard_map/ppermute | solution.py:14
  4.3 3.5 %collective-permute-start.1 = (bf16[512,128]{1,0:T(8,128)(2,1)S(1)}, bf16[512,128]{1,0:T(8,128)(2,1)S(1)}, u32[]{:S(2)}, u32[]{:S(2)}) collective-permute-start(bf16[512,128]{1,0:T(8,128)(2,1)S(1)} %shard_map.89.refs_0_.refs_5_), channel_id=1, source_target_pairs={{0,4},{1,5},{2,6},{3,7},{4,0},{5,1},{6,2},{7,3},{8,12},{9,13},{10,... | collective-permute-start | bytes 393224 | tf_op jit(solution)/shard_map/ppermute | solution.py:250
  7.8 1.6 %collective-permute-start.4 = (bf16[512,128]{1,0:T(8,128)(2,1)S(1)}, bf16[512,128]{1,0:T(8,128)(2,1)S(1)}, u32[]{:S(2)}, u32[]{:S(2)}) collective-permute-start(bf16[512,128]{1,0:T(8,128)(2,1)S(1)} %shard_map.89.refs_0_.refs_5_), channel_id=1, source_target_pairs={{0,2},{1,3},{2,0},{3,1},{4,6},{5,7},{6,4},{7,5},{8,10},{9,11},{10,... | collective-permute-start | bytes 393224 | tf_op jit(solution)/shard_map/ppermute | solution.py:250
  9.4 1.5 %collective-permute-start.3 = (bf16[512,128]{1,0:T(8,128)(2,1)S(1)}, bf16[512,128]{1,0:T(8,128)(2,1)S(1)}, u32[]{:S(2)}, u32[]{:S(2)}) collective-permute-start(bf16[512,128]{1,0:T(8,128)(2,1)S(1)} %shard_map.89.refs_0_.refs_5_), channel_id=1, source_target_pairs={{0,1},{1,0},{2,3},{3,2},{4,5},{5,4},{6,7},{7,6},{8,9},{9,8},{10,11... | collective-permute-start | bytes 393224 | tf_op jit(solution)/shard_map/ppermute | solution.py:250
  11.3 2.2 %collective-permute-done.1.refs_1_ = bf16[512,128]{1,0:T(8,128)(2,1)S(1)} collective-permute-done((bf16[512,128]{1,0:T(8,128)(2,1)S(1)}, bf16[512,128]{1,0:T(8,128)(2,1)S(1)}, u32[]{:S(2)}, u32[]{:S(2)}) %collective-permute-start.1) | collective-permute-done | bytes 131104 | tf_op jit(solution)/shard_map/ppermute | solution.py:250
  13.5 2.4 %collective-permute-start.7 = (bf16[512,128]{1,0:T(8,128)(2,1)S(1)}, bf16[512,128]{1,0:T(8,128)(2,1)S(1)}, u32[]{:S(2)}, u32[]{:S(2)}) collective-permute-start(bf16[512,128]{1,0:T(8,128)(2,1)S(1)} %collective-permute-done.1.refs_1_), channel_id=1, source_target_pairs={{0,2},{1,3},{2,0},{3,1},{4,6},{5,7},{6,4},{7,5},{8,10},{9,11},{10,... | collective-permute-start | bytes 393224 | tf_op jit(solution)/shard_map/ppermute | solution.py:250
  15.9 1.5 %collective-permute-start.6 = (bf16[512,128]{1,0:T(8,128)(2,1)S(1)}, bf16[512,128]{1,0:T(8,128)(2,1)S(1)}, u32[]{:S(2)}, u32[]{:S(2)}) collective-permute-start(bf16[512,128]{1,0:T(8,128)(2,1)S(1)} %collective-permute-done.1.refs_1_), channel_id=1, source_target_pairs={{0,1},{1,0},{2,3},{3,2},{4,5},{5,4},{6,7},{7,6},{8,9},{9,8},{10,11... | collective-permute-start | bytes 393224 | tf_op jit(solution)/shard_map/ppermute | solution.py:250
  18.4 2.9 %shard_map.87.right = bf16[6,4096,128]{2,1,0:T(8,128)(2,1)S(1)} custom-call(bf16[6,4096,128]{2,1,0:T(8,128)(2,1)} %bitcast.6), custom_call_target="tpu_custom_call" | custom-call | tf_op jit(solution)/shard_map/pallas_call | solution.py:222
  21.3 2.9 %shard_map.86.left = bf16[6,4096,128]{2,1,0:T(8,128)(2,1)S(1)} custom-call(bf16[6,4096,128]{2,1,0:T(8,128)(2,1)} %bitcast.7), custom_call_target="tpu_custom_call" | custom-call | tf_op jit(solution)/shard_map/pallas_call | solution.py:222
  24.8 2.1 %shard_map.90 = (bf16[4224,128]{1,0:T(8,128)(2,1)S(1)}, bf16[512,128]{1,0:T(8,128)(2,1)S(1)}, bf16[512,128]{1,0:T(8,128)(2,1)S(1)}, bf16[512,128]{1,0:T(8,128)(2,1)S(1)}, f32[8,128]{1,0:T(8,128)S(1)}) custom-call(s32[1]{0:T(128)} %bitcast.place, s32[192]{0:T(256)S(1)} %select_n.17.links, bf16[6,4096,128]{2,1,0:T(8,128)(2,1)S(1)} %shard_map.86.left, ...), custom_call_target="tpu_custom_call" | custom-call | tf_op jit(solution)/shard_map/pallas_call | solution.py:211
  26.9 2.3 %collective-permute-start.12 = (bf16[512,128]{1,0:T(8,128)(2,1)S(1)}, bf16[512,128]{1,0:T(8,128)(2,1)S(1)}, u32[]{:S(2)}, u32[]{:S(2)}) collective-permute-start(bf16[512,128]{1,0:T(8,128)(2,1)S(1)} %get-tuple-element.46), channel_id=1, source_target_pairs={{0,3},{1,2},{2,1},{3,0},{4,7},{5,6},{6,5},{7,4},{8,11},{9,10},{10,... | collective-permute-start | bytes 393224 | tf_op jit(solution)/shard_map/ppermute | solution.py:250
  30.4 2.9 %shard_map.91 = (bf16[512,128]{1,0:T(8,128)(2,1)S(1)}, bf16[512,128]{1,0:T(8,128)(2,1)S(1)}, bf16[512,128]{1,0:T(8,128)(2,1)S(1)}, f32[512,128]{1,0:T(8,128)S(1)...) custom-call(s32[1]{0:T(128)} %bitcast.place, s32[192]{0:T(256)S(1)} %select_n.17.links, ...), custom_call_target="tpu_custom_call" | custom-call | tf_op jit(solution)/shard_map/pallas_call | solution.py:211
  33.3 2.9 %collective-permute-start.8 = (f32[8,128]{1,0:T(8,128)S(1)}, f32[8,128]{1,0:T(8,128)S(1)}, u32[]{:S(2)}, u32[]{:S(2)}) collective-permute-start(f32[8,128]{1,0:T(8,128)S(1)} %get-tuple-element.39.mine), channel_id=1, source_target_pairs={{0,4},{1,5},{2,6},{3,7},{4,0},{5,1},{6,2},{7,3},{8,12},{9,13},{10,... | collective-permute-start | bytes 12296 | tf_op jit(solution)/shard_map/ppermute | solution.py:250
  36.2 1.7 %collective-permute-done.8.other = f32[8,128]{1,0:T(8,128)S(1)} collective-permute-done((f32[8,128]{1,0:T(8,128)S(1)}, f32[8,128]{1,0:T(8,128)S(1)}, u32[]{:S(2)}, u32[]{:S(2)}) %collective-permute-start.8) | collective-permute-done | bytes 4128 | tf_op jit(solution)/shard_map/ppermute | solution.py:250
  37.9 2.8 %collective-permute-start.9 = (bf16[528,128]{1,0:T(8,128)(2,1)S(1)}, bf16[528,128]{1,0:T(8,128)(2,1)S(1)}, u32[]{:S(2)}, u32[]{:S(2)}) collective-permute-start(bf16[528,128]{1,0:T(8,128)(2,1)S(1)} %get-tuple-element.42), channel_id=1, source_target_pairs={{0,3},{1,2},{2,1},{3,0},{4,7},{5,6},{6,5},{7,4},{8,11},{9,10},{10,... | collective-permute-start | bytes 405512 | tf_op jit(solution)/shard_map/ppermute | solution.py:250
  41.5 2.9 %collective-permute-start.15 = (bf16[512,128]{1,0:T(8,128)(2,1)S(1)}, bf16[512,128]{1,0:T(8,128)(2,1)S(1)}, u32[]{:S(2)}, u32[]{:S(2)}) collective-permute-start(bf16[512,128]{1,0:T(8,128)(2,1)S(1)} %shard_map.93), channel_id=1, source_target_pairs={{0,4},{1,5},{2,6},{3,7},{4,0},{5,1},{6,2},{7,3},{8,12},{9,13},{10,... | collective-permute-start | bytes 393224 | tf_op jit(solution)/shard_map/ppermute | solution.py:250
  44.4 1.4 %collective-permute-start.16 = (f32[8,128]{1,0:T(8,128)S(1)}, f32[8,128]{1,0:T(8,128)S(1)}, u32[]{:S(2)}, u32[]{:S(2)}) collective-permute-start(f32[8,128]{1,0:T(8,128)S(1)} %get-tuple-element.49.refs_7_), channel_id=1, source_target_pairs={{0,1},{1,0},{2,3},{3,2},{4,5},{5,4},{6,7},{7,6},{8,9},{9,8},{10,11... | collective-permute-start | bytes 12296 | tf_op jit(solution)/shard_map/ppermute | solution.py:250
  45.8 2.2 %collective-permute-done.16.refs_8_ = f32[8,128]{1,0:T(8,128)S(1)} collective-permute-done((f32[8,128]{1,0:T(8,128)S(1)}, f32[8,128]{1,0:T(8,128)S(1)}, u32[]{:S(2)}, u32[]{:S(2)}) %collective-permute-start.16) | collective-permute-done | bytes 4128 | tf_op jit(solution)/shard_map/ppermute | solution.py:250
  48.5 2.4 %collective-permute-start.17 = (bf16[512,128]{1,0:T(8,128)(2,1)S(1)}, bf16[512,128]{1,0:T(8,128)(2,1)S(1)}, u32[]{:S(2)}, u32[]{:S(2)}) collective-permute-start(bf16[512,128]{1,0:T(8,128)(2,1)S(1)} %get-tuple-element.51.refs_0_.vector), channel_id=1, source_target_pairs={{0,4},{1,5},{2,6},{3,7},{4,0},{5,1},{6,2},{7,3},{8,12},{9,13},{10,... | collective-permute-start | bytes 393224 | tf_op jit(solution)/shard_map/ppermute | solution.py:250
  50.8 5.0 %collective-permute-start.20 = (bf16[512,128]{1,0:T(8,128)(2,1)S(1)}, bf16[512,128]{1,0:T(8,128)(2,1)S(1)}, u32[]{:S(2)}, u32[]{:S(2)}) collective-permute-start(bf16[512,128]{1,0:T(8,128)(2,1)S(1)} %get-tuple-element.51.refs_0_.vector), channel_id=1, source_target_pairs={{0,2},{1,3},{2,0},{3,1},{4,6},{5,7},{6,4},{7,5},{8,10},{9,11},{10,... | collective-permute-start | bytes 393224 | tf_op jit(solution)/shard_map/ppermute | solution.py:250
  57.3 2.5 %collective-permute-start.23 = (bf16[512,128]{1,0:T(8,128)(2,1)S(1)}, bf16[512,128]{1,0:T(8,128)(2,1)S(1)}, u32[]{:S(2)}, u32[]{:S(2)}) collective-permute-start(bf16[512,128]{1,0:T(8,128)(2,1)S(1)} %collective-permute-done.17.refs_1_), channel_id=1, source_target_pairs={{0,2},{1,3},{2,0},{3,1},{4,6},{5,7},{6,4},{7,5},{8,10},{9,11},{10,... | collective-permute-start | bytes 393224 | tf_op jit(solution)/shard_map/ppermute | solution.py:250
  61.3 1.6 %collective-permute-done.19.refs_3_ = bf16[512,128]{1,0:T(8,128)(2,1)S(1)} collective-permute-done((bf16[512,128]{1,0:T(8,128)(2,1)S(1)}, bf16[512,128]{1,0:T(8,128)(2,1)S(1)}, u32[]{:S(2)}, u32[]{:S(2)}) %collective-permute-start.19) | collective-permute-done | bytes 131104 | tf_op jit(solution)/shard_map/ppermute | solution.py:250
  63.7 1.1 %collective-permute-done.22.refs_6_ = bf16[512,128]{1,0:T(8,128)(2,1)S(1)} collective-permute-done((bf16[512,128]{1,0:T(8,128)(2,1)S(1)}, bf16[512,128]{1,0:T(8,128)(2,1)S(1)}, u32[]{:S(2)}, u32[]{:S(2)}) %collective-permute-start.22) | collective-permute-done | bytes 131104 | tf_op jit(solution)/shard_map/ppermute | solution.py:250
  64.8 2.7 %collective-permute-done.21.refs_5_ = bf16[512,128]{1,0:T(8,128)(2,1)S(1)} collective-permute-done((bf16[512,128]{1,0:T(8,128)(2,1)S(1)}, bf16[512,128]{1,0:T(8,128)(2,1)S(1)}, u32[]{:S(2)}, u32[]{:S(2)}) %collective-permute-start.21) | collective-permute-done | bytes 131104 | tf_op jit(solution)/shard_map/ppermute | solution.py:250
  67.5 2.1 %shard_map.95 = (bf16[4224,128]{1,0:T(8,128)(2,1)S(1)}, bf16[512,128]{1,0:T(8,128)(2,1)S(1)}, bf16[512,128]{1,0:T(8,128)(2,1)S(1)}, bf16[512,128]{1,0:T(8,128)(2,1)S(1)}) custom-call(s32[1]{0:T(128)} %bitcast.place, s32[192]{0:T(256)S(1)} %select_n.17.links, bf16[6,4096,128]{2,1,0:T(8,128)(2,1)S(1)} %shard_map.86.left, ...), custom_call_target="tpu_custom_call" | custom-call | tf_op jit(solution)/shard_map/pallas_call | solution.py:211
  70.1 1.5 %collective-permute-start.28 = (bf16[512,128]{1,0:T(8,128)(2,1)S(1)}, bf16[512,128]{1,0:T(8,128)(2,1)S(1)}, u32[]{:S(2)}, u32[]{:S(2)}) collective-permute-start(bf16[512,128]{1,0:T(8,128)(2,1)S(1)} %get-tuple-element.59), channel_id=1, source_target_pairs={{0,1},{1,0},{2,3},{3,2},{4,5},{5,4},{6,7},{7,6},{8,9},{9,8},{10,11... | collective-permute-start | bytes 393224 | tf_op jit(solution)/shard_map/ppermute | solution.py:250
  71.6 1.5 %collective-permute-start.29 = (bf16[512,128]{1,0:T(8,128)(2,1)S(1)}, bf16[512,128]{1,0:T(8,128)(2,1)S(1)}, u32[]{:S(2)}, u32[]{:S(2)}) collective-permute-start(bf16[512,128]{1,0:T(8,128)(2,1)S(1)} %get-tuple-element.60), channel_id=1, source_target_pairs={{0,2},{1,3},{2,0},{3,1},{4,6},{5,7},{6,4},{7,5},{8,10},{9,11},{10,... | collective-permute-start | bytes 393224 | tf_op jit(solution)/shard_map/ppermute | solution.py:250
  73.1 2.8 %shard_map.96 = (bf16[512,128]{1,0:T(8,128)(2,1)S(1)}, bf16[512,128]{1,0:T(8,128)(2,1)S(1)}, bf16[512,128]{1,0:T(8,128)(2,1)S(1)}, f32[512,128]{1,0:T(8,128)S(1)}, f32[512,128]{1,0:T(8,128)S(1)}) custom-call(s32[1]{0:T(128)} %bitcast.place, s32[192]{0:T(256)S(1)} %select_n.17.links, bf16[6,4096,128]{2,1,0:T(8,128)(2,1)S(1)} %shard_map.86.left, ...), custom_call_target="tpu_custom_call" | custom-call | tf_op jit(solution)/shard_map/pallas_call | solution.py:211
  76.0 1.2 %collective-permute-start.24 = (bf16[512,128]{1,0:T(8,128)(2,1)S(1)}, bf16[512,128]{1,0:T(8,128)(2,1)S(1)}, u32[]{:S(2)}, u32[]{:S(2)}) collective-permute-start(bf16[512,128]{1,0:T(8,128)(2,1)S(1)} %get-tuple-element.54), channel_id=1, source_target_pairs={{0,3},{1,2},{2,1},{3,0},{4,7},{5,6},{6,5},{7,4},{8,11},{9,10},{10,... | collective-permute-start | bytes 393224 | tf_op jit(solution)/shard_map/ppermute | solution.py:250
  78.0 1.5 %collective-permute-start.26 = (bf16[512,128]{1,0:T(8,128)(2,1)S(1)}, bf16[512,128]{1,0:T(8,128)(2,1)S(1)}, u32[]{:S(2)}, u32[]{:S(2)}) collective-permute-start(bf16[512,128]{1,0:T(8,128)(2,1)S(1)} %get-tuple-element.56), channel_id=1, source_target_pairs={{0,2},{1,3},{2,0},{3,1},{4,6},{5,7},{6,4},{7,5},{8,10},{9,11},{10,... | collective-permute-start | bytes 393224 | tf_op jit(solution)/shard_map/ppermute | solution.py:250
  82.0 1.3 %collective-permute-done.25.refs_1_ = bf16[512,128]{1,0:T(8,128)(2,1)S(1)} collective-permute-done((bf16[512,128]{1,0:T(8,128)(2,1)S(1)}, bf16[512,128]{1,0:T(8,128)(2,1)S(1)}, u32[]{:S(2)}, u32[]{:S(2)}) %collective-permute-start.25) | collective-permute-done | bytes 131104 | tf_op jit(solution)/shard_map/ppermute | solution.py:250
  83.6 3.3 %collective-permute-done.30.refs_3_ = bf16[512,128]{1,0:T(8,128)(2,1)S(1)} collective-permute-done((bf16[512,128]{1,0:T(8,128)(2,1)S(1)}, bf16[512,128]{1,0:T(8,128)(2,1)S(1)}, u32[]{:S(2)}, u32[]{:S(2)}) %collective-permute-start.30) | collective-permute-done | bytes 131104 | tf_op jit(solution)/shard_map/ppermute | solution.py:250
  (49 shorter events, 14.5 us)
Async XLA Ops:
  0.6 3.4 %collective-permute-start = (f32[512]{0:T(512)}, f32[512]{0:T(512)S(1)}, u32[]{:S(2)}, u32[]{:S(2)}) collective-permute-start(f32[512]{0:T(512)} %param.8), channel_id=1, source_target_pairs={{0,8},{8,16},{16,24},{1,9},{9,17},{17,25},{2,10},{10,18},{18,26},{... | collective-permute-start | bytes 6152 | tf_op jit(solution)/shard_map/ppermute | solution.py:14
  4.3 9.2 %collective-permute-start.1 = (bf16[512,128]{1,0:T(8,128)(2,1)S(1)}, bf16[512,128]{1,0:T(8,128)(2,1)S(1)}, u32[]{:S(2)}, u32[]{:S(2)}) collective-permute-start(bf16[512,128]{1,0:T(8,128)(2,1)S(1)} %shard_map.89.refs_0_.refs_5_), channel_id=1, source_target_pairs={{0,4},{1,5},{2,6},{3,7},{4,0},{5,1},{6,2},{7,3},{8,12},{9,13},{10,... | collective-permute-start | bytes 393224 | tf_op jit(solution)/shard_map/ppermute | solution.py:250
  7.8 9.7 %collective-permute-start.4 = (bf16[512,128]{1,0:T(8,128)(2,1)S(1)}, bf16[512,128]{1,0:T(8,128)(2,1)S(1)}, u32[]{:S(2)}, u32[]{:S(2)}) collective-permute-start(bf16[512,128]{1,0:T(8,128)(2,1)S(1)} %shard_map.89.refs_0_.refs_5_), channel_id=1, source_target_pairs={{0,2},{1,3},{2,0},{3,1},{4,6},{5,7},{6,4},{7,5},{8,10},{9,11},{10,... | collective-permute-start | bytes 393224 | tf_op jit(solution)/shard_map/ppermute | solution.py:250
  9.4 14.8 %collective-permute-start.3 = (bf16[512,128]{1,0:T(8,128)(2,1)S(1)}, bf16[512,128]{1,0:T(8,128)(2,1)S(1)}, u32[]{:S(2)}, u32[]{:S(2)}) collective-permute-start(bf16[512,128]{1,0:T(8,128)(2,1)S(1)} %shard_map.89.refs_0_.refs_5_), channel_id=1, source_target_pairs={{0,1},{1,0},{2,3},{3,2},{4,5},{5,4},{6,7},{7,6},{8,9},{9,8},{10,11... | collective-permute-start | bytes 393224 | tf_op jit(solution)/shard_map/ppermute | solution.py:250
  10.9 13.3 %collective-permute-start.2 = (bf16[512,128]{1,0:T(8,128)(2,1)S(1)}, bf16[512,128]{1,0:T(8,128)(2,1)S(1)}, u32[]{:S(2)}, u32[]{:S(2)}) collective-permute-start(bf16[512,128]{1,0:T(8,128)(2,1)S(1)} %shard_map.89.refs_0_.refs_5_), channel_id=1, source_target_pairs={{0,3},{1,2},{2,1},{3,0},{4,7},{5,6},{6,5},{7,4},{8,11},{9,10},{10,... | collective-permute-start | bytes 393224 | tf_op jit(solution)/shard_map/ppermute | solution.py:250
  13.5 10.7 %collective-permute-start.7 = (bf16[512,128]{1,0:T(8,128)(2,1)S(1)}, bf16[512,128]{1,0:T(8,128)(2,1)S(1)}, u32[]{:S(2)}, u32[]{:S(2)}) collective-permute-start(bf16[512,128]{1,0:T(8,128)(2,1)S(1)} %collective-permute-done.1.refs_1_), channel_id=1, source_target_pairs={{0,2},{1,3},{2,0},{3,1},{4,6},{5,7},{6,4},{7,5},{8,10},{9,11},{10,... | collective-permute-start | bytes 393224 | tf_op jit(solution)/shard_map/ppermute | solution.py:250
  15.9 8.3 %collective-permute-start.6 = (bf16[512,128]{1,0:T(8,128)(2,1)S(1)}, bf16[512,128]{1,0:T(8,128)(2,1)S(1)}, u32[]{:S(2)}, u32[]{:S(2)}) collective-permute-start(bf16[512,128]{1,0:T(8,128)(2,1)S(1)} %collective-permute-done.1.refs_1_), channel_id=1, source_target_pairs={{0,1},{1,0},{2,3},{3,2},{4,5},{5,4},{6,7},{7,6},{8,9},{9,8},{10,11... | collective-permute-start | bytes 393224 | tf_op jit(solution)/shard_map/ppermute | solution.py:250
  17.4 7.3 %collective-permute-start.5 = (bf16[512,128]{1,0:T(8,128)(2,1)S(1)}, bf16[512,128]{1,0:T(8,128)(2,1)S(1)}, u32[]{:S(2)}, u32[]{:S(2)}) collective-permute-start(bf16[512,128]{1,0:T(8,128)(2,1)S(1)} %collective-permute-done.1.refs_1_), channel_id=1, source_target_pairs={{0,3},{1,2},{2,1},{3,0},{4,7},{5,6},{6,5},{7,4},{8,11},{9,10},{10,... | collective-permute-start | bytes 393224 | tf_op jit(solution)/shard_map/ppermute | solution.py:250
  24.1 6.3 %copy-start = (f32[512,128]{1,0:T(8,128)S(1)}, f32[512,128]{1,0:T(8,128)}, u32[]{:S(2)}) copy-start(f32[512,128]{1,0:T(8,128)} %hdiag.1) | copy-start | bytes 786436
  26.9 14.1 %collective-permute-start.12 = (bf16[512,128]{1,0:T(8,128)(2,1)S(1)}, bf16[512,128]{1,0:T(8,128)(2,1)S(1)}, u32[]{:S(2)}, u32[]{:S(2)}) collective-permute-start(bf16[512,128]{1,0:T(8,128)(2,1)S(1)} %get-tuple-element.46), channel_id=1, source_target_pairs={{0,3},{1,2},{2,1},{3,0},{4,7},{5,6},{6,5},{7,4},{8,11},{9,10},{10,... | collective-permute-start | bytes 393224 | tf_op jit(solution)/shard_map/ppermute | solution.py:250
  29.1 12.3 %collective-permute-start.13 = (bf16[512,128]{1,0:T(8,128)(2,1)S(1)}, bf16[512,128]{1,0:T(8,128)(2,1)S(1)}, u32[]{:S(2)}, u32[]{:S(2)}) collective-permute-start(bf16[512,128]{1,0:T(8,128)(2,1)S(1)} %get-tuple-element.47), channel_id=1, source_target_pairs={{0,1},{1,0},{2,3},{3,2},{4,5},{5,4},{6,7},{7,6},{8,9},{9,8},{10,11... | collective-permute-start | bytes 393224 | tf_op jit(solution)/shard_map/ppermute | solution.py:250
  29.7 11.8 %collective-permute-start.14 = (bf16[512,128]{1,0:T(8,128)(2,1)S(1)}, bf16[512,128]{1,0:T(8,128)(2,1)S(1)}, u32[]{:S(2)}, u32[]{:S(2)}) collective-permute-start(bf16[512,128]{1,0:T(8,128)(2,1)S(1)} %get-tuple-element.48), channel_id=1, source_target_pairs={{0,2},{1,3},{2,0},{3,1},{4,6},{5,7},{6,4},{7,5},{8,10},{9,11},{10,... | collective-permute-start | bytes 393224 | tf_op jit(solution)/shard_map/ppermute | solution.py:250
  33.3 4.6 %collective-permute-start.8 = (f32[8,128]{1,0:T(8,128)S(1)}, f32[8,128]{1,0:T(8,128)S(1)}, u32[]{:S(2)}, u32[]{:S(2)}) collective-permute-start(f32[8,128]{1,0:T(8,128)S(1)} %get-tuple-element.39.mine), channel_id=1, source_target_pairs={{0,4},{1,5},{2,6},{3,7},{4,0},{5,1},{6,2},{7,3},{8,12},{9,13},{10,... | collective-permute-start | bytes 12296 | tf_op jit(solution)/shard_map/ppermute | solution.py:250
  37.9 10.1 %collective-permute-start.9 = (bf16[528,128]{1,0:T(8,128)(2,1)S(1)}, bf16[528,128]{1,0:T(8,128)(2,1)S(1)}, u32[]{:S(2)}, u32[]{:S(2)}) collective-permute-start(bf16[528,128]{1,0:T(8,128)(2,1)S(1)} %get-tuple-element.42), channel_id=1, source_target_pairs={{0,3},{1,2},{2,1},{3,0},{4,7},{5,6},{6,5},{7,4},{8,11},{9,10},{10,... | collective-permute-start | bytes 405512 | tf_op jit(solution)/shard_map/ppermute | solution.py:250
  40.7 7.5 %collective-permute-start.11 = (bf16[528,128]{1,0:T(8,128)(2,1)S(1)}, bf16[528,128]{1,0:T(8,128)(2,1)S(1)}, u32[]{:S(2)}, u32[]{:S(2)}) collective-permute-start(bf16[528,128]{1,0:T(8,128)(2,1)S(1)} %get-tuple-element.44), channel_id=1, source_target_pairs={{0,2},{1,3},{2,0},{3,1},{4,6},{5,7},{6,4},{7,5},{8,10},{9,11},{10,... | collective-permute-start | bytes 405512 | tf_op jit(solution)/shard_map/ppermute | solution.py:250
  40.9 7.1 %collective-permute-start.10 = (bf16[512,128]{1,0:T(8,128)(2,1)S(1)}, bf16[512,128]{1,0:T(8,128)(2,1)S(1)}, u32[]{:S(2)}, u32[]{:S(2)}) collective-permute-start(bf16[512,128]{1,0:T(8,128)(2,1)S(1)} %get-tuple-element.43), channel_id=1, source_target_pairs={{0,1},{1,0},{2,3},{3,2},{4,5},{5,4},{6,7},{7,6},{8,9},{9,8},{10,11... | collective-permute-start | bytes 393224 | tf_op jit(solution)/shard_map/ppermute | solution.py:250
  41.5 6.7 %collective-permute-start.15 = (bf16[512,128]{1,0:T(8,128)(2,1)S(1)}, bf16[512,128]{1,0:T(8,128)(2,1)S(1)}, u32[]{:S(2)}, u32[]{:S(2)}) collective-permute-start(bf16[512,128]{1,0:T(8,128)(2,1)S(1)} %shard_map.93), channel_id=1, source_target_pairs={{0,4},{1,5},{2,6},{3,7},{4,0},{5,1},{6,2},{7,3},{8,12},{9,13},{10,... | collective-permute-start | bytes 393224 | tf_op jit(solution)/shard_map/ppermute | solution.py:250
  44.4 3.6 %collective-permute-start.16 = (f32[8,128]{1,0:T(8,128)S(1)}, f32[8,128]{1,0:T(8,128)S(1)}, u32[]{:S(2)}, u32[]{:S(2)}) collective-permute-start(f32[8,128]{1,0:T(8,128)S(1)} %get-tuple-element.49.refs_7_), channel_id=1, source_target_pairs={{0,1},{1,0},{2,3},{3,2},{4,5},{5,4},{6,7},{7,6},{8,9},{9,8},{10,11... | collective-permute-start | bytes 12296 | tf_op jit(solution)/shard_map/ppermute | solution.py:250
  48.5 8.8 %collective-permute-start.17 = (bf16[512,128]{1,0:T(8,128)(2,1)S(1)}, bf16[512,128]{1,0:T(8,128)(2,1)S(1)}, u32[]{:S(2)}, u32[]{:S(2)}) collective-permute-start(bf16[512,128]{1,0:T(8,128)(2,1)S(1)} %get-tuple-element.51.refs_0_.vector), channel_id=1, source_target_pairs={{0,4},{1,5},{2,6},{3,7},{4,0},{5,1},{6,2},{7,3},{8,12},{9,13},{10,... | collective-permute-start | bytes 393224 | tf_op jit(solution)/shard_map/ppermute | solution.py:250
  50.8 10.0 %collective-permute-start.20 = (bf16[512,128]{1,0:T(8,128)(2,1)S(1)}, bf16[512,128]{1,0:T(8,128)(2,1)S(1)}, u32[]{:S(2)}, u32[]{:S(2)}) collective-permute-start(bf16[512,128]{1,0:T(8,128)(2,1)S(1)} %get-tuple-element.51.refs_0_.vector), channel_id=1, source_target_pairs={{0,2},{1,3},{2,0},{3,1},{4,6},{5,7},{6,4},{7,5},{8,10},{9,11},{10,... | collective-permute-start | bytes 393224 | tf_op jit(solution)/shard_map/ppermute | solution.py:250
  55.8 7.1 %collective-permute-start.19 = (bf16[512,128]{1,0:T(8,128)(2,1)S(1)}, bf16[512,128]{1,0:T(8,128)(2,1)S(1)}, u32[]{:S(2)}, u32[]{:S(2)}) collective-permute-start(bf16[512,128]{1,0:T(8,128)(2,1)S(1)} %get-tuple-element.51.refs_0_.vector), channel_id=1, source_target_pairs={{0,1},{1,0},{2,3},{3,2},{4,5},{5,4},{6,7},{7,6},{8,9},{9,8},{10,11... | collective-permute-start | bytes 393224 | tf_op jit(solution)/shard_map/ppermute | solution.py:250
  56.5 6.4 %collective-permute-start.18 = (bf16[512,128]{1,0:T(8,128)(2,1)S(1)}, bf16[512,128]{1,0:T(8,128)(2,1)S(1)}, u32[]{:S(2)}, u32[]{:S(2)}) collective-permute-start(bf16[512,128]{1,0:T(8,128)(2,1)S(1)} %get-tuple-element.51.refs_0_.vector), channel_id=1, source_target_pairs={{0,3},{1,2},{2,1},{3,0},{4,7},{5,6},{6,5},{7,4},{8,11},{9,10},{10,... | collective-permute-start | bytes 393224 | tf_op jit(solution)/shard_map/ppermute | solution.py:250
  57.3 6.4 %collective-permute-start.23 = (bf16[512,128]{1,0:T(8,128)(2,1)S(1)}, bf16[512,128]{1,0:T(8,128)(2,1)S(1)}, u32[]{:S(2)}, u32[]{:S(2)}) collective-permute-start(bf16[512,128]{1,0:T(8,128)(2,1)S(1)} %collective-permute-done.17.refs_1_), channel_id=1, source_target_pairs={{0,2},{1,3},{2,0},{3,1},{4,6},{5,7},{6,4},{7,5},{8,10},{9,11},{10,... | collective-permute-start | bytes 393224 | tf_op jit(solution)/shard_map/ppermute | solution.py:250
  59.8 5.0 %collective-permute-start.22 = (bf16[512,128]{1,0:T(8,128)(2,1)S(1)}, bf16[512,128]{1,0:T(8,128)(2,1)S(1)}, u32[]{:S(2)}, u32[]{:S(2)}) collective-permute-start(bf16[512,128]{1,0:T(8,128)(2,1)S(1)} %collective-permute-done.17.refs_1_), channel_id=1, source_target_pairs={{0,1},{1,0},{2,3},{3,2},{4,5},{5,4},{6,7},{7,6},{8,9},{9,8},{10,11... | collective-permute-start | bytes 393224 | tf_op jit(solution)/shard_map/ppermute | solution.py:250
  60.9 6.6 %collective-permute-start.21 = (bf16[512,128]{1,0:T(8,128)(2,1)S(1)}, bf16[512,128]{1,0:T(8,128)(2,1)S(1)}, u32[]{:S(2)}, u32[]{:S(2)}) collective-permute-start(bf16[512,128]{1,0:T(8,128)(2,1)S(1)} %collective-permute-done.17.refs_1_), channel_id=1, source_target_pairs={{0,3},{1,2},{2,1},{3,0},{4,7},{5,6},{6,5},{7,4},{8,11},{9,10},{10,... | collective-permute-start | bytes 393224 | tf_op jit(solution)/shard_map/ppermute | solution.py:250
  69.6 8.5 %collective-permute-start.27 = (bf16[512,128]{1,0:T(8,128)(2,1)S(1)}, bf16[512,128]{1,0:T(8,128)(2,1)S(1)}, u32[]{:S(2)}, u32[]{:S(2)}) collective-permute-start(bf16[512,128]{1,0:T(8,128)(2,1)S(1)} %get-tuple-element.58), channel_id=1, source_target_pairs={{0,3},{1,2},{2,1},{3,0},{4,7},{5,6},{6,5},{7,4},{8,11},{9,10},{10,... | collective-permute-start | bytes 393224 | tf_op jit(solution)/shard_map/ppermute | solution.py:250
  70.1 9.4 %collective-permute-start.28 = (bf16[512,128]{1,0:T(8,128)(2,1)S(1)}, bf16[512,128]{1,0:T(8,128)(2,1)S(1)}, u32[]{:S(2)}, u32[]{:S(2)}) collective-permute-start(bf16[512,128]{1,0:T(8,128)(2,1)S(1)} %get-tuple-element.59), channel_id=1, source_target_pairs={{0,1},{1,0},{2,3},{3,2},{4,5},{5,4},{6,7},{7,6},{8,9},{9,8},{10,11... | collective-permute-start | bytes 393224 | tf_op jit(solution)/shard_map/ppermute | solution.py:250
  71.6 7.9 %collective-permute-start.29 = (bf16[512,128]{1,0:T(8,128)(2,1)S(1)}, bf16[512,128]{1,0:T(8,128)(2,1)S(1)}, u32[]{:S(2)}, u32[]{:S(2)}) collective-permute-start(bf16[512,128]{1,0:T(8,128)(2,1)S(1)} %get-tuple-element.60), channel_id=1, source_target_pairs={{0,2},{1,3},{2,0},{3,1},{4,6},{5,7},{6,4},{7,5},{8,10},{9,11},{10,... | collective-permute-start | bytes 393224 | tf_op jit(solution)/shard_map/ppermute | solution.py:250
  76.0 6.0 %collective-permute-start.24 = (bf16[512,128]{1,0:T(8,128)(2,1)S(1)}, bf16[512,128]{1,0:T(8,128)(2,1)S(1)}, u32[]{:S(2)}, u32[]{:S(2)}) collective-permute-start(bf16[512,128]{1,0:T(8,128)(2,1)S(1)} %get-tuple-element.54), channel_id=1, source_target_pairs={{0,3},{1,2},{2,1},{3,0},{4,7},{5,6},{6,5},{7,4},{8,11},{9,10},{10,... | collective-permute-start | bytes 393224 | tf_op jit(solution)/shard_map/ppermute | solution.py:250
  77.2 6.1 %collective-permute-start.25 = (bf16[512,128]{1,0:T(8,128)(2,1)S(1)}, bf16[512,128]{1,0:T(8,128)(2,1)S(1)}, u32[]{:S(2)}, u32[]{:S(2)}) collective-permute-start(bf16[512,128]{1,0:T(8,128)(2,1)S(1)} %get-tuple-element.55), channel_id=1, source_target_pairs={{0,1},{1,0},{2,3},{3,2},{4,5},{5,4},{6,7},{7,6},{8,9},{9,8},{10,11... | collective-permute-start | bytes 393224 | tf_op jit(solution)/shard_map/ppermute | solution.py:250
  78.0 5.6 %collective-permute-start.26 = (bf16[512,128]{1,0:T(8,128)(2,1)S(1)}, bf16[512,128]{1,0:T(8,128)(2,1)S(1)}, u32[]{:S(2)}, u32[]{:S(2)}) collective-permute-start(bf16[512,128]{1,0:T(8,128)(2,1)S(1)} %get-tuple-element.56), channel_id=1, source_target_pairs={{0,2},{1,3},{2,0},{3,1},{4,6},{5,7},{6,4},{7,5},{8,10},{9,11},{10,... | collective-permute-start | bytes 393224 | tf_op jit(solution)/shard_map/ppermute | solution.py:250
  79.6 7.3 %collective-permute-start.30 = (bf16[512,128]{1,0:T(8,128)(2,1)S(1)}, bf16[512,128]{1,0:T(8,128)(2,1)S(1)}, u32[]{:S(2)}, u32[]{:S(2)}) collective-permute-start(bf16[512,128]{1,0:T(8,128)(2,1)S(1)} %shard_map.97), channel_id=1, source_target_pairs={{0,4},{1,5},{2,6},{3,7},{4,0},{5,1},{6,2},{7,3},{8,12},{9,13},{10,... | collective-permute-start | bytes 393224 | tf_op jit(solution)/shard_map/ppermute | solution.py:250

commit v4 on v3

--- a/solution.py
+++ b/solution.py
@@ -52,13 +52,13 @@
     return (sigma_two, quotient.reshape(1))
 
 
-def scaled_products(vector, links, left, right, chunks, per, store):
+def scaled_products(vector, links, left, right, chunks, per, packed, store):
     width = vector.shape[1]
     nsector = vector.shape[0] // width - 1
     nterms = left.shape[0]
 
-    def inner_of(i):
-        rows = pl.ds(pl.multiple_of(i * width, width), width)
+    def inner_of(i, t, place):
+        rows = pl.ds((t * per + place) * width if packed else pl.multiple_of(i * width, width), width)
         blocks = []
         for k in range(nterms):
             at = pl.multiple_of(links[k * nsector + i] * width, width)
@@ -73,7 +73,7 @@
     waiting = None
     for t, chunk in enumerate(chunks):
         for i in range(per):
-            now = inner_of(chunk * per + i)
+            now = inner_of(chunk * per + i, t, i)
             if waiting is not None:
                 store(*waiting[:2], outer_of(*waiting[2]))
             waiting = (t, i, now)
@@ -91,7 +91,7 @@
 TAIL = 16
 
 
-def chunk_sums(offsets, rows, place, links, left, right, vector, outs, numer):
+def chunk_sums(offsets, rows, place, links, left, right, vector, outs, numer, packed=False):
     width = vector.shape[1]
     chunks = [place[0] ^ offset for offset in offsets]
 
@@ -102,7 +102,7 @@
             start = pl.multiple_of(chunks[t] * rows + i * width, width)
             numer[...] += squares(sums, vector[pl.ds(start, width), :].astype(jnp.float32))
 
-    scaled_products(vector, links, left, right, chunks, rows // width, store)
+    scaled_products(vector, links, left, right, chunks, rows // width, packed, store)
 
 
 def first_kernel(offsets, first, dots, place, links, left, right, *refs):
@@ -115,7 +115,7 @@
     numer = outs[-1] if dots else None
     if dots:
         numer[...] = jnp.zeros_like(numer)
-    chunk_sums(first, rows, place, links, left, right, vector, outs, numer)
+    chunk_sums(first, rows, place, links, left, right, vector, outs, numer, packed=True)
 
 
 def last_kernel(offsets, dots, place, links, left, right, vector, *refs):
@@ -142,14 +142,14 @@
     return tail.astype(jnp.bfloat16)
 
 
-def tail_kernel(nlate, mine, other, *refs):
-    chunks, both, outs = refs[:nlate], refs[nlate], refs[nlate + 1 :]
-    both[...] = mine[...] + other[...]
-    tail = three_roundings(jnp.sum(both[...], axis=0, keepdims=True))
-    for chunk, out in zip(chunks, outs):
-        rows = chunk.shape[0]
-        out[:rows, :] = chunk[...]
-        out[rows:, :] = tail
+def plus_kernel(mine, other, out):
+    out[...] = mine[...] + other[...]
+
+
+def tail_kernel(chunk, part, out):
+    rows = chunk.shape[0]
+    out[:rows, :] = chunk[...]
+    out[rows:, :] = three_roundings(jnp.sum(part[...], axis=0, keepdims=True))
 
 
 def added_kernel(kept, *refs):
@@ -170,10 +170,10 @@
 
 def correct_kernel(nmore, *refs):
     kept, more, refs = refs[0], refs[1 : 1 + nmore], refs[1 + nmore :]
-    psi, hdiag, mine, other, denom, correction, theta = refs
+    psi, hdiag, part, denom, correction, theta = refs
     rows = psi.shape[0]
     total = kept[...]
-    numer = jnp.sum(mine[...] + other[...], keepdims=True)
+    numer = jnp.sum(part[...], keepdims=True)
     for m in more:
         total = total + m[:rows, :].astype(jnp.float32)
         if m.shape[0] > rows:
@@ -203,6 +203,18 @@
         copy.wait()
 
 
+def load_chunks_kernel(offsets, place, source, target, sems):
+    rows = target.shape[1] // len(offsets)
+    copies = [
+        pltpu.make_async_copy(source.at[:, rows_at(place[0] ^ offset, rows)], target.at[:, pl.ds(t * rows, rows)], sems.at[t])
+        for t, offset in enumerate(offsets)
+    ]
+    for copy in copies:
+        copy.start()
+    for copy in copies:
+        copy.wait()
+
+
 VMEM = pl.BlockSpec(memory_space=pltpu.VMEM)
 SMEM = pl.BlockSpec(memory_space=pltpu.SMEM)
 
@@ -227,6 +239,19 @@
         scratch_shapes=[pltpu.SemaphoreType.DMA((count,))],
         compiler_params=pltpu.CompilerParams(vmem_limit_bytes=1 << 20),
     )(pltpu.with_memory_space_constraint(array, pltpu.HBM))
+    return pltpu.with_memory_space_constraint(held, pltpu.VMEM)
+
+
+def loaded_chunks(place, operators, offsets, rows):
+    nterms, _, width = operators.shape
+    held = pl.pallas_call(
+        partial(load_chunks_kernel, offsets),
+        out_shape=pltpu.VMEM((nterms, len(offsets) * rows, width), operators.dtype),
+        in_specs=[SMEM, pl.BlockSpec(memory_space=pltpu.HBM)],
+        out_specs=VMEM,
+        scratch_shapes=[pltpu.SemaphoreType.DMA((len(offsets),))],
+        compiler_params=pltpu.CompilerParams(vmem_limit_bytes=1 << 20),
+    )(place, pltpu.with_memory_space_constraint(operators, pltpu.HBM))
     return pltpu.with_memory_space_constraint(held, pltpu.VMEM)
 
 
@@ -257,21 +282,18 @@
             pieces[half ^ r] = exchange(pieces[half], r)
         return pieces
 
-    def apply_terms(pieces, left, right, dots):
+    def apply_terms(pieces, lead_left, left, lead_right, right, dots):
         across = [half ^ r for r in inside]
-        soon = inside.index(1)
-        late = [t for t in range(len(inside)) if t != soon]
         whole = shape((devices * rows + width, width), jnp.bfloat16)
-        fixed = (place, links, left, right)
         vector, *lead = on_chip(
             partial(first_kernel, list(pieces), across, dots),
             [whole] + [sent] * len(across) + [tile] * dots,
-            2, *fixed, *pieces.values(),
+            2, place, links, lead_left, lead_right, *pieces.values(),
         )
         outs = on_chip(
             partial(last_kernel, inside + [half, 0], dots),
             [sent] * len(inside) + [kept] * 2 + [tile] * (2 * dots),
-            2, *fixed, vector, *((hdiag, lead[-1]) if dots else ()),
+            2, place, links, left, right, vector, *((hdiag, lead[-1]) if dots else ()),
         )
         ours, (crossing, own, *sums) = outs[: len(inside)], outs[len(inside) :]
         if dots:
@@ -281,28 +303,28 @@
         crossing = on_chip(added_kernel, [sent], 0, crossing, *came)[0]
         theirs = exchange(crossing, half)
         if dots:
-            both, *tails = on_chip(
-                partial(tail_kernel, len(ours) - 1), [tile] + [tailed] * (len(ours) - 1), 0, numer, other, *(ours[t] for t in late)
-            )
-            beside = exchange(both, inside[soon])
-            for t, message in zip(late, tails):
-                ours[t] = message
-            sums = [both, beside, denom]
+            part = on_chip(plus_kernel, [tile], 0, numer, other)[0]
+            for b in [1 << b for b in range(half.bit_length() - 2)]:
+                part = on_chip(plus_kernel, [tile], 0, part, exchange(part, b))[0]
+            if inside:
+                ours[-1] = on_chip(tail_kernel, [tailed], 0, ours[-1], part)[0]
+            sums = [part, denom]
         ours = [exchange(chunk, r) for r, chunk in zip(inside, ours)]
         return [own, *ours, theirs], sums
 
-    nterms = left_ops.shape[1]
     links = jnp.where(blockmask[0] != 0, couple[0], nsector).reshape(-1)
     place, links, left_ops, right_operators = lax.optimization_barrier((place, links, left_ops, right_operators))
-    left = loaded(left_ops[0], nterms)
-    right = loaded(right_operators[0], nterms)
+    lead_left = loaded_chunks(place, left_ops[0], [half ^ r for r in inside], rows)
+    left = pltpu.with_memory_space_constraint(left_ops[0], pltpu.VMEM)
+    lead_right = loaded_chunks(place, right_operators[0], [half ^ r for r in inside], rows)
+    right = pltpu.with_memory_space_constraint(right_operators[0], pltpu.VMEM)
     earlier = shifted(lam, "seg", 1)
     weights = jnp.where(lax.axis_index("seg") == 0, jnp.ones_like(earlier), earlier).reshape(-1, width)
     held = loaded(amat, 1)
     psi = on_chip(weigh_kernel, [sent], 0, weights, held)[0]
-    terms, sums = apply_terms(gather(psi), left, right, True)
+    terms, sums = apply_terms(gather(psi), lead_left, left, lead_right, right, True)
     correction, theta = on_chip(partial(correct_kernel, half), [sent, tile], 0, *terms, psi, hdiag, *sums)
-    terms, _ = apply_terms(gather(correction), left, right, False)
+    terms, _ = apply_terms(gather(correction), lead_left, left, lead_right, right, False)
     sigma_two = on_chip(final_kernel, [kept], 0, terms[0], correction, hdiag, *terms[1:])[0]
     return (sigma_two, theta[0, :1])
 

time: 87.9 us -> 89.9 us (1.023)
  waiting for transfers between devices: 18.9 us -> 23.7 us
  Pallas kernels: 18 us -> 16.2 us
  starting transfers between devices: 48.8 us -> 47.5 us
    pallas_call x3 -> x1, Pallas kernels: 6.62 us -> 0.91 us  [loaded(): pl.pallas_call(load_kernel, out_shape=pltpu.VMEM(array.shape, array.dtype...]
    ppermute x30, waiting for transfers between devices: 18.8 us -> 23.7 us  [exchange(): return lax.ppermute(array, 'ops', [(o, o ^ by) for o in range(devices)])]
    pallas_call x0 -> x2, Pallas kernels: none -> 3.61 us  [loaded_chunks(): pl.pallas_call(partial(load_chunks_kernel, offsets), out_shape=pltpu.VMEM...]
    ppermute x30, starting transfers between devices: 46.4 us -> 45.1 us  [exchange(): return lax.ppermute(array, 'ops', [(o, o ^ by) for o in range(devices)])]
    pallas_call x10 -> x12, Pallas kernels: 11.4 us -> 11.6 us  [on_chip(): pl.pallas_call(kernel, out_shape=out_shape, in_specs=[SMEM] * nscalar + [...]
  transfers between devices with their start and end apart: 31 -> 31, of which waited for: 14 -> 16; matrix products, arithmetic and copies ran while one was open for 1% -> 1% of each run, Pallas kernels for 14% -> 12%
where the time goes in v4:
time: 89.9 us; the launch traced here: 89.6 us
  starting transfers between devices  47.5 us (53%)
  waiting for transfers between devices  23.7 us (26%)
  Pallas kernels  16.2 us (18%)
    ppermute x30, starting transfers between devices, exchange(): return lax.ppermute(array, 'ops', [(o, o ^ by) for o in range(devices)])  45.1 us
    ppermute x30, waiting for transfers between devices, exchange(): return lax.ppermute(array, 'ops', [(o, o ^ by) for o in range(devices)])  23.7 us
    pallas_call x12, Pallas kernels, on_chip(): pl.pallas_call(kernel, out_shape=out_shape, in_specs=[SMEM] * nscalar + [...  11.6 us
    pallas_call x2, Pallas kernels, loaded_chunks(): pl.pallas_call(partial(load_chunks_kernel, offsets), out_shape=pltpu.VMEM...  3.61 us
    ppermute x1, starting transfers between devices, shifted(): return lax.ppermute(array, axis, pairs)  2.4 us
  transfers between devices with their start and end apart: 31, of which 16 were waited for; matrix products, arithmetic and copies ran while one was open for 1% of the time, Pallas kernels for 12%

profile of v4, /device:TPU:0, one launch (start us, length us, event | category | flops | bytes accessed | tf_op | source)
XLA Modules:
  0.0 89.6 jit_solution(5292506007122248588)
XLA Ops:
  0.6 2.4 %collective-permute-start = (f32[512]{0:T(512)}, f32[512]{0:T(512)S(1)}, u32[]{:S(2)}, u32[]{:S(2)}) collective-permute-start(f32[512]{0:T(512)} %param.8), channel_id=1, source_target_pairs={{0,8},{8,16},{16,24},{1,9},{9,17},{17,25},{2,10},{10,18},{18,26},{... | collective-permute-start | bytes 6152 | tf_op jit(solution)/shard_map/ppermute | solution.py:14
  4.3 3.5 %collective-permute-start.1 = (bf16[512,128]{1,0:T(8,128)(2,1)S(1)}, bf16[512,128]{1,0:T(8,128)(2,1)S(1)}, u32[]{:S(2)}, u32[]{:S(2)}) collective-permute-start(bf16[512,128]{1,0:T(8,128)(2,1)S(1)} %shard_map.89.refs_0_.refs_5_), channel_id=1, source_target_pairs={{0,4},{1,5},{2,6},{3,7},{4,0},{5,1},{6,2},{7,3},{8,12},{9,13},{10,... | collective-permute-start | bytes 393224 | tf_op jit(solution)/shard_map/ppermute | solution.py:275
  7.8 1.6 %collective-permute-start.4 = (bf16[512,128]{1,0:T(8,128)(2,1)S(1)}, bf16[512,128]{1,0:T(8,128)(2,1)S(1)}, u32[]{:S(2)}, u32[]{:S(2)}) collective-permute-start(bf16[512,128]{1,0:T(8,128)(2,1)S(1)} %shard_map.89.refs_0_.refs_5_), channel_id=1, source_target_pairs={{0,2},{1,3},{2,0},{3,1},{4,6},{5,7},{6,4},{7,5},{8,10},{9,11},{10,... | collective-permute-start | bytes 393224 | tf_op jit(solution)/shard_map/ppermute | solution.py:275
  9.4 1.5 %collective-permute-start.3 = (bf16[512,128]{1,0:T(8,128)(2,1)S(1)}, bf16[512,128]{1,0:T(8,128)(2,1)S(1)}, u32[]{:S(2)}, u32[]{:S(2)}) collective-permute-start(bf16[512,128]{1,0:T(8,128)(2,1)S(1)} %shard_map.89.refs_0_.refs_5_), channel_id=1, source_target_pairs={{0,1},{1,0},{2,3},{3,2},{4,5},{5,4},{6,7},{7,6},{8,9},{9,8},{10,11... | collective-permute-start | bytes 393224 | tf_op jit(solution)/shard_map/ppermute | solution.py:275
  11.3 2.2 %collective-permute-done.1.refs_1_ = bf16[512,128]{1,0:T(8,128)(2,1)S(1)} collective-permute-done((bf16[512,128]{1,0:T(8,128)(2,1)S(1)}, bf16[512,128]{1,0:T(8,128)(2,1)S(1)}, u32[]{:S(2)}, u32[]{:S(2)}) %collective-permute-start.1) | collective-permute-done | bytes 131104 | tf_op jit(solution)/shard_map/ppermute | solution.py:275
  13.5 2.4 %collective-permute-start.7 = (bf16[512,128]{1,0:T(8,128)(2,1)S(1)}, bf16[512,128]{1,0:T(8,128)(2,1)S(1)}, u32[]{:S(2)}, u32[]{:S(2)}) collective-permute-start(bf16[512,128]{1,0:T(8,128)(2,1)S(1)} %collective-permute-done.1.refs_1_), channel_id=1, source_target_pairs={{0,2},{1,3},{2,0},{3,1},{4,6},{5,7},{6,4},{7,5},{8,10},{9,11},{10,... | collective-permute-start | bytes 393224 | tf_op jit(solution)/shard_map/ppermute | solution.py:275
  15.9 1.5 %collective-permute-start.6 = (bf16[512,128]{1,0:T(8,128)(2,1)S(1)}, bf16[512,128]{1,0:T(8,128)(2,1)S(1)}, u32[]{:S(2)}, u32[]{:S(2)}) collective-permute-start(bf16[512,128]{1,0:T(8,128)(2,1)S(1)} %collective-permute-done.1.refs_1_), channel_id=1, source_target_pairs={{0,1},{1,0},{2,3},{3,2},{4,5},{5,4},{6,7},{7,6},{8,9},{9,8},{10,11... | collective-permute-start | bytes 393224 | tf_op jit(solution)/shard_map/ppermute | solution.py:275
  18.4 1.8 %shard_map.87.right = bf16[6,1536,128]{2,1,0:T(8,128)(2,1)S(1)} custom-call(s32[1]{0:T(128)} %bitcast.place, bf16[6,4096,128]{2,1,0:T(8,128)(2,1)} %bitcast.11), custom_call_target="tpu_custom_call" | custom-call | tf_op jit(solution)/shard_map/pallas_call | solution.py:247
  20.2 1.8 %shard_map.86.left = bf16[6,1536,128]{2,1,0:T(8,128)(2,1)S(1)} custom-call(s32[1]{0:T(128)} %bitcast.place, bf16[6,4096,128]{2,1,0:T(8,128)(2,1)} %bitcast.6), custom_call_target="tpu_custom_call" | custom-call | tf_op jit(solution)/shard_map/pallas_call | solution.py:247
  23.3 1.4 %collective-permute-done.5.refs_5_ = bf16[512,128]{1,0:T(8,128)(2,1)S(1)} collective-permute-done((bf16[512,128]{1,0:T(8,128)(2,1)S(1)}, bf16[512,128]{1,0:T(8,128)(2,1)S(1)}, u32[]{:S(2)}, u32[]{:S(2)}) %collective-permute-start.5) | collective-permute-done | bytes 131104 | tf_op jit(solution)/shard_map/ppermute | solution.py:275
  24.8 2.2 %shard_map.90 = (bf16[4224,128]{1,0:T(8,128)(2,1)S(1)}, bf16[512,128]{1,0:T(8,128)(2,1)S(1)}, bf16[512,128]{1,0:T(8,128)(2,1)S(1)}, bf16[512,128]{1,0:T(8,128)(2,1)S(1)}, f32[8,128]{1,0:T(8,128)S(1)}) custom-call(s32[1]{0:T(128)} %bitcast.place, s32[192]{0:T(256)S(1)} %select_n.17.links, bf16[6,1536,128]{2,1,0:T(8,128)(2,1)S(1)} %shard_map.86.left, ...), custom_call_target="tpu_custom_call" | custom-call | tf_op jit(solution)/shard_map/pallas_call | solution.py:223
  26.9 1.8 %collective-permute-start.13 = (bf16[512,128]{1,0:T(8,128)(2,1)S(1)}, bf16[512,128]{1,0:T(8,128)(2,1)S(1)}, u32[]{:S(2)}, u32[]{:S(2)}) collective-permute-start(bf16[512,128]{1,0:T(8,128)(2,1)S(1)} %get-tuple-element.41), channel_id=1, source_target_pairs={{0,3},{1,2},{2,1},{3,0},{4,7},{5,6},{6,5},{7,4},{8,11},{9,10},{10,... | collective-permute-start | bytes 393224 | tf_op jit(solution)/shard_map/ppermute | solution.py:275
  30.5 3.0 %shard_map.91 = (bf16[512,128]{1,0:T(8,128)(2,1)S(1)}, bf16[512,128]{1,0:T(8,128)(2,1)S(1)}, bf16[512,128]{1,0:T(8,128)(2,1)S(1)}, f32[512,128]{1,0:T(8,128)S(1)...) custom-call(s32[1]{0:T(128)} %bitcast.place, s32[192]{0:T(256)S(1)} %select_n.17.links, ...), custom_call_target="tpu_custom_call" | custom-call | tf_op jit(solution)/shard_map/pallas_call | solution.py:223
  33.5 2.7 %collective-permute-start.10 = (f32[8,128]{1,0:T(8,128)S(1)}, f32[8,128]{1,0:T(8,128)S(1)}, u32[]{:S(2)}, u32[]{:S(2)}) collective-permute-start(f32[8,128]{1,0:T(8,128)S(1)} %get-tuple-element.39.mine), channel_id=1, source_target_pairs={{0,4},{1,5},{2,6},{3,7},{4,0},{5,1},{6,2},{7,3},{8,12},{9,13},{10,... | collective-permute-start | bytes 12296 | tf_op jit(solution)/shard_map/ppermute | solution.py:275
  36.3 1.9 %collective-permute-done.10.other = f32[8,128]{1,0:T(8,128)S(1)} collective-permute-done((f32[8,128]{1,0:T(8,128)S(1)}, f32[8,128]{1,0:T(8,128)S(1)}, u32[]{:S(2)}, u32[]{:S(2)}) %collective-permute-start.10) | collective-permute-done | bytes 4128 | tf_op jit(solution)/shard_map/ppermute | solution.py:275
  39.4 2.3 %collective-permute-done.11.other = f32[8,128]{1,0:T(8,128)S(1)} collective-permute-done((f32[8,128]{1,0:T(8,128)S(1)}, f32[8,128]{1,0:T(8,128)S(1)}, u32[]{:S(2)}, u32[]{:S(2)}) %collective-permute-start.11) | collective-permute-done | bytes 4128 | tf_op jit(solution)/shard_map/ppermute | solution.py:275
  41.7 1.4 %collective-permute-start.12 = (bf16[528,128]{1,0:T(8,128)(2,1)S(1)}, bf16[528,128]{1,0:T(8,128)(2,1)S(1)}, u32[]{:S(2)}, u32[]{:S(2)}) collective-permute-start(bf16[528,128]{1,0:T(8,128)(2,1)S(1)} %shard_map.94), channel_id=1, source_target_pairs={{0,2},{1,3},{2,0},{3,1},{4,6},{5,7},{6,4},{7,5},{8,10},{9,11},{10,... | collective-permute-start | bytes 405512 | tf_op jit(solution)/shard_map/ppermute | solution.py:275
  43.1 1.4 %collective-permute-start.8 = (bf16[512,128]{1,0:T(8,128)(2,1)S(1)}, bf16[512,128]{1,0:T(8,128)(2,1)S(1)}, u32[]{:S(2)}, u32[]{:S(2)}) collective-permute-start(bf16[512,128]{1,0:T(8,128)(2,1)S(1)} %get-tuple-element.36), channel_id=1, source_target_pairs={{0,3},{1,2},{2,1},{3,0},{4,7},{5,6},{6,5},{7,4},{8,11},{9,10},{10,... | collective-permute-start | bytes 393224 | tf_op jit(solution)/shard_map/ppermute | solution.py:275
  45.4 2.7 %collective-permute-start.16 = (bf16[512,128]{1,0:T(8,128)(2,1)S(1)}, bf16[512,128]{1,0:T(8,128)(2,1)S(1)}, u32[]{:S(2)}, u32[]{:S(2)}) collective-permute-start(bf16[512,128]{1,0:T(8,128)(2,1)S(1)} %shard_map.95), channel_id=1, source_target_pairs={{0,4},{1,5},{2,6},{3,7},{4,0},{5,1},{6,2},{7,3},{8,12},{9,13},{10,... | collective-permute-start | bytes 393224 | tf_op jit(solution)/shard_map/ppermute | solution.py:275
  48.1 1.6 %collective-permute-done.8.refs_1_ = bf16[512,128]{1,0:T(8,128)(2,1)S(1)} collective-permute-done((bf16[512,128]{1,0:T(8,128)(2,1)S(1)}, bf16[512,128]{1,0:T(8,128)(2,1)S(1)}, u32[]{:S(2)}, u32[]{:S(2)}) %collective-permute-start.8) | collective-permute-done | bytes 131104 | tf_op jit(solution)/shard_map/ppermute | solution.py:275
  50.9 3.9 %collective-permute-done.16.refs_4_ = bf16[512,128]{1,0:T(8,128)(2,1)S(1)} collective-permute-done((bf16[512,128]{1,0:T(8,128)(2,1)S(1)}, bf16[512,128]{1,0:T(8,128)(2,1)S(1)}, u32[]{:S(2)}, u32[]{:S(2)}) %collective-permute-start.16) | collective-permute-done | bytes 131104 | tf_op jit(solution)/shard_map/ppermute | solution.py:275
  55.7 4.0 %collective-permute-start.20 = (bf16[512,128]{1,0:T(8,128)(2,1)S(1)}, bf16[512,128]{1,0:T(8,128)(2,1)S(1)}, u32[]{:S(2)}, u32[]{:S(2)}) collective-permute-start(bf16[512,128]{1,0:T(8,128)(2,1)S(1)} %get-tuple-element.45.refs_0_.vector), channel_id=1, source_target_pairs={{0,2},{1,3},{2,0},{3,1},{4,6},{5,7},{6,4},{7,5},{8,10},{9,11},{10,... | collective-permute-start | bytes 393224 | tf_op jit(solution)/shard_map/ppermute | solution.py:275
  61.2 2.1 %collective-permute-start.23 = (bf16[512,128]{1,0:T(8,128)(2,1)S(1)}, bf16[512,128]{1,0:T(8,128)(2,1)S(1)}, u32[]{:S(2)}, u32[]{:S(2)}) collective-permute-start(bf16[512,128]{1,0:T(8,128)(2,1)S(1)} %collective-permute-done.17.refs_1_), channel_id=1, source_target_pairs={{0,2},{1,3},{2,0},{3,1},{4,6},{5,7},{6,4},{7,5},{8,10},{9,11},{10,... | collective-permute-start | bytes 393224 | tf_op jit(solution)/shard_map/ppermute | solution.py:275
  63.8 1.5 %collective-permute-start.21 = (bf16[512,128]{1,0:T(8,128)(2,1)S(1)}, bf16[512,128]{1,0:T(8,128)(2,1)S(1)}, u32[]{:S(2)}, u32[]{:S(2)}) collective-permute-start(bf16[512,128]{1,0:T(8,128)(2,1)S(1)} %collective-permute-done.17.refs_1_), channel_id=1, source_target_pairs={{0,3},{1,2},{2,1},{3,0},{4,7},{5,6},{6,5},{7,4},{8,11},{9,10},{10,... | collective-permute-start | bytes 393224 | tf_op jit(solution)/shard_map/ppermute | solution.py:275
  68.2 1.8 %collective-permute-done.21.refs_5_ = bf16[512,128]{1,0:T(8,128)(2,1)S(1)} collective-permute-done((bf16[512,128]{1,0:T(8,128)(2,1)S(1)}, bf16[512,128]{1,0:T(8,128)(2,1)S(1)}, u32[]{:S(2)}, u32[]{:S(2)}) %collective-permute-start.21) | collective-permute-done | bytes 131104 | tf_op jit(solution)/shard_map/ppermute | solution.py:275
  70.0 2.1 %shard_map.97 = (bf16[4224,128]{1,0:T(8,128)(2,1)S(1)}, bf16[512,128]{1,0:T(8,128)(2,1)S(1)}, bf16[512,128]{1,0:T(8,128)(2,1)S(1)}, bf16[512,128]{1,0:T(8,128)(2,1)S(1)}) custom-call(s32[1]{0:T(128)} %bitcast.place, s32[192]{0:T(256)S(1)} %select_n.17.links, bf16[6,1536,128]{2,1,0:T(8,128)(2,1)S(1)} %shard_map.86.left, ...), custom_call_target="tpu_custom_call" | custom-call | tf_op jit(solution)/shard_map/pallas_call | solution.py:223
  72.2 3.5 %collective-permute-start.27 = (bf16[512,128]{1,0:T(8,128)(2,1)S(1)}, bf16[512,128]{1,0:T(8,128)(2,1)S(1)}, u32[]{:S(2)}, u32[]{:S(2)}) collective-permute-start(bf16[512,128]{1,0:T(8,128)(2,1)S(1)} %get-tuple-element.52), channel_id=1, source_target_pairs={{0,3},{1,2},{2,1},{3,0},{4,7},{5,6},{6,5},{7,4},{8,11},{9,10},{10,... | collective-permute-start | bytes 393224 | tf_op jit(solution)/shard_map/ppermute | solution.py:275
  76.3 2.9 %shard_map.98 = (bf16[512,128]{1,0:T(8,128)(2,1)S(1)}, bf16[512,128]{1,0:T(8,128)(2,1)S(1)}, bf16[512,128]{1,0:T(8,128)(2,1)S(1)}, f32[512,128]{1,0:T(8,128)S(1)}, f32[512,128]{1,0:T(8,128)S(1)}) custom-call(s32[1]{0:T(128)} %bitcast.place, s32[192]{0:T(256)S(1)} %select_n.17.links, bf16[6,4096,128]{2,1,0:T(8,128)(2,1)S(1)} %bitcast.10, ...), custom_call_target="tpu_custom_call" | custom-call | tf_op jit(solution)/shard_map/pallas_call | solution.py:223
  79.2 2.9 %collective-permute-start.24 = (bf16[512,128]{1,0:T(8,128)(2,1)S(1)}, bf16[512,128]{1,0:T(8,128)(2,1)S(1)}, u32[]{:S(2)}, u32[]{:S(2)}) collective-permute-start(bf16[512,128]{1,0:T(8,128)(2,1)S(1)} %get-tuple-element.48), channel_id=1, source_target_pairs={{0,3},{1,2},{2,1},{3,0},{4,7},{5,6},{6,5},{7,4},{8,11},{9,10},{10,... | collective-permute-start | bytes 393224 | tf_op jit(solution)/shard_map/ppermute | solution.py:275
  82.8 2.2 %collective-permute-start.30 = (bf16[512,128]{1,0:T(8,128)(2,1)S(1)}, bf16[512,128]{1,0:T(8,128)(2,1)S(1)}, u32[]{:S(2)}, u32[]{:S(2)}) collective-permute-start(bf16[512,128]{1,0:T(8,128)(2,1)S(1)} %shard_map.99), channel_id=1, source_target_pairs={{0,4},{1,5},{2,6},{3,7},{4,0},{5,1},{6,2},{7,3},{8,12},{9,13},{10,... | collective-permute-start | bytes 393224 | tf_op jit(solution)/shard_map/ppermute | solution.py:275
  85.6 1.5 %collective-permute-done.25.refs_1_ = bf16[512,128]{1,0:T(8,128)(2,1)S(1)} collective-permute-done((bf16[512,128]{1,0:T(8,128)(2,1)S(1)}, bf16[512,128]{1,0:T(8,128)(2,1)S(1)}, u32[]{:S(2)}, u32[]{:S(2)}) %collective-permute-start.25) | collective-permute-done | bytes 131104 | tf_op jit(solution)/shard_map/ppermute | solution.py:275
  87.2 1.5 %collective-permute-done.30.refs_3_ = bf16[512,128]{1,0:T(8,128)(2,1)S(1)} collective-permute-done((bf16[512,128]{1,0:T(8,128)(2,1)S(1)}, bf16[512,128]{1,0:T(8,128)(2,1)S(1)}, u32[]{:S(2)}, u32[]{:S(2)}) %collective-permute-start.30) | collective-permute-done | bytes 131104 | tf_op jit(solution)/shard_map/ppermute | solution.py:275
  (61 shorter events, 17.7 us)
Async XLA Ops:
  0.6 3.4 %collective-permute-start = (f32[512]{0:T(512)}, f32[512]{0:T(512)S(1)}, u32[]{:S(2)}, u32[]{:S(2)}) collective-permute-start(f32[512]{0:T(512)} %param.8), channel_id=1, source_target_pairs={{0,8},{8,16},{16,24},{1,9},{9,17},{17,25},{2,10},{10,18},{18,26},{... | collective-permute-start | bytes 6152 | tf_op jit(solution)/shard_map/ppermute | solution.py:14
  4.3 9.2 %collective-permute-start.1 = (bf16[512,128]{1,0:T(8,128)(2,1)S(1)}, bf16[512,128]{1,0:T(8,128)(2,1)S(1)}, u32[]{:S(2)}, u32[]{:S(2)}) collective-permute-start(bf16[512,128]{1,0:T(8,128)(2,1)S(1)} %shard_map.89.refs_0_.refs_5_), channel_id=1, source_target_pairs={{0,4},{1,5},{2,6},{3,7},{4,0},{5,1},{6,2},{7,3},{8,12},{9,13},{10,... | collective-permute-start | bytes 393224 | tf_op jit(solution)/shard_map/ppermute | solution.py:275
  7.8 9.7 %collective-permute-start.4 = (bf16[512,128]{1,0:T(8,128)(2,1)S(1)}, bf16[512,128]{1,0:T(8,128)(2,1)S(1)}, u32[]{:S(2)}, u32[]{:S(2)}) collective-permute-start(bf16[512,128]{1,0:T(8,128)(2,1)S(1)} %shard_map.89.refs_0_.refs_5_), channel_id=1, source_target_pairs={{0,2},{1,3},{2,0},{3,1},{4,6},{5,7},{6,4},{7,5},{8,10},{9,11},{10,... | collective-permute-start | bytes 393224 | tf_op jit(solution)/shard_map/ppermute | solution.py:275
  9.4 12.7 %collective-permute-start.3 = (bf16[512,128]{1,0:T(8,128)(2,1)S(1)}, bf16[512,128]{1,0:T(8,128)(2,1)S(1)}, u32[]{:S(2)}, u32[]{:S(2)}) collective-permute-start(bf16[512,128]{1,0:T(8,128)(2,1)S(1)} %shard_map.89.refs_0_.refs_5_), channel_id=1, source_target_pairs={{0,1},{1,0},{2,3},{3,2},{4,5},{5,4},{6,7},{7,6},{8,9},{9,8},{10,11... | collective-permute-start | bytes 393224 | tf_op jit(solution)/shard_map/ppermute | solution.py:275
  10.9 11.2 %collective-permute-start.2 = (bf16[512,128]{1,0:T(8,128)(2,1)S(1)}, bf16[512,128]{1,0:T(8,128)(2,1)S(1)}, u32[]{:S(2)}, u32[]{:S(2)}) collective-permute-start(bf16[512,128]{1,0:T(8,128)(2,1)S(1)} %shard_map.89.refs_0_.refs_5_), channel_id=1, source_target_pairs={{0,3},{1,2},{2,1},{3,0},{4,7},{5,6},{6,5},{7,4},{8,11},{9,10},{10,... | collective-permute-start | bytes 393224 | tf_op jit(solution)/shard_map/ppermute | solution.py:275
  13.5 8.6 %collective-permute-start.7 = (bf16[512,128]{1,0:T(8,128)(2,1)S(1)}, bf16[512,128]{1,0:T(8,128)(2,1)S(1)}, u32[]{:S(2)}, u32[]{:S(2)}) collective-permute-start(bf16[512,128]{1,0:T(8,128)(2,1)S(1)} %collective-permute-done.1.refs_1_), channel_id=1, source_target_pairs={{0,2},{1,3},{2,0},{3,1},{4,6},{5,7},{6,4},{7,5},{8,10},{9,11},{10,... | collective-permute-start | bytes 393224 | tf_op jit(solution)/shard_map/ppermute | solution.py:275
  15.9 7.4 %collective-permute-start.6 = (bf16[512,128]{1,0:T(8,128)(2,1)S(1)}, bf16[512,128]{1,0:T(8,128)(2,1)S(1)}, u32[]{:S(2)}, u32[]{:S(2)}) collective-permute-start(bf16[512,128]{1,0:T(8,128)(2,1)S(1)} %collective-permute-done.1.refs_1_), channel_id=1, source_target_pairs={{0,1},{1,0},{2,3},{3,2},{4,5},{5,4},{6,7},{7,6},{8,9},{9,8},{10,11... | collective-permute-start | bytes 393224 | tf_op jit(solution)/shard_map/ppermute | solution.py:275
  17.4 7.3 %collective-permute-start.5 = (bf16[512,128]{1,0:T(8,128)(2,1)S(1)}, bf16[512,128]{1,0:T(8,128)(2,1)S(1)}, u32[]{:S(2)}, u32[]{:S(2)}) collective-permute-start(bf16[512,128]{1,0:T(8,128)(2,1)S(1)} %collective-permute-done.1.refs_1_), channel_id=1, source_target_pairs={{0,3},{1,2},{2,1},{3,0},{4,7},{5,6},{6,5},{7,4},{8,11},{9,10},{10,... | collective-permute-start | bytes 393224 | tf_op jit(solution)/shard_map/ppermute | solution.py:275
  18.4 12.1 %slice-start.2 = ((s8[6291456]{0:T(1024)(128)(4,1)}), s8[4194304]{0:T(1024)(128)(4,1)S(1)}, s32[]{:S(2)}) async-start(s8[6291456]{0:T(1024)(128)(4,1)} %bitcast.12), calls=%async_computation.2 | async-start | bytes 8388608
  26.9 17.6 %collective-permute-start.13 = (bf16[512,128]{1,0:T(8,128)(2,1)S(1)}, bf16[512,128]{1,0:T(8,128)(2,1)S(1)}, u32[]{:S(2)}, u32[]{:S(2)}) collective-permute-start(bf16[512,128]{1,0:T(8,128)(2,1)S(1)} %get-tuple-element.41), channel_id=1, source_target_pairs={{0,3},{1,2},{2,1},{3,0},{4,7},{5,6},{6,5},{7,4},{8,11},{9,10},{10,... | collective-permute-start | bytes 393224 | tf_op jit(solution)/shard_map/ppermute | solution.py:275
  28.7 16.6 %collective-permute-start.14 = (bf16[512,128]{1,0:T(8,128)(2,1)S(1)}, bf16[512,128]{1,0:T(8,128)(2,1)S(1)}, u32[]{:S(2)}, u32[]{:S(2)}) collective-permute-start(bf16[512,128]{1,0:T(8,128)(2,1)S(1)} %get-tuple-element.42), channel_id=1, source_target_pairs={{0,1},{1,0},{2,3},{3,2},{4,5},{5,4},{6,7},{7,6},{8,9},{9,8},{10,11... | collective-permute-start | bytes 393224 | tf_op jit(solution)/shard_map/ppermute | solution.py:275
  29.8 15.6 %collective-permute-start.15 = (bf16[512,128]{1,0:T(8,128)(2,1)S(1)}, bf16[512,128]{1,0:T(8,128)(2,1)S(1)}, u32[]{:S(2)}, u32[]{:S(2)}) collective-permute-start(bf16[512,128]{1,0:T(8,128)(2,1)S(1)} %get-tuple-element.43), channel_id=1, source_target_pairs={{0,2},{1,3},{2,0},{3,1},{4,6},{5,7},{6,4},{7,5},{8,10},{9,11},{10,... | collective-permute-start | bytes 393224 | tf_op jit(solution)/shard_map/ppermute | solution.py:275
  33.5 4.6 %collective-permute-start.10 = (f32[8,128]{1,0:T(8,128)S(1)}, f32[8,128]{1,0:T(8,128)S(1)}, u32[]{:S(2)}, u32[]{:S(2)}) collective-permute-start(f32[8,128]{1,0:T(8,128)S(1)} %get-tuple-element.39.mine), channel_id=1, source_target_pairs={{0,4},{1,5},{2,6},{3,7},{4,0},{5,1},{6,2},{7,3},{8,12},{9,13},{10,... | collective-permute-start | bytes 12296 | tf_op jit(solution)/shard_map/ppermute | solution.py:275
  38.1 3.6 %collective-permute-start.11 = (f32[8,128]{1,0:T(8,128)S(1)}, f32[8,128]{1,0:T(8,128)S(1)}, u32[]{:S(2)}, u32[]{:S(2)}) collective-permute-start(f32[8,128]{1,0:T(8,128)S(1)} %shard_map.92.mine), channel_id=1, source_target_pairs={{0,1},{1,0},{2,3},{3,2},{4,5},{5,4},{6,7},{7,6},{8,9},{9,8},{10,11... | collective-permute-start | bytes 12296 | tf_op jit(solution)/shard_map/ppermute | solution.py:275
  41.7 9.1 %collective-permute-start.12 = (bf16[528,128]{1,0:T(8,128)(2,1)S(1)}, bf16[528,128]{1,0:T(8,128)(2,1)S(1)}, u32[]{:S(2)}, u32[]{:S(2)}) collective-permute-start(bf16[528,128]{1,0:T(8,128)(2,1)S(1)} %shard_map.94), channel_id=1, source_target_pairs={{0,2},{1,3},{2,0},{3,1},{4,6},{5,7},{6,4},{7,5},{8,10},{9,11},{10,... | collective-permute-start | bytes 405512 | tf_op jit(solution)/shard_map/ppermute | solution.py:275
  43.1 6.6 %collective-permute-start.8 = (bf16[512,128]{1,0:T(8,128)(2,1)S(1)}, bf16[512,128]{1,0:T(8,128)(2,1)S(1)}, u32[]{:S(2)}, u32[]{:S(2)}) collective-permute-start(bf16[512,128]{1,0:T(8,128)(2,1)S(1)} %get-tuple-element.36), channel_id=1, source_target_pairs={{0,3},{1,2},{2,1},{3,0},{4,7},{5,6},{6,5},{7,4},{8,11},{9,10},{10,... | collective-permute-start | bytes 393224 | tf_op jit(solution)/shard_map/ppermute | solution.py:275
  44.5 6.3 %collective-permute-start.9 = (bf16[512,128]{1,0:T(8,128)(2,1)S(1)}, bf16[512,128]{1,0:T(8,128)(2,1)S(1)}, u32[]{:S(2)}, u32[]{:S(2)}) collective-permute-start(bf16[512,128]{1,0:T(8,128)(2,1)S(1)} %get-tuple-element.37), channel_id=1, source_target_pairs={{0,1},{1,0},{2,3},{3,2},{4,5},{5,4},{6,7},{7,6},{8,9},{9,8},{10,11... | collective-permute-start | bytes 393224 | tf_op jit(solution)/shard_map/ppermute | solution.py:275
  45.4 9.3 %collective-permute-start.16 = (bf16[512,128]{1,0:T(8,128)(2,1)S(1)}, bf16[512,128]{1,0:T(8,128)(2,1)S(1)}, u32[]{:S(2)}, u32[]{:S(2)}) collective-permute-start(bf16[512,128]{1,0:T(8,128)(2,1)S(1)} %shard_map.95), channel_id=1, source_target_pairs={{0,4},{1,5},{2,6},{3,7},{4,0},{5,1},{6,2},{7,3},{8,12},{9,13},{10,... | collective-permute-start | bytes 393224 | tf_op jit(solution)/shard_map/ppermute | solution.py:275
  55.0 6.2 %collective-permute-start.17 = (bf16[512,128]{1,0:T(8,128)(2,1)S(1)}, bf16[512,128]{1,0:T(8,128)(2,1)S(1)}, u32[]{:S(2)}, u32[]{:S(2)}) collective-permute-start(bf16[512,128]{1,0:T(8,128)(2,1)S(1)} %get-tuple-element.45.refs_0_.vector), channel_id=1, source_target_pairs={{0,4},{1,5},{2,6},{3,7},{4,0},{5,1},{6,2},{7,3},{8,12},{9,13},{10,... | collective-permute-start | bytes 393224 | tf_op jit(solution)/shard_map/ppermute | solution.py:275
  55.7 8.1 %collective-permute-start.20 = (bf16[512,128]{1,0:T(8,128)(2,1)S(1)}, bf16[512,128]{1,0:T(8,128)(2,1)S(1)}, u32[]{:S(2)}, u32[]{:S(2)}) collective-permute-start(bf16[512,128]{1,0:T(8,128)(2,1)S(1)} %get-tuple-element.45.refs_0_.vector), channel_id=1, source_target_pairs={{0,2},{1,3},{2,0},{3,1},{4,6},{5,7},{6,4},{7,5},{8,10},{9,11},{10,... | collective-permute-start | bytes 393224 | tf_op jit(solution)/shard_map/ppermute | solution.py:275
  59.7 6.7 %collective-permute-start.19 = (bf16[512,128]{1,0:T(8,128)(2,1)S(1)}, bf16[512,128]{1,0:T(8,128)(2,1)S(1)}, u32[]{:S(2)}, u32[]{:S(2)}) collective-permute-start(bf16[512,128]{1,0:T(8,128)(2,1)S(1)} %get-tuple-element.45.refs_0_.vector), channel_id=1, source_target_pairs={{0,1},{1,0},{2,3},{3,2},{4,5},{5,4},{6,7},{7,6},{8,9},{9,8},{10,11... | collective-permute-start | bytes 393224 | tf_op jit(solution)/shard_map/ppermute | solution.py:275
  60.2 6.2 %collective-permute-start.18 = (bf16[512,128]{1,0:T(8,128)(2,1)S(1)}, bf16[512,128]{1,0:T(8,128)(2,1)S(1)}, u32[]{:S(2)}, u32[]{:S(2)}) collective-permute-start(bf16[512,128]{1,0:T(8,128)(2,1)S(1)} %get-tuple-element.45.refs_0_.vector), channel_id=1, source_target_pairs={{0,3},{1,2},{2,1},{3,0},{4,7},{5,6},{6,5},{7,4},{8,11},{9,10},{10,... | collective-permute-start | bytes 393224 | tf_op jit(solution)/shard_map/ppermute | solution.py:275
  61.2 6.4 %collective-permute-start.23 = (bf16[512,128]{1,0:T(8,128)(2,1)S(1)}, bf16[512,128]{1,0:T(8,128)(2,1)S(1)}, u32[]{:S(2)}, u32[]{:S(2)}) collective-permute-start(bf16[512,128]{1,0:T(8,128)(2,1)S(1)} %collective-permute-done.17.refs_1_), channel_id=1, source_target_pairs={{0,2},{1,3},{2,0},{3,1},{4,6},{5,7},{6,4},{7,5},{8,10},{9,11},{10,... | collective-permute-start | bytes 393224 | tf_op jit(solution)/shard_map/ppermute | solution.py:275
  63.3 5.0 %collective-permute-start.22 = (bf16[512,128]{1,0:T(8,128)(2,1)S(1)}, bf16[512,128]{1,0:T(8,128)(2,1)S(1)}, u32[]{:S(2)}, u32[]{:S(2)}) collective-permute-start(bf16[512,128]{1,0:T(8,128)(2,1)S(1)} %collective-permute-done.17.refs_1_), channel_id=1, source_target_pairs={{0,1},{1,0},{2,3},{3,2},{4,5},{5,4},{6,7},{7,6},{8,9},{9,8},{10,11... | collective-permute-start | bytes 393224 | tf_op jit(solution)/shard_map/ppermute | solution.py:275
  63.8 6.2 %collective-permute-start.21 = (bf16[512,128]{1,0:T(8,128)(2,1)S(1)}, bf16[512,128]{1,0:T(8,128)(2,1)S(1)}, u32[]{:S(2)}, u32[]{:S(2)}) collective-permute-start(bf16[512,128]{1,0:T(8,128)(2,1)S(1)} %collective-permute-done.17.refs_1_), channel_id=1, source_target_pairs={{0,3},{1,2},{2,1},{3,0},{4,7},{5,6},{6,5},{7,4},{8,11},{9,10},{10,... | collective-permute-start | bytes 393224 | tf_op jit(solution)/shard_map/ppermute | solution.py:275
  72.2 10.1 %collective-permute-start.27 = (bf16[512,128]{1,0:T(8,128)(2,1)S(1)}, bf16[512,128]{1,0:T(8,128)(2,1)S(1)}, u32[]{:S(2)}, u32[]{:S(2)}) collective-permute-start(bf16[512,128]{1,0:T(8,128)(2,1)S(1)} %get-tuple-element.52), channel_id=1, source_target_pairs={{0,3},{1,2},{2,1},{3,0},{4,7},{5,6},{6,5},{7,4},{8,11},{9,10},{10,... | collective-permute-start | bytes 393224 | tf_op jit(solution)/shard_map/ppermute | solution.py:275
  75.7 7.1 %collective-permute-start.28 = (bf16[512,128]{1,0:T(8,128)(2,1)S(1)}, bf16[512,128]{1,0:T(8,128)(2,1)S(1)}, u32[]{:S(2)}, u32[]{:S(2)}) collective-permute-start(bf16[512,128]{1,0:T(8,128)(2,1)S(1)} %get-tuple-element.53), channel_id=1, source_target_pairs={{0,1},{1,0},{2,3},{3,2},{4,5},{5,4},{6,7},{7,6},{8,9},{9,8},{10,11... | collective-permute-start | bytes 393224 | tf_op jit(solution)/shard_map/ppermute | solution.py:275
  75.8 7.0 %collective-permute-start.29 = (bf16[512,128]{1,0:T(8,128)(2,1)S(1)}, bf16[512,128]{1,0:T(8,128)(2,1)S(1)}, u32[]{:S(2)}, u32[]{:S(2)}) collective-permute-start(bf16[512,128]{1,0:T(8,128)(2,1)S(1)} %get-tuple-element.54), channel_id=1, source_target_pairs={{0,2},{1,3},{2,0},{3,1},{4,6},{5,7},{6,4},{7,5},{8,10},{9,11},{10,... | collective-permute-start | bytes 393224 | tf_op jit(solution)/shard_map/ppermute | solution.py:275
  79.2 6.4 %collective-permute-start.24 = (bf16[512,128]{1,0:T(8,128)(2,1)S(1)}, bf16[512,128]{1,0:T(8,128)(2,1)S(1)}, u32[]{:S(2)}, u32[]{:S(2)}) collective-permute-start(bf16[512,128]{1,0:T(8,128)(2,1)S(1)} %get-tuple-element.48), channel_id=1, source_target_pairs={{0,3},{1,2},{2,1},{3,0},{4,7},{5,6},{6,5},{7,4},{8,11},{9,10},{10,... | collective-permute-start | bytes 393224 | tf_op jit(solution)/shard_map/ppermute | solution.py:275
  82.1 5.0 %collective-permute-start.25 = (bf16[512,128]{1,0:T(8,128)(2,1)S(1)}, bf16[512,128]{1,0:T(8,128)(2,1)S(1)}, u32[]{:S(2)}, u32[]{:S(2)}) collective-permute-start(bf16[512,128]{1,0:T(8,128)(2,1)S(1)} %get-tuple-element.49), channel_id=1, source_target_pairs={{0,1},{1,0},{2,3},{3,2},{4,5},{5,4},{6,7},{7,6},{8,9},{9,8},{10,11... | collective-permute-start | bytes 393224 | tf_op jit(solution)/shard_map/ppermute | solution.py:275
  82.3 5.0 %collective-permute-start.26 = (bf16[512,128]{1,0:T(8,128)(2,1)S(1)}, bf16[512,128]{1,0:T(8,128)(2,1)S(1)}, u32[]{:S(2)}, u32[]{:S(2)}) collective-permute-start(bf16[512,128]{1,0:T(8,128)(2,1)S(1)} %get-tuple-element.50), channel_id=1, source_target_pairs={{0,2},{1,3},{2,0},{3,1},{4,6},{5,7},{6,4},{7,5},{8,10},{9,11},{10,... | collective-permute-start | bytes 393224 | tf_op jit(solution)/shard_map/ppermute | solution.py:275
  82.8 5.9 %collective-permute-start.30 = (bf16[512,128]{1,0:T(8,128)(2,1)S(1)}, bf16[512,128]{1,0:T(8,128)(2,1)S(1)}, u32[]{:S(2)}, u32[]{:S(2)}) collective-permute-start(bf16[512,128]{1,0:T(8,128)(2,1)S(1)} %shard_map.99), channel_id=1, source_target_pairs={{0,4},{1,5},{2,6},{3,7},{4,0},{5,1},{6,2},{7,3},{8,12},{9,13},{10,... | collective-permute-start | bytes 393224 | tf_op jit(solution)/shard_map/ppermute | solution.py:275
  (4 other events, 39.3 us)

commit v5 on v4

--- a/solution.py
+++ b/solution.py
@@ -105,13 +105,20 @@
     scaled_products(vector, links, left, right, chunks, rows // width, packed, store)
 
 
+def lay_kernel(offsets, place, *refs):
+    vector = refs[-1]
+    rows, width = refs[0].shape
+    for piece, offset in zip(refs[:-1], offsets):
+        vector[rows_at(place[0] ^ offset, rows), :] = piece[...]
+    vector[vector.shape[0] - width :, :] = jnp.zeros((width, width), vector.dtype)
+
+
 def first_kernel(offsets, first, dots, place, links, left, right, *refs):
     npiece = len(offsets)
-    pieces, vector, outs = refs[:npiece], refs[npiece], refs[npiece + 1 :]
-    rows, width = pieces[0].shape
+    pieces, vector, outs = refs[:npiece], refs[npiece + 1], refs[npiece + 2 :]
+    rows = outs[0].shape[0]
     for piece, offset in zip(pieces, offsets):
         vector[rows_at(place[0] ^ offset, rows), :] = piece[...]
-    vector[npiece * rows :, :] = jnp.zeros((width, width), vector.dtype)
     numer = outs[-1] if dots else None
     if dots:
         numer[...] = jnp.zeros_like(numer)
@@ -219,12 +226,13 @@
 SMEM = pl.BlockSpec(memory_space=pltpu.SMEM)
 
 
-def on_chip(kernel, out_shape, nscalar, *args, limit=8 << 20):
+def on_chip(kernel, out_shape, nscalar, *args, limit=8 << 20, aliases={}):
     outs = pl.pallas_call(
         kernel,
         out_shape=out_shape,
         in_specs=[SMEM] * nscalar + [VMEM] * (len(args) - nscalar),
         out_specs=[VMEM] * len(out_shape),
+        input_output_aliases=aliases,
         compiler_params=pltpu.CompilerParams(vmem_limit_bytes=limit),
     )(*args)
     return list(outs)
@@ -285,10 +293,13 @@
     def apply_terms(pieces, lead_left, left, lead_right, right, dots):
         across = [half ^ r for r in inside]
         whole = shape((devices * rows + width, width), jnp.bfloat16)
+        early, late = list(pieces)[: len(pieces) - len(inside)], list(pieces)[len(pieces) - len(inside) :]
+        laid = on_chip(partial(lay_kernel, early), [whole], 1, place, *(pieces[p] for p in early))[0]
         vector, *lead = on_chip(
-            partial(first_kernel, list(pieces), across, dots),
+            partial(first_kernel, late, across, dots),
             [whole] + [sent] * len(across) + [tile] * dots,
-            2, place, links, lead_left, lead_right, *pieces.values(),
+            2, place, links, lead_left, lead_right, *(pieces[p] for p in late), laid,
+            aliases={4 + len(late): 0},
         )
         outs = on_chip(
             partial(last_kernel, inside + [half, 0], dots),

time: 89.9 us -> 89.6 us (level)
    pallas_call x12 -> x14, Pallas kernels: 11.6 us -> 11.5 us  [on_chip(): pl.pallas_call(kernel, out_shape=out_shape, in_specs=[SMEM] * nscalar + [...]
  transfers between devices with their start and end apart: 31 -> 31, of which waited for: 16 -> 15; matrix products, arithmetic and copies ran while one was open for 1% -> 1% of each run, Pallas kernels for 12% -> 12%
where the time goes in v5:
time: 89.6 us; the launch traced here: 89.4 us
  starting transfers between devices  47.5 us (53%)
  waiting for transfers between devices  23.7 us (26%)
  Pallas kernels  16 us (18%)
    ppermute x30, starting transfers between devices, exchange(): return lax.ppermute(array, 'ops', [(o, o ^ by) for o in range(devices)])  45.1 us
    ppermute x30, waiting for transfers between devices, exchange(): return lax.ppermute(array, 'ops', [(o, o ^ by) for o in range(devices)])  23.6 us
    pallas_call x14, Pallas kernels, on_chip(): pl.pallas_call(kernel, out_shape=out_shape, in_specs=[SMEM] * nscalar + [...  11.5 us
    pallas_call x2, Pallas kernels, loaded_chunks(): pl.pallas_call(partial(load_chunks_kernel, offsets), out_shape=pltpu.VMEM...  3.61 us
    ppermute x1, starting transfers between devices, shifted(): return lax.ppermute(array, axis, pairs)  2.4 us
  transfers between devices with their start and end apart: 31, of which 15 were waited for; matrix products, arithmetic and copies ran while one was open for 1% of the time, Pallas kernels for 12%

profile of v5, /device:TPU:0, one launch (start us, length us, event | category | flops | bytes accessed | tf_op | source)
XLA Modules:
  0.0 89.4 jit_solution(16881837617950689812)
XLA Ops:
  0.6 2.4 %collective-permute-start = (f32[512]{0:T(512)}, f32[512]{0:T(512)S(1)}, u32[]{:S(2)}, u32[]{:S(2)}) collective-permute-start(f32[512]{0:T(512)} %param.8), channel_id=1, source_target_pairs={{0,8},{8,16},{16,24},{1,9},{9,17},{17,25},{2,10},{10,18},{18,26},{... | collective-permute-start | bytes 6152 | tf_op jit(solution)/shard_map/ppermute | solution.py:14
  4.3 3.5 %collective-permute-start.1 = (bf16[512,128]{1,0:T(8,128)(2,1)S(1)}, bf16[512,128]{1,0:T(8,128)(2,1)S(1)}, u32[]{:S(2)}, u32[]{:S(2)}) collective-permute-start(bf16[512,128]{1,0:T(8,128)(2,1)S(1)} %shard_map.89.refs_0_.refs_5_), channel_id=1, source_target_pairs={{0,4},{1,5},{2,6},{3,7},{4,0},{5,1},{6,2},{7,3},{8,12},{9,13},{10,... | collective-permute-start | bytes 393224 | tf_op jit(solution)/shard_map/ppermute | solution.py:283
  7.8 1.6 %collective-permute-start.7 = (bf16[512,128]{1,0:T(8,128)(2,1)S(1)}, bf16[512,128]{1,0:T(8,128)(2,1)S(1)}, u32[]{:S(2)}, u32[]{:S(2)}) collective-permute-start(bf16[512,128]{1,0:T(8,128)(2,1)S(1)} %shard_map.89.refs_0_.refs_5_), channel_id=1, source_target_pairs={{0,2},{1,3},{2,0},{3,1},{4,6},{5,7},{6,4},{7,5},{8,10},{9,11},{10,... | collective-permute-start | bytes 393224 | tf_op jit(solution)/shard_map/ppermute | solution.py:283
  9.4 1.5 %collective-permute-start.6 = (bf16[512,128]{1,0:T(8,128)(2,1)S(1)}, bf16[512,128]{1,0:T(8,128)(2,1)S(1)}, u32[]{:S(2)}, u32[]{:S(2)}) collective-permute-start(bf16[512,128]{1,0:T(8,128)(2,1)S(1)} %shard_map.89.refs_0_.refs_5_), channel_id=1, source_target_pairs={{0,1},{1,0},{2,3},{3,2},{4,5},{5,4},{6,7},{7,6},{8,9},{9,8},{10,11... | collective-permute-start | bytes 393224 | tf_op jit(solution)/shard_map/ppermute | solution.py:283
  11.3 2.2 %collective-permute-done.1.refs_1_ = bf16[512,128]{1,0:T(8,128)(2,1)S(1)} collective-permute-done((bf16[512,128]{1,0:T(8,128)(2,1)S(1)}, bf16[512,128]{1,0:T(8,128)(2,1)S(1)}, u32[]{:S(2)}, u32[]{:S(2)}) %collective-permute-start.1) | collective-permute-done | bytes 131104 | tf_op jit(solution)/shard_map/ppermute | solution.py:283
  13.5 2.4 %collective-permute-start.4 = (bf16[512,128]{1,0:T(8,128)(2,1)S(1)}, bf16[512,128]{1,0:T(8,128)(2,1)S(1)}, u32[]{:S(2)}, u32[]{:S(2)}) collective-permute-start(bf16[512,128]{1,0:T(8,128)(2,1)S(1)} %collective-permute-done.1.refs_1_), channel_id=1, source_target_pairs={{0,2},{1,3},{2,0},{3,1},{4,6},{5,7},{6,4},{7,5},{8,10},{9,11},{10,... | collective-permute-start | bytes 393224 | tf_op jit(solution)/shard_map/ppermute | solution.py:283
  15.9 1.5 %collective-permute-start.3 = (bf16[512,128]{1,0:T(8,128)(2,1)S(1)}, bf16[512,128]{1,0:T(8,128)(2,1)S(1)}, u32[]{:S(2)}, u32[]{:S(2)}) collective-permute-start(bf16[512,128]{1,0:T(8,128)(2,1)S(1)} %collective-permute-done.1.refs_1_), channel_id=1, source_target_pairs={{0,1},{1,0},{2,3},{3,2},{4,5},{5,4},{6,7},{7,6},{8,9},{9,8},{10,11... | collective-permute-start | bytes 393224 | tf_op jit(solution)/shard_map/ppermute | solution.py:283
  18.4 1.8 %shard_map.87.right = bf16[6,1536,128]{2,1,0:T(8,128)(2,1)S(1)} custom-call(s32[1]{0:T(128)} %bitcast.place, bf16[6,4096,128]{2,1,0:T(8,128)(2,1)} %bitcast.11), custom_call_target="tpu_custom_call" | custom-call | tf_op jit(solution)/shard_map/pallas_call | solution.py:255
  20.2 1.8 %shard_map.86.left = bf16[6,1536,128]{2,1,0:T(8,128)(2,1)S(1)} custom-call(s32[1]{0:T(128)} %bitcast.place, bf16[6,4096,128]{2,1,0:T(8,128)(2,1)} %bitcast.6), custom_call_target="tpu_custom_call" | custom-call | tf_op jit(solution)/shard_map/pallas_call | solution.py:255
  23.3 1.4 %collective-permute-done.2.refs_0_ = bf16[512,128]{1,0:T(8,128)(2,1)S(1)} collective-permute-done((bf16[512,128]{1,0:T(8,128)(2,1)S(1)}, bf16[512,128]{1,0:T(8,128)(2,1)S(1)}, u32[]{:S(2)}, u32[]{:S(2)}) %collective-permute-start.2) | collective-permute-done | bytes 131104 | tf_op jit(solution)/shard_map/ppermute | solution.py:283
  24.8 2.1 %shard_map.91 = (bf16[4224,128]{1,0:T(8,128)(2,1)S(1)}, bf16[512,128]{1,0:T(8,128)(2,1)S(1)}, bf16[512,128]{1,0:T(8,128)(2,1)S(1)}, bf16[512,128]{1,0:T(8,128)(2,1)S(1)}, f32[8,128]{1,0:T(8,128)S(1)}) custom-call(s32[1]{0:T(128)} %bitcast.place, s32[192]{0:T(256)S(1)} %select_n.17.links, ...), custom_call_target="tpu_custom_call", output_to_operand_aliasing={{0}: (7, {})} | custom-call | tf_op jit(solution)/shard_map/pallas_call | solution.py:230
  26.8 1.8 %collective-permute-start.13 = (bf16[512,128]{1,0:T(8,128)(2,1)S(1)}, bf16[512,128]{1,0:T(8,128)(2,1)S(1)}, u32[]{:S(2)}, u32[]{:S(2)}) collective-permute-start(bf16[512,128]{1,0:T(8,128)(2,1)S(1)} %get-tuple-element.41), channel_id=1, source_target_pairs={{0,3},{1,2},{2,1},{3,0},{4,7},{5,6},{6,5},{7,4},{8,11},{9,10},{10,... | collective-permute-start | bytes 393224 | tf_op jit(solution)/shard_map/ppermute | solution.py:283
  30.4 2.9 %shard_map.92 = (bf16[512,128]{1,0:T(8,128)(2,1)S(1)}, bf16[512,128]{1,0:T(8,128)(2,1)S(1)}, bf16[512,128]{1,0:T(8,128)(2,1)S(1)}, f32[512,128]{1,0:T(8,128)S(1)...) custom-call(s32[1]{0:T(128)} %bitcast.place, s32[192]{0:T(256)S(1)} %select_n.17.links, ...), custom_call_target="tpu_custom_call" | custom-call | tf_op jit(solution)/shard_map/pallas_call | solution.py:230
  33.3 2.7 %collective-permute-start.10 = (f32[8,128]{1,0:T(8,128)S(1)}, f32[8,128]{1,0:T(8,128)S(1)}, u32[]{:S(2)}, u32[]{:S(2)}) collective-permute-start(f32[8,128]{1,0:T(8,128)S(1)} %get-tuple-element.39.mine), channel_id=1, source_target_pairs={{0,4},{1,5},{2,6},{3,7},{4,0},{5,1},{6,2},{7,3},{8,12},{9,13},{10,... | collective-permute-start | bytes 12296 | tf_op jit(solution)/shard_map/ppermute | solution.py:283
  36.1 1.8 %collective-permute-done.10.other = f32[8,128]{1,0:T(8,128)S(1)} collective-permute-done((f32[8,128]{1,0:T(8,128)S(1)}, f32[8,128]{1,0:T(8,128)S(1)}, u32[]{:S(2)}, u32[]{:S(2)}) %collective-permute-start.10) | collective-permute-done | bytes 4128 | tf_op jit(solution)/shard_map/ppermute | solution.py:283
  39.2 2.4 %collective-permute-done.11.other = f32[8,128]{1,0:T(8,128)S(1)} collective-permute-done((f32[8,128]{1,0:T(8,128)S(1)}, f32[8,128]{1,0:T(8,128)S(1)}, u32[]{:S(2)}, u32[]{:S(2)}) %collective-permute-start.11) | collective-permute-done | bytes 4128 | tf_op jit(solution)/shard_map/ppermute | solution.py:283
  41.6 1.4 %collective-permute-start.12 = (bf16[528,128]{1,0:T(8,128)(2,1)S(1)}, bf16[528,128]{1,0:T(8,128)(2,1)S(1)}, u32[]{:S(2)}, u32[]{:S(2)}) collective-permute-start(bf16[528,128]{1,0:T(8,128)(2,1)S(1)} %shard_map.95), channel_id=1, source_target_pairs={{0,2},{1,3},{2,0},{3,1},{4,6},{5,7},{6,4},{7,5},{8,10},{9,11},{10,... | collective-permute-start | bytes 405512 | tf_op jit(solution)/shard_map/ppermute | solution.py:283
  42.9 1.4 %collective-permute-start.8 = (bf16[512,128]{1,0:T(8,128)(2,1)S(1)}, bf16[512,128]{1,0:T(8,128)(2,1)S(1)}, u32[]{:S(2)}, u32[]{:S(2)}) collective-permute-start(bf16[512,128]{1,0:T(8,128)(2,1)S(1)} %get-tuple-element.36), channel_id=1, source_target_pairs={{0,3},{1,2},{2,1},{3,0},{4,7},{5,6},{6,5},{7,4},{8,11},{9,10},{10,... | collective-permute-start | bytes 393224 | tf_op jit(solution)/shard_map/ppermute | solution.py:283
  45.2 2.7 %collective-permute-start.16 = (bf16[512,128]{1,0:T(8,128)(2,1)S(1)}, bf16[512,128]{1,0:T(8,128)(2,1)S(1)}, u32[]{:S(2)}, u32[]{:S(2)}) collective-permute-start(bf16[512,128]{1,0:T(8,128)(2,1)S(1)} %shard_map.96), channel_id=1, source_target_pairs={{0,4},{1,5},{2,6},{3,7},{4,0},{5,1},{6,2},{7,3},{8,12},{9,13},{10,... | collective-permute-start | bytes 393224 | tf_op jit(solution)/shard_map/ppermute | solution.py:283
  47.9 1.6 %collective-permute-done.8.refs_1_ = bf16[512,128]{1,0:T(8,128)(2,1)S(1)} collective-permute-done((bf16[512,128]{1,0:T(8,128)(2,1)S(1)}, bf16[512,128]{1,0:T(8,128)(2,1)S(1)}, u32[]{:S(2)}, u32[]{:S(2)}) %collective-permute-start.8) | collective-permute-done | bytes 131104 | tf_op jit(solution)/shard_map/ppermute | solution.py:283
  50.7 3.9 %collective-permute-done.16.refs_4_ = bf16[512,128]{1,0:T(8,128)(2,1)S(1)} collective-permute-done((bf16[512,128]{1,0:T(8,128)(2,1)S(1)}, bf16[512,128]{1,0:T(8,128)(2,1)S(1)}, u32[]{:S(2)}, u32[]{:S(2)}) %collective-permute-start.16) | collective-permute-done | bytes 131104 | tf_op jit(solution)/shard_map/ppermute | solution.py:283
  55.5 4.0 %collective-permute-start.23 = (bf16[512,128]{1,0:T(8,128)(2,1)S(1)}, bf16[512,128]{1,0:T(8,128)(2,1)S(1)}, u32[]{:S(2)}, u32[]{:S(2)}) collective-permute-start(bf16[512,128]{1,0:T(8,128)(2,1)S(1)} %get-tuple-element.45.refs_0_.vector), channel_id=1, source_target_pairs={{0,2},{1,3},{2,0},{3,1},{4,6},{5,7},{6,4},{7,5},{8,10},{9,11},{10,... | collective-permute-start | bytes 393224 | tf_op jit(solution)/shard_map/ppermute | solution.py:283
  61.0 2.1 %collective-permute-start.20 = (bf16[512,128]{1,0:T(8,128)(2,1)S(1)}, bf16[512,128]{1,0:T(8,128)(2,1)S(1)}, u32[]{:S(2)}, u32[]{:S(2)}) collective-permute-start(bf16[512,128]{1,0:T(8,128)(2,1)S(1)} %collective-permute-done.17.refs_1_), channel_id=1, source_target_pairs={{0,2},{1,3},{2,0},{3,1},{4,6},{5,7},{6,4},{7,5},{8,10},{9,11},{10,... | collective-permute-start | bytes 393224 | tf_op jit(solution)/shard_map/ppermute | solution.py:283
  63.6 1.5 %collective-permute-start.18 = (bf16[512,128]{1,0:T(8,128)(2,1)S(1)}, bf16[512,128]{1,0:T(8,128)(2,1)S(1)}, u32[]{:S(2)}, u32[]{:S(2)}) collective-permute-start(bf16[512,128]{1,0:T(8,128)(2,1)S(1)} %collective-permute-done.17.refs_1_), channel_id=1, source_target_pairs={{0,3},{1,2},{2,1},{3,0},{4,7},{5,6},{6,5},{7,4},{8,11},{9,10},{10,... | collective-permute-start | bytes 393224 | tf_op jit(solution)/shard_map/ppermute | solution.py:283
  68.0 1.9 %collective-permute-done.18.refs_0_ = bf16[512,128]{1,0:T(8,128)(2,1)S(1)} collective-permute-done((bf16[512,128]{1,0:T(8,128)(2,1)S(1)}, bf16[512,128]{1,0:T(8,128)(2,1)S(1)}, u32[]{:S(2)}, u32[]{:S(2)}) %collective-permute-start.18) | collective-permute-done | bytes 131104 | tf_op jit(solution)/shard_map/ppermute | solution.py:283
  69.9 2.1 %shard_map.99 = (bf16[4224,128]{1,0:T(8,128)(2,1)S(1)}, bf16[512,128]{1,0:T(8,128)(2,1)S(1)}, bf16[512,128]{1,0:T(8,128)(2,1)S(1)}, bf16[512,128]{1,0:T(8,128)(2,1)S(1)}) custom-call(s32[1]{0:T(128)} %bitcast.place, s32[192]{0:T(256)S(1)} %select_n.17.links, bf16[6,1536,128]{2,1,0:T(8,128)(2,1)S(1)} %shard_map.86.left, ...), custom_call_target="tpu_custom_call", output_to_operand_aliasing={{0}: (7, {})} | custom-call | tf_op jit(solution)/shard_map/pallas_call | solution.py:230
  72.0 3.5 %collective-permute-start.27 = (bf16[512,128]{1,0:T(8,128)(2,1)S(1)}, bf16[512,128]{1,0:T(8,128)(2,1)S(1)}, u32[]{:S(2)}, u32[]{:S(2)}) collective-permute-start(bf16[512,128]{1,0:T(8,128)(2,1)S(1)} %get-tuple-element.52), channel_id=1, source_target_pairs={{0,3},{1,2},{2,1},{3,0},{4,7},{5,6},{6,5},{7,4},{8,11},{9,10},{10,... | collective-permute-start | bytes 393224 | tf_op jit(solution)/shard_map/ppermute | solution.py:283
  76.1 2.9 %shard_map.100 = (bf16[512,128]{1,0:T(8,128)(2,1)S(1)}, bf16[512,128]{1,0:T(8,128)(2,1)S(1)}, bf16[512,128]{1,0:T(8,128)(2,1)S(1)}, f32[512,128]{1,0:T(8,128)S(1)}, f32[512,128]{1,0:T(8,128)S(1)}) custom-call(s32[1]{0:T(128)} %bitcast.place, s32[192]{0:T(256)S(1)} %select_n.17.links, bf16[6,4096,128]{2,1,0:T(8,128)(2,1)S(1)} %bitcast.10, ...), custom_call_target="tpu_custom_call" | custom-call | tf_op jit(solution)/shard_map/pallas_call | solution.py:230
  79.0 2.9 %collective-permute-start.24 = (bf16[512,128]{1,0:T(8,128)(2,1)S(1)}, bf16[512,128]{1,0:T(8,128)(2,1)S(1)}, u32[]{:S(2)}, u32[]{:S(2)}) collective-permute-start(bf16[512,128]{1,0:T(8,128)(2,1)S(1)} %get-tuple-element.48), channel_id=1, source_target_pairs={{0,3},{1,2},{2,1},{3,0},{4,7},{5,6},{6,5},{7,4},{8,11},{9,10},{10,... | collective-permute-start | bytes 393224 | tf_op jit(solution)/shard_map/ppermute | solution.py:283
  82.7 2.2 %collective-permute-start.30 = (bf16[512,128]{1,0:T(8,128)(2,1)S(1)}, bf16[512,128]{1,0:T(8,128)(2,1)S(1)}, u32[]{:S(2)}, u32[]{:S(2)}) collective-permute-start(bf16[512,128]{1,0:T(8,128)(2,1)S(1)} %shard_map.101), channel_id=1, source_target_pairs={{0,4},{1,5},{2,6},{3,7},{4,0},{5,1},{6,2},{7,3},{8,12},{9,13},{10,... | collective-permute-start | bytes 393224 | tf_op jit(solution)/shard_map/ppermute | solution.py:283
  85.4 1.5 %collective-permute-done.25.refs_1_ = bf16[512,128]{1,0:T(8,128)(2,1)S(1)} collective-permute-done((bf16[512,128]{1,0:T(8,128)(2,1)S(1)}, bf16[512,128]{1,0:T(8,128)(2,1)S(1)}, u32[]{:S(2)}, u32[]{:S(2)}) %collective-permute-start.25) | collective-permute-done | bytes 131104 | tf_op jit(solution)/shard_map/ppermute | solution.py:283
  87.0 1.6 %collective-permute-done.30.refs_3_ = bf16[512,128]{1,0:T(8,128)(2,1)S(1)} collective-permute-done((bf16[512,128]{1,0:T(8,128)(2,1)S(1)}, bf16[512,128]{1,0:T(8,128)(2,1)S(1)}, u32[]{:S(2)}, u32[]{:S(2)}) %collective-permute-start.30) | collective-permute-done | bytes 131104 | tf_op jit(solution)/shard_map/ppermute | solution.py:283
  (63 shorter events, 17.6 us)
Async XLA Ops:
  0.6 3.4 %collective-permute-start = (f32[512]{0:T(512)}, f32[512]{0:T(512)S(1)}, u32[]{:S(2)}, u32[]{:S(2)}) collective-permute-start(f32[512]{0:T(512)} %param.8), channel_id=1, source_target_pairs={{0,8},{8,16},{16,24},{1,9},{9,17},{17,25},{2,10},{10,18},{18,26},{... | collective-permute-start | bytes 6152 | tf_op jit(solution)/shard_map/ppermute | solution.py:14
  4.3 9.2 %collective-permute-start.1 = (bf16[512,128]{1,0:T(8,128)(2,1)S(1)}, bf16[512,128]{1,0:T(8,128)(2,1)S(1)}, u32[]{:S(2)}, u32[]{:S(2)}) collective-permute-start(bf16[512,128]{1,0:T(8,128)(2,1)S(1)} %shard_map.89.refs_0_.refs_5_), channel_id=1, source_target_pairs={{0,4},{1,5},{2,6},{3,7},{4,0},{5,1},{6,2},{7,3},{8,12},{9,13},{10,... | collective-permute-start | bytes 393224 | tf_op jit(solution)/shard_map/ppermute | solution.py:283
  7.8 9.7 %collective-permute-start.7 = (bf16[512,128]{1,0:T(8,128)(2,1)S(1)}, bf16[512,128]{1,0:T(8,128)(2,1)S(1)}, u32[]{:S(2)}, u32[]{:S(2)}) collective-permute-start(bf16[512,128]{1,0:T(8,128)(2,1)S(1)} %shard_map.89.refs_0_.refs_5_), channel_id=1, source_target_pairs={{0,2},{1,3},{2,0},{3,1},{4,6},{5,7},{6,4},{7,5},{8,10},{9,11},{10,... | collective-permute-start | bytes 393224 | tf_op jit(solution)/shard_map/ppermute | solution.py:283
  9.4 12.7 %collective-permute-start.6 = (bf16[512,128]{1,0:T(8,128)(2,1)S(1)}, bf16[512,128]{1,0:T(8,128)(2,1)S(1)}, u32[]{:S(2)}, u32[]{:S(2)}) collective-permute-start(bf16[512,128]{1,0:T(8,128)(2,1)S(1)} %shard_map.89.refs_0_.refs_5_), channel_id=1, source_target_pairs={{0,1},{1,0},{2,3},{3,2},{4,5},{5,4},{6,7},{7,6},{8,9},{9,8},{10,11... | collective-permute-start | bytes 393224 | tf_op jit(solution)/shard_map/ppermute | solution.py:283
  10.9 11.2 %collective-permute-start.5 = (bf16[512,128]{1,0:T(8,128)(2,1)S(1)}, bf16[512,128]{1,0:T(8,128)(2,1)S(1)}, u32[]{:S(2)}, u32[]{:S(2)}) collective-permute-start(bf16[512,128]{1,0:T(8,128)(2,1)S(1)} %shard_map.89.refs_0_.refs_5_), channel_id=1, source_target_pairs={{0,3},{1,2},{2,1},{3,0},{4,7},{5,6},{6,5},{7,4},{8,11},{9,10},{10,... | collective-permute-start | bytes 393224 | tf_op jit(solution)/shard_map/ppermute | solution.py:283
  13.5 8.7 %collective-permute-start.4 = (bf16[512,128]{1,0:T(8,128)(2,1)S(1)}, bf16[512,128]{1,0:T(8,128)(2,1)S(1)}, u32[]{:S(2)}, u32[]{:S(2)}) collective-permute-start(bf16[512,128]{1,0:T(8,128)(2,1)S(1)} %collective-permute-done.1.refs_1_), channel_id=1, source_target_pairs={{0,2},{1,3},{2,0},{3,1},{4,6},{5,7},{6,4},{7,5},{8,10},{9,11},{10,... | collective-permute-start | bytes 393224 | tf_op jit(solution)/shard_map/ppermute | solution.py:283
  15.9 7.4 %collective-permute-start.3 = (bf16[512,128]{1,0:T(8,128)(2,1)S(1)}, bf16[512,128]{1,0:T(8,128)(2,1)S(1)}, u32[]{:S(2)}, u32[]{:S(2)}) collective-permute-start(bf16[512,128]{1,0:T(8,128)(2,1)S(1)} %collective-permute-done.1.refs_1_), channel_id=1, source_target_pairs={{0,1},{1,0},{2,3},{3,2},{4,5},{5,4},{6,7},{7,6},{8,9},{9,8},{10,11... | collective-permute-start | bytes 393224 | tf_op jit(solution)/shard_map/ppermute | solution.py:283
  17.4 7.3 %collective-permute-start.2 = (bf16[512,128]{1,0:T(8,128)(2,1)S(1)}, bf16[512,128]{1,0:T(8,128)(2,1)S(1)}, u32[]{:S(2)}, u32[]{:S(2)}) collective-permute-start(bf16[512,128]{1,0:T(8,128)(2,1)S(1)} %collective-permute-done.1.refs_1_), channel_id=1, source_target_pairs={{0,3},{1,2},{2,1},{3,0},{4,7},{5,6},{6,5},{7,4},{8,11},{9,10},{10,... | collective-permute-start | bytes 393224 | tf_op jit(solution)/shard_map/ppermute | solution.py:283
  18.4 12.0 %slice-start.2 = ((s8[6291456]{0:T(1024)(128)(4,1)}), s8[4194304]{0:T(1024)(128)(4,1)S(1)}, s32[]{:S(2)}) async-start(s8[6291456]{0:T(1024)(128)(4,1)} %bitcast.12), calls=%async_computation.2 | async-start | bytes 8388608
  26.8 17.5 %collective-permute-start.13 = (bf16[512,128]{1,0:T(8,128)(2,1)S(1)}, bf16[512,128]{1,0:T(8,128)(2,1)S(1)}, u32[]{:S(2)}, u32[]{:S(2)}) collective-permute-start(bf16[512,128]{1,0:T(8,128)(2,1)S(1)} %get-tuple-element.41), channel_id=1, source_target_pairs={{0,3},{1,2},{2,1},{3,0},{4,7},{5,6},{6,5},{7,4},{8,11},{9,10},{10,... | collective-permute-start | bytes 393224 | tf_op jit(solution)/shard_map/ppermute | solution.py:283
  28.6 16.5 %collective-permute-start.14 = (bf16[512,128]{1,0:T(8,128)(2,1)S(1)}, bf16[512,128]{1,0:T(8,128)(2,1)S(1)}, u32[]{:S(2)}, u32[]{:S(2)}) collective-permute-start(bf16[512,128]{1,0:T(8,128)(2,1)S(1)} %get-tuple-element.42), channel_id=1, source_target_pairs={{0,1},{1,0},{2,3},{3,2},{4,5},{5,4},{6,7},{7,6},{8,9},{9,8},{10,11... | collective-permute-start | bytes 393224 | tf_op jit(solution)/shard_map/ppermute | solution.py:283
  29.7 15.5 %collective-permute-start.15 = (bf16[512,128]{1,0:T(8,128)(2,1)S(1)}, bf16[512,128]{1,0:T(8,128)(2,1)S(1)}, u32[]{:S(2)}, u32[]{:S(2)}) collective-permute-start(bf16[512,128]{1,0:T(8,128)(2,1)S(1)} %get-tuple-element.43), channel_id=1, source_target_pairs={{0,2},{1,3},{2,0},{3,1},{4,6},{5,7},{6,4},{7,5},{8,10},{9,11},{10,... | collective-permute-start | bytes 393224 | tf_op jit(solution)/shard_map/ppermute | solution.py:283
  33.3 4.6 %collective-permute-start.10 = (f32[8,128]{1,0:T(8,128)S(1)}, f32[8,128]{1,0:T(8,128)S(1)}, u32[]{:S(2)}, u32[]{:S(2)}) collective-permute-start(f32[8,128]{1,0:T(8,128)S(1)} %get-tuple-element.39.mine), channel_id=1, source_target_pairs={{0,4},{1,5},{2,6},{3,7},{4,0},{5,1},{6,2},{7,3},{8,12},{9,13},{10,... | collective-permute-start | bytes 12296 | tf_op jit(solution)/shard_map/ppermute | solution.py:283
  37.9 3.6 %collective-permute-start.11 = (f32[8,128]{1,0:T(8,128)S(1)}, f32[8,128]{1,0:T(8,128)S(1)}, u32[]{:S(2)}, u32[]{:S(2)}) collective-permute-start(f32[8,128]{1,0:T(8,128)S(1)} %shard_map.93.mine), channel_id=1, source_target_pairs={{0,1},{1,0},{2,3},{3,2},{4,5},{5,4},{6,7},{7,6},{8,9},{9,8},{10,11... | collective-permute-start | bytes 12296 | tf_op jit(solution)/shard_map/ppermute | solution.py:283
  41.6 9.1 %collective-permute-start.12 = (bf16[528,128]{1,0:T(8,128)(2,1)S(1)}, bf16[528,128]{1,0:T(8,128)(2,1)S(1)}, u32[]{:S(2)}, u32[]{:S(2)}) collective-permute-start(bf16[528,128]{1,0:T(8,128)(2,1)S(1)} %shard_map.95), channel_id=1, source_target_pairs={{0,2},{1,3},{2,0},{3,1},{4,6},{5,7},{6,4},{7,5},{8,10},{9,11},{10,... | collective-permute-start | bytes 405512 | tf_op jit(solution)/shard_map/ppermute | solution.py:283
  42.9 6.6 %collective-permute-start.8 = (bf16[512,128]{1,0:T(8,128)(2,1)S(1)}, bf16[512,128]{1,0:T(8,128)(2,1)S(1)}, u32[]{:S(2)}, u32[]{:S(2)}) collective-permute-start(bf16[512,128]{1,0:T(8,128)(2,1)S(1)} %get-tuple-element.36), channel_id=1, source_target_pairs={{0,3},{1,2},{2,1},{3,0},{4,7},{5,6},{6,5},{7,4},{8,11},{9,10},{10,... | collective-permute-start | bytes 393224 | tf_op jit(solution)/shard_map/ppermute | solution.py:283
  44.3 6.3 %collective-permute-start.9 = (bf16[512,128]{1,0:T(8,128)(2,1)S(1)}, bf16[512,128]{1,0:T(8,128)(2,1)S(1)}, u32[]{:S(2)}, u32[]{:S(2)}) collective-permute-start(bf16[512,128]{1,0:T(8,128)(2,1)S(1)} %get-tuple-element.37), channel_id=1, source_target_pairs={{0,1},{1,0},{2,3},{3,2},{4,5},{5,4},{6,7},{7,6},{8,9},{9,8},{10,11... | collective-permute-start | bytes 393224 | tf_op jit(solution)/shard_map/ppermute | solution.py:283
  45.2 9.3 %collective-permute-start.16 = (bf16[512,128]{1,0:T(8,128)(2,1)S(1)}, bf16[512,128]{1,0:T(8,128)(2,1)S(1)}, u32[]{:S(2)}, u32[]{:S(2)}) collective-permute-start(bf16[512,128]{1,0:T(8,128)(2,1)S(1)} %shard_map.96), channel_id=1, source_target_pairs={{0,4},{1,5},{2,6},{3,7},{4,0},{5,1},{6,2},{7,3},{8,12},{9,13},{10,... | collective-permute-start | bytes 393224 | tf_op jit(solution)/shard_map/ppermute | solution.py:283
  54.8 6.2 %collective-permute-start.17 = (bf16[512,128]{1,0:T(8,128)(2,1)S(1)}, bf16[512,128]{1,0:T(8,128)(2,1)S(1)}, u32[]{:S(2)}, u32[]{:S(2)}) collective-permute-start(bf16[512,128]{1,0:T(8,128)(2,1)S(1)} %get-tuple-element.45.refs_0_.vector), channel_id=1, source_target_pairs={{0,4},{1,5},{2,6},{3,7},{4,0},{5,1},{6,2},{7,3},{8,12},{9,13},{10,... | collective-permute-start | bytes 393224 | tf_op jit(solution)/shard_map/ppermute | solution.py:283
  55.5 8.1 %collective-permute-start.23 = (bf16[512,128]{1,0:T(8,128)(2,1)S(1)}, bf16[512,128]{1,0:T(8,128)(2,1)S(1)}, u32[]{:S(2)}, u32[]{:S(2)}) collective-permute-start(bf16[512,128]{1,0:T(8,128)(2,1)S(1)} %get-tuple-element.45.refs_0_.vector), channel_id=1, source_target_pairs={{0,2},{1,3},{2,0},{3,1},{4,6},{5,7},{6,4},{7,5},{8,10},{9,11},{10,... | collective-permute-start | bytes 393224 | tf_op jit(solution)/shard_map/ppermute | solution.py:283
  59.5 6.7 %collective-permute-start.22 = (bf16[512,128]{1,0:T(8,128)(2,1)S(1)}, bf16[512,128]{1,0:T(8,128)(2,1)S(1)}, u32[]{:S(2)}, u32[]{:S(2)}) collective-permute-start(bf16[512,128]{1,0:T(8,128)(2,1)S(1)} %get-tuple-element.45.refs_0_.vector), channel_id=1, source_target_pairs={{0,1},{1,0},{2,3},{3,2},{4,5},{5,4},{6,7},{7,6},{8,9},{9,8},{10,11... | collective-permute-start | bytes 393224 | tf_op jit(solution)/shard_map/ppermute | solution.py:283
  59.9 6.3 %collective-permute-start.21 = (bf16[512,128]{1,0:T(8,128)(2,1)S(1)}, bf16[512,128]{1,0:T(8,128)(2,1)S(1)}, u32[]{:S(2)}, u32[]{:S(2)}) collective-permute-start(bf16[512,128]{1,0:T(8,128)(2,1)S(1)} %get-tuple-element.45.refs_0_.vector), channel_id=1, source_target_pairs={{0,3},{1,2},{2,1},{3,0},{4,7},{5,6},{6,5},{7,4},{8,11},{9,10},{10,... | collective-permute-start | bytes 393224 | tf_op jit(solution)/shard_map/ppermute | solution.py:283
  61.0 6.4 %collective-permute-start.20 = (bf16[512,128]{1,0:T(8,128)(2,1)S(1)}, bf16[512,128]{1,0:T(8,128)(2,1)S(1)}, u32[]{:S(2)}, u32[]{:S(2)}) collective-permute-start(bf16[512,128]{1,0:T(8,128)(2,1)S(1)} %collective-permute-done.17.refs_1_), channel_id=1, source_target_pairs={{0,2},{1,3},{2,0},{3,1},{4,6},{5,7},{6,4},{7,5},{8,10},{9,11},{10,... | collective-permute-start | bytes 393224 | tf_op jit(solution)/shard_map/ppermute | solution.py:283
  63.1 5.0 %collective-permute-start.19 = (bf16[512,128]{1,0:T(8,128)(2,1)S(1)}, bf16[512,128]{1,0:T(8,128)(2,1)S(1)}, u32[]{:S(2)}, u32[]{:S(2)}) collective-permute-start(bf16[512,128]{1,0:T(8,128)(2,1)S(1)} %collective-permute-done.17.refs_1_), channel_id=1, source_target_pairs={{0,1},{1,0},{2,3},{3,2},{4,5},{5,4},{6,7},{7,6},{8,9},{9,8},{10,11... | collective-permute-start | bytes 393224 | tf_op jit(solution)/shard_map/ppermute | solution.py:283
  63.6 6.3 %collective-permute-start.18 = (bf16[512,128]{1,0:T(8,128)(2,1)S(1)}, bf16[512,128]{1,0:T(8,128)(2,1)S(1)}, u32[]{:S(2)}, u32[]{:S(2)}) collective-permute-start(bf16[512,128]{1,0:T(8,128)(2,1)S(1)} %collective-permute-done.17.refs_1_), channel_id=1, source_target_pairs={{0,3},{1,2},{2,1},{3,0},{4,7},{5,6},{6,5},{7,4},{8,11},{9,10},{10,... | collective-permute-start | bytes 393224 | tf_op jit(solution)/shard_map/ppermute | solution.py:283
  72.0 10.0 %collective-permute-start.27 = (bf16[512,128]{1,0:T(8,128)(2,1)S(1)}, bf16[512,128]{1,0:T(8,128)(2,1)S(1)}, u32[]{:S(2)}, u32[]{:S(2)}) collective-permute-start(bf16[512,128]{1,0:T(8,128)(2,1)S(1)} %get-tuple-element.52), channel_id=1, source_target_pairs={{0,3},{1,2},{2,1},{3,0},{4,7},{5,6},{6,5},{7,4},{8,11},{9,10},{10,... | collective-permute-start | bytes 393224 | tf_op jit(solution)/shard_map/ppermute | solution.py:283
  75.5 7.1 %collective-permute-start.28 = (bf16[512,128]{1,0:T(8,128)(2,1)S(1)}, bf16[512,128]{1,0:T(8,128)(2,1)S(1)}, u32[]{:S(2)}, u32[]{:S(2)}) collective-permute-start(bf16[512,128]{1,0:T(8,128)(2,1)S(1)} %get-tuple-element.53), channel_id=1, source_target_pairs={{0,1},{1,0},{2,3},{3,2},{4,5},{5,4},{6,7},{7,6},{8,9},{9,8},{10,11... | collective-permute-start | bytes 393224 | tf_op jit(solution)/shard_map/ppermute | solution.py:283
  75.5 7.1 %collective-permute-start.29 = (bf16[512,128]{1,0:T(8,128)(2,1)S(1)}, bf16[512,128]{1,0:T(8,128)(2,1)S(1)}, u32[]{:S(2)}, u32[]{:S(2)}) collective-permute-start(bf16[512,128]{1,0:T(8,128)(2,1)S(1)} %get-tuple-element.54), channel_id=1, source_target_pairs={{0,2},{1,3},{2,0},{3,1},{4,6},{5,7},{6,4},{7,5},{8,10},{9,11},{10,... | collective-permute-start | bytes 393224 | tf_op jit(solution)/shard_map/ppermute | solution.py:283
  79.0 6.4 %collective-permute-start.24 = (bf16[512,128]{1,0:T(8,128)(2,1)S(1)}, bf16[512,128]{1,0:T(8,128)(2,1)S(1)}, u32[]{:S(2)}, u32[]{:S(2)}) collective-permute-start(bf16[512,128]{1,0:T(8,128)(2,1)S(1)} %get-tuple-element.48), channel_id=1, source_target_pairs={{0,3},{1,2},{2,1},{3,0},{4,7},{5,6},{6,5},{7,4},{8,11},{9,10},{10,... | collective-permute-start | bytes 393224 | tf_op jit(solution)/shard_map/ppermute | solution.py:283
  81.9 5.0 %collective-permute-start.25 = (bf16[512,128]{1,0:T(8,128)(2,1)S(1)}, bf16[512,128]{1,0:T(8,128)(2,1)S(1)}, u32[]{:S(2)}, u32[]{:S(2)}) collective-permute-start(bf16[512,128]{1,0:T(8,128)(2,1)S(1)} %get-tuple-element.49), channel_id=1, source_target_pairs={{0,1},{1,0},{2,3},{3,2},{4,5},{5,4},{6,7},{7,6},{8,9},{9,8},{10,11... | collective-permute-start | bytes 393224 | tf_op jit(solution)/shard_map/ppermute | solution.py:283
  82.0 5.0 %collective-permute-start.26 = (bf16[512,128]{1,0:T(8,128)(2,1)S(1)}, bf16[512,128]{1,0:T(8,128)(2,1)S(1)}, u32[]{:S(2)}, u32[]{:S(2)}) collective-permute-start(bf16[512,128]{1,0:T(8,128)(2,1)S(1)} %get-tuple-element.50), channel_id=1, source_target_pairs={{0,2},{1,3},{2,0},{3,1},{4,6},{5,7},{6,4},{7,5},{8,10},{9,11},{10,... | collective-permute-start | bytes 393224 | tf_op jit(solution)/shard_map/ppermute | solution.py:283
  82.7 5.9 %collective-permute-start.30 = (bf16[512,128]{1,0:T(8,128)(2,1)S(1)}, bf16[512,128]{1,0:T(8,128)(2,1)S(1)}, u32[]{:S(2)}, u32[]{:S(2)}) collective-permute-start(bf16[512,128]{1,0:T(8,128)(2,1)S(1)} %shard_map.101), channel_id=1, source_target_pairs={{0,4},{1,5},{2,6},{3,7},{4,0},{5,1},{6,2},{7,3},{8,12},{9,13},{10,... | collective-permute-start | bytes 393224 | tf_op jit(solution)/shard_map/ppermute | solution.py:283
  (4 other events, 38.8 us)

commit v6 on v5

--- a/solution.py
+++ b/solution.py
@@ -167,9 +167,13 @@
     out[...] = total.astype(out.dtype)
 
 
-def final_kernel(kept, vector, hdiag, *refs):
+def base_kernel(kept, vector, hdiag, out):
+    out[...] = kept[...] + hdiag[...] * vector[...].astype(jnp.float32)
+
+
+def final_kernel(base, *refs):
     out = refs[-1]
-    total = kept[...] + hdiag[...] * vector[...].astype(jnp.float32)
+    total = base[...]
     for came in refs[:-1]:
         total = total + came[...].astype(jnp.float32)
     out[...] = total
@@ -336,7 +340,8 @@
     terms, sums = apply_terms(gather(psi), lead_left, left, lead_right, right, True)
     correction, theta = on_chip(partial(correct_kernel, half), [sent, tile], 0, *terms, psi, hdiag, *sums)
     terms, _ = apply_terms(gather(correction), lead_left, left, lead_right, right, False)
-    sigma_two = on_chip(final_kernel, [kept], 0, terms[0], correction, hdiag, *terms[1:])[0]
+    base = on_chip(base_kernel, [kept], 0, terms[0], correction, hdiag)[0]
+    sigma_two = on_chip(final_kernel, [kept], 0, base, *terms[1:])[0]
     return (sigma_two, theta[0, :1])
 
 

time: 89.6 us -> 89.6 us (level)
    pallas_call x14 -> x15, Pallas kernels: 11.5 us -> 11.5 us  [on_chip(): pl.pallas_call(kernel, out_shape=out_shape, in_specs=[SMEM] * nscalar + [...]
where the time goes in v6:
time: 89.6 us; the launch traced here: 89.4 us
  starting transfers between devices  47.5 us (53%)
  waiting for transfers between devices  23.6 us (26%)
  Pallas kernels  16.1 us (18%)
    ppermute x30, starting transfers between devices, exchange(): return lax.ppermute(array, 'ops', [(o, o ^ by) for o in range(devices)])  45.1 us
    ppermute x30, waiting for transfers between devices, exchange(): return lax.ppermute(array, 'ops', [(o, o ^ by) for o in range(devices)])  23.6 us
    pallas_call x15, Pallas kernels, on_chip(): pl.pallas_call(kernel, out_shape=out_shape, in_specs=[SMEM] * nscalar + [...  11.5 us
    pallas_call x2, Pallas kernels, loaded_chunks(): pl.pallas_call(partial(load_chunks_kernel, offsets), out_shape=pltpu.VMEM...  3.61 us
    ppermute x1, starting transfers between devices, shifted(): return lax.ppermute(array, axis, pairs)  2.4 us
  transfers between devices with their start and end apart: 31, of which 15 were waited for; matrix products, arithmetic and copies ran while one was open for 1% of the time, Pallas kernels for 12%

profile of v6, /device:TPU:0, one launch (start us, length us, event | category | flops | bytes accessed | tf_op | source)
XLA Modules:
  0.0 89.4 jit_solution(8555348951139333139)
XLA Ops:
  0.6 2.4 %collective-permute-start = (f32[512]{0:T(512)}, f32[512]{0:T(512)S(1)}, u32[]{:S(2)}, u32[]{:S(2)}) collective-permute-start(f32[512]{0:T(512)} %param.8), channel_id=1, source_target_pairs={{0,8},{8,16},{16,24},{1,9},{9,17},{17,25},{2,10},{10,18},{18,26},{... | collective-permute-start | bytes 6152 | tf_op jit(solution)/shard_map/ppermute | solution.py:14
  4.3 3.5 %collective-permute-start.1 = (bf16[512,128]{1,0:T(8,128)(2,1)S(1)}, bf16[512,128]{1,0:T(8,128)(2,1)S(1)}, u32[]{:S(2)}, u32[]{:S(2)}) collective-permute-start(bf16[512,128]{1,0:T(8,128)(2,1)S(1)} %shard_map.89.refs_0_.refs_5_), channel_id=1, source_target_pairs={{0,4},{1,5},{2,6},{3,7},{4,0},{5,1},{6,2},{7,3},{8,12},{9,13},{10,... | collective-permute-start | bytes 393224 | tf_op jit(solution)/shard_map/ppermute | solution.py:287
  7.8 1.6 %collective-permute-start.7 = (bf16[512,128]{1,0:T(8,128)(2,1)S(1)}, bf16[512,128]{1,0:T(8,128)(2,1)S(1)}, u32[]{:S(2)}, u32[]{:S(2)}) collective-permute-start(bf16[512,128]{1,0:T(8,128)(2,1)S(1)} %shard_map.89.refs_0_.refs_5_), channel_id=1, source_target_pairs={{0,2},{1,3},{2,0},{3,1},{4,6},{5,7},{6,4},{7,5},{8,10},{9,11},{10,... | collective-permute-start | bytes 393224 | tf_op jit(solution)/shard_map/ppermute | solution.py:287
  9.4 1.5 %collective-permute-start.6 = (bf16[512,128]{1,0:T(8,128)(2,1)S(1)}, bf16[512,128]{1,0:T(8,128)(2,1)S(1)}, u32[]{:S(2)}, u32[]{:S(2)}) collective-permute-start(bf16[512,128]{1,0:T(8,128)(2,1)S(1)} %shard_map.89.refs_0_.refs_5_), channel_id=1, source_target_pairs={{0,1},{1,0},{2,3},{3,2},{4,5},{5,4},{6,7},{7,6},{8,9},{9,8},{10,11... | collective-permute-start | bytes 393224 | tf_op jit(solution)/shard_map/ppermute | solution.py:287
  11.3 2.2 %collective-permute-done.1.refs_1_ = bf16[512,128]{1,0:T(8,128)(2,1)S(1)} collective-permute-done((bf16[512,128]{1,0:T(8,128)(2,1)S(1)}, bf16[512,128]{1,0:T(8,128)(2,1)S(1)}, u32[]{:S(2)}, u32[]{:S(2)}) %collective-permute-start.1) | collective-permute-done | bytes 131104 | tf_op jit(solution)/shard_map/ppermute | solution.py:287
  13.5 2.4 %collective-permute-start.4 = (bf16[512,128]{1,0:T(8,128)(2,1)S(1)}, bf16[512,128]{1,0:T(8,128)(2,1)S(1)}, u32[]{:S(2)}, u32[]{:S(2)}) collective-permute-start(bf16[512,128]{1,0:T(8,128)(2,1)S(1)} %collective-permute-done.1.refs_1_), channel_id=1, source_target_pairs={{0,2},{1,3},{2,0},{3,1},{4,6},{5,7},{6,4},{7,5},{8,10},{9,11},{10,... | collective-permute-start | bytes 393224 | tf_op jit(solution)/shard_map/ppermute | solution.py:287
  15.9 1.5 %collective-permute-start.3 = (bf16[512,128]{1,0:T(8,128)(2,1)S(1)}, bf16[512,128]{1,0:T(8,128)(2,1)S(1)}, u32[]{:S(2)}, u32[]{:S(2)}) collective-permute-start(bf16[512,128]{1,0:T(8,128)(2,1)S(1)} %collective-permute-done.1.refs_1_), channel_id=1, source_target_pairs={{0,1},{1,0},{2,3},{3,2},{4,5},{5,4},{6,7},{7,6},{8,9},{9,8},{10,11... | collective-permute-start | bytes 393224 | tf_op jit(solution)/shard_map/ppermute | solution.py:287
  18.4 1.8 %shard_map.87.right = bf16[6,1536,128]{2,1,0:T(8,128)(2,1)S(1)} custom-call(s32[1]{0:T(128)} %bitcast.place, bf16[6,4096,128]{2,1,0:T(8,128)(2,1)} %bitcast.11), custom_call_target="tpu_custom_call" | custom-call | tf_op jit(solution)/shard_map/pallas_call | solution.py:259
  20.2 1.8 %shard_map.86.left = bf16[6,1536,128]{2,1,0:T(8,128)(2,1)S(1)} custom-call(s32[1]{0:T(128)} %bitcast.place, bf16[6,4096,128]{2,1,0:T(8,128)(2,1)} %bitcast.6), custom_call_target="tpu_custom_call" | custom-call | tf_op jit(solution)/shard_map/pallas_call | solution.py:259
  23.3 1.4 %collective-permute-done.2.refs_0_ = bf16[512,128]{1,0:T(8,128)(2,1)S(1)} collective-permute-done((bf16[512,128]{1,0:T(8,128)(2,1)S(1)}, bf16[512,128]{1,0:T(8,128)(2,1)S(1)}, u32[]{:S(2)}, u32[]{:S(2)}) %collective-permute-start.2) | collective-permute-done | bytes 131104 | tf_op jit(solution)/shard_map/ppermute | solution.py:287
  24.8 2.1 %shard_map.91 = (bf16[4224,128]{1,0:T(8,128)(2,1)S(1)}, bf16[512,128]{1,0:T(8,128)(2,1)S(1)}, bf16[512,128]{1,0:T(8,128)(2,1)S(1)}, bf16[512,128]{1,0:T(8,128)(2,1)S(1)}, f32[8,128]{1,0:T(8,128)S(1)}) custom-call(s32[1]{0:T(128)} %bitcast.place, s32[192]{0:T(256)S(1)} %select_n.17.links, ...), custom_call_target="tpu_custom_call", output_to_operand_aliasing={{0}: (7, {})} | custom-call | tf_op jit(solution)/shard_map/pallas_call | solution.py:234
  26.8 1.8 %collective-permute-start.13 = (bf16[512,128]{1,0:T(8,128)(2,1)S(1)}, bf16[512,128]{1,0:T(8,128)(2,1)S(1)}, u32[]{:S(2)}, u32[]{:S(2)}) collective-permute-start(bf16[512,128]{1,0:T(8,128)(2,1)S(1)} %get-tuple-element.41), channel_id=1, source_target_pairs={{0,3},{1,2},{2,1},{3,0},{4,7},{5,6},{6,5},{7,4},{8,11},{9,10},{10,... | collective-permute-start | bytes 393224 | tf_op jit(solution)/shard_map/ppermute | solution.py:287
  30.4 2.9 %shard_map.92 = (bf16[512,128]{1,0:T(8,128)(2,1)S(1)}, bf16[512,128]{1,0:T(8,128)(2,1)S(1)}, bf16[512,128]{1,0:T(8,128)(2,1)S(1)}, f32[512,128]{1,0:T(8,128)S(1)...) custom-call(s32[1]{0:T(128)} %bitcast.place, s32[192]{0:T(256)S(1)} %select_n.17.links, ...), custom_call_target="tpu_custom_call" | custom-call | tf_op jit(solution)/shard_map/pallas_call | solution.py:234
  33.3 2.7 %collective-permute-start.10 = (f32[8,128]{1,0:T(8,128)S(1)}, f32[8,128]{1,0:T(8,128)S(1)}, u32[]{:S(2)}, u32[]{:S(2)}) collective-permute-start(f32[8,128]{1,0:T(8,128)S(1)} %get-tuple-element.39.mine), channel_id=1, source_target_pairs={{0,4},{1,5},{2,6},{3,7},{4,0},{5,1},{6,2},{7,3},{8,12},{9,13},{10,... | collective-permute-start | bytes 12296 | tf_op jit(solution)/shard_map/ppermute | solution.py:287
  36.1 1.8 %collective-permute-done.10.other = f32[8,128]{1,0:T(8,128)S(1)} collective-permute-done((f32[8,128]{1,0:T(8,128)S(1)}, f32[8,128]{1,0:T(8,128)S(1)}, u32[]{:S(2)}, u32[]{:S(2)}) %collective-permute-start.10) | collective-permute-done | bytes 4128 | tf_op jit(solution)/shard_map/ppermute | solution.py:287
  39.2 2.4 %collective-permute-done.11.other = f32[8,128]{1,0:T(8,128)S(1)} collective-permute-done((f32[8,128]{1,0:T(8,128)S(1)}, f32[8,128]{1,0:T(8,128)S(1)}, u32[]{:S(2)}, u32[]{:S(2)}) %collective-permute-start.11) | collective-permute-done | bytes 4128 | tf_op jit(solution)/shard_map/ppermute | solution.py:287
  41.6 1.4 %collective-permute-start.12 = (bf16[528,128]{1,0:T(8,128)(2,1)S(1)}, bf16[528,128]{1,0:T(8,128)(2,1)S(1)}, u32[]{:S(2)}, u32[]{:S(2)}) collective-permute-start(bf16[528,128]{1,0:T(8,128)(2,1)S(1)} %shard_map.95), channel_id=1, source_target_pairs={{0,2},{1,3},{2,0},{3,1},{4,6},{5,7},{6,4},{7,5},{8,10},{9,11},{10,... | collective-permute-start | bytes 405512 | tf_op jit(solution)/shard_map/ppermute | solution.py:287
  42.9 1.4 %collective-permute-start.8 = (bf16[512,128]{1,0:T(8,128)(2,1)S(1)}, bf16[512,128]{1,0:T(8,128)(2,1)S(1)}, u32[]{:S(2)}, u32[]{:S(2)}) collective-permute-start(bf16[512,128]{1,0:T(8,128)(2,1)S(1)} %get-tuple-element.36), channel_id=1, source_target_pairs={{0,3},{1,2},{2,1},{3,0},{4,7},{5,6},{6,5},{7,4},{8,11},{9,10},{10,... | collective-permute-start | bytes 393224 | tf_op jit(solution)/shard_map/ppermute | solution.py:287
  45.2 2.7 %collective-permute-start.16 = (bf16[512,128]{1,0:T(8,128)(2,1)S(1)}, bf16[512,128]{1,0:T(8,128)(2,1)S(1)}, u32[]{:S(2)}, u32[]{:S(2)}) collective-permute-start(bf16[512,128]{1,0:T(8,128)(2,1)S(1)} %shard_map.96), channel_id=1, source_target_pairs={{0,4},{1,5},{2,6},{3,7},{4,0},{5,1},{6,2},{7,3},{8,12},{9,13},{10,... | collective-permute-start | bytes 393224 | tf_op jit(solution)/shard_map/ppermute | solution.py:287
  47.9 1.6 %collective-permute-done.8.refs_1_ = bf16[512,128]{1,0:T(8,128)(2,1)S(1)} collective-permute-done((bf16[512,128]{1,0:T(8,128)(2,1)S(1)}, bf16[512,128]{1,0:T(8,128)(2,1)S(1)}, u32[]{:S(2)}, u32[]{:S(2)}) %collective-permute-start.8) | collective-permute-done | bytes 131104 | tf_op jit(solution)/shard_map/ppermute | solution.py:287
  50.7 3.9 %collective-permute-done.16.refs_4_ = bf16[512,128]{1,0:T(8,128)(2,1)S(1)} collective-permute-done((bf16[512,128]{1,0:T(8,128)(2,1)S(1)}, bf16[512,128]{1,0:T(8,128)(2,1)S(1)}, u32[]{:S(2)}, u32[]{:S(2)}) %collective-permute-start.16) | collective-permute-done | bytes 131104 | tf_op jit(solution)/shard_map/ppermute | solution.py:287
  55.5 4.0 %collective-permute-start.23 = (bf16[512,128]{1,0:T(8,128)(2,1)S(1)}, bf16[512,128]{1,0:T(8,128)(2,1)S(1)}, u32[]{:S(2)}, u32[]{:S(2)}) collective-permute-start(bf16[512,128]{1,0:T(8,128)(2,1)S(1)} %get-tuple-element.45.refs_0_.vector), channel_id=1, source_target_pairs={{0,2},{1,3},{2,0},{3,1},{4,6},{5,7},{6,4},{7,5},{8,10},{9,11},{10,... | collective-permute-start | bytes 393224 | tf_op jit(solution)/shard_map/ppermute | solution.py:287
  61.0 2.1 %collective-permute-start.20 = (bf16[512,128]{1,0:T(8,128)(2,1)S(1)}, bf16[512,128]{1,0:T(8,128)(2,1)S(1)}, u32[]{:S(2)}, u32[]{:S(2)}) collective-permute-start(bf16[512,128]{1,0:T(8,128)(2,1)S(1)} %collective-permute-done.17.refs_1_), channel_id=1, source_target_pairs={{0,2},{1,3},{2,0},{3,1},{4,6},{5,7},{6,4},{7,5},{8,10},{9,11},{10,... | collective-permute-start | bytes 393224 | tf_op jit(solution)/shard_map/ppermute | solution.py:287
  63.6 1.5 %collective-permute-start.18 = (bf16[512,128]{1,0:T(8,128)(2,1)S(1)}, bf16[512,128]{1,0:T(8,128)(2,1)S(1)}, u32[]{:S(2)}, u32[]{:S(2)}) collective-permute-start(bf16[512,128]{1,0:T(8,128)(2,1)S(1)} %collective-permute-done.17.refs_1_), channel_id=1, source_target_pairs={{0,3},{1,2},{2,1},{3,0},{4,7},{5,6},{6,5},{7,4},{8,11},{9,10},{10,... | collective-permute-start | bytes 393224 | tf_op jit(solution)/shard_map/ppermute | solution.py:287
  68.0 1.9 %collective-permute-done.18.refs_0_ = bf16[512,128]{1,0:T(8,128)(2,1)S(1)} collective-permute-done((bf16[512,128]{1,0:T(8,128)(2,1)S(1)}, bf16[512,128]{1,0:T(8,128)(2,1)S(1)}, u32[]{:S(2)}, u32[]{:S(2)}) %collective-permute-start.18) | collective-permute-done | bytes 131104 | tf_op jit(solution)/shard_map/ppermute | solution.py:287
  69.9 2.1 %shard_map.99 = (bf16[4224,128]{1,0:T(8,128)(2,1)S(1)}, bf16[512,128]{1,0:T(8,128)(2,1)S(1)}, bf16[512,128]{1,0:T(8,128)(2,1)S(1)}, bf16[512,128]{1,0:T(8,128)(2,1)S(1)}) custom-call(s32[1]{0:T(128)} %bitcast.place, s32[192]{0:T(256)S(1)} %select_n.17.links, bf16[6,1536,128]{2,1,0:T(8,128)(2,1)S(1)} %shard_map.86.left, ...), custom_call_target="tpu_custom_call", output_to_operand_aliasing={{0}: (7, {})} | custom-call | tf_op jit(solution)/shard_map/pallas_call | solution.py:234
  72.0 3.5 %collective-permute-start.27 = (bf16[512,128]{1,0:T(8,128)(2,1)S(1)}, bf16[512,128]{1,0:T(8,128)(2,1)S(1)}, u32[]{:S(2)}, u32[]{:S(2)}) collective-permute-start(bf16[512,128]{1,0:T(8,128)(2,1)S(1)} %get-tuple-element.52), channel_id=1, source_target_pairs={{0,3},{1,2},{2,1},{3,0},{4,7},{5,6},{6,5},{7,4},{8,11},{9,10},{10,... | collective-permute-start | bytes 393224 | tf_op jit(solution)/shard_map/ppermute | solution.py:287
  76.1 2.9 %shard_map.100 = (bf16[512,128]{1,0:T(8,128)(2,1)S(1)}, bf16[512,128]{1,0:T(8,128)(2,1)S(1)}, bf16[512,128]{1,0:T(8,128)(2,1)S(1)}, f32[512,128]{1,0:T(8,128)S(1)}, f32[512,128]{1,0:T(8,128)S(1)}) custom-call(s32[1]{0:T(128)} %bitcast.place, s32[192]{0:T(256)S(1)} %select_n.17.links, bf16[6,4096,128]{2,1,0:T(8,128)(2,1)S(1)} %bitcast.10, ...), custom_call_target="tpu_custom_call" | custom-call | tf_op jit(solution)/shard_map/pallas_call | solution.py:234
  79.0 2.9 %collective-permute-start.24 = (bf16[512,128]{1,0:T(8,128)(2,1)S(1)}, bf16[512,128]{1,0:T(8,128)(2,1)S(1)}, u32[]{:S(2)}, u32[]{:S(2)}) collective-permute-start(bf16[512,128]{1,0:T(8,128)(2,1)S(1)} %get-tuple-element.48), channel_id=1, source_target_pairs={{0,3},{1,2},{2,1},{3,0},{4,7},{5,6},{6,5},{7,4},{8,11},{9,10},{10,... | collective-permute-start | bytes 393224 | tf_op jit(solution)/shard_map/ppermute | solution.py:287
  82.7 2.2 %collective-permute-start.30 = (bf16[512,128]{1,0:T(8,128)(2,1)S(1)}, bf16[512,128]{1,0:T(8,128)(2,1)S(1)}, u32[]{:S(2)}, u32[]{:S(2)}) collective-permute-start(bf16[512,128]{1,0:T(8,128)(2,1)S(1)} %shard_map.102), channel_id=1, source_target_pairs={{0,4},{1,5},{2,6},{3,7},{4,0},{5,1},{6,2},{7,3},{8,12},{9,13},{10,... | collective-permute-start | bytes 393224 | tf_op jit(solution)/shard_map/ppermute | solution.py:287
  85.4 1.5 %collective-permute-done.25.refs_1_ = bf16[512,128]{1,0:T(8,128)(2,1)S(1)} collective-permute-done((bf16[512,128]{1,0:T(8,128)(2,1)S(1)}, bf16[512,128]{1,0:T(8,128)(2,1)S(1)}, u32[]{:S(2)}, u32[]{:S(2)}) %collective-permute-start.25) | collective-permute-done | bytes 131104 | tf_op jit(solution)/shard_map/ppermute | solution.py:287
  87.0 1.6 %collective-permute-done.30.refs_3_ = bf16[512,128]{1,0:T(8,128)(2,1)S(1)} collective-permute-done((bf16[512,128]{1,0:T(8,128)(2,1)S(1)}, bf16[512,128]{1,0:T(8,128)(2,1)S(1)}, u32[]{:S(2)}, u32[]{:S(2)}) %collective-permute-start.30) | collective-permute-done | bytes 131104 | tf_op jit(solution)/shard_map/ppermute | solution.py:287
  (64 shorter events, 17.6 us)
Async XLA Ops:
  0.6 3.4 %collective-permute-start = (f32[512]{0:T(512)}, f32[512]{0:T(512)S(1)}, u32[]{:S(2)}, u32[]{:S(2)}) collective-permute-start(f32[512]{0:T(512)} %param.8), channel_id=1, source_target_pairs={{0,8},{8,16},{16,24},{1,9},{9,17},{17,25},{2,10},{10,18},{18,26},{... | collective-permute-start | bytes 6152 | tf_op jit(solution)/shard_map/ppermute | solution.py:14
  4.3 9.2 %collective-permute-start.1 = (bf16[512,128]{1,0:T(8,128)(2,1)S(1)}, bf16[512,128]{1,0:T(8,128)(2,1)S(1)}, u32[]{:S(2)}, u32[]{:S(2)}) collective-permute-start(bf16[512,128]{1,0:T(8,128)(2,1)S(1)} %shard_map.89.refs_0_.refs_5_), channel_id=1, source_target_pairs={{0,4},{1,5},{2,6},{3,7},{4,0},{5,1},{6,2},{7,3},{8,12},{9,13},{10,... | collective-permute-start | bytes 393224 | tf_op jit(solution)/shard_map/ppermute | solution.py:287
  7.8 9.7 %collective-permute-start.7 = (bf16[512,128]{1,0:T(8,128)(2,1)S(1)}, bf16[512,128]{1,0:T(8,128)(2,1)S(1)}, u32[]{:S(2)}, u32[]{:S(2)}) collective-permute-start(bf16[512,128]{1,0:T(8,128)(2,1)S(1)} %shard_map.89.refs_0_.refs_5_), channel_id=1, source_target_pairs={{0,2},{1,3},{2,0},{3,1},{4,6},{5,7},{6,4},{7,5},{8,10},{9,11},{10,... | collective-permute-start | bytes 393224 | tf_op jit(solution)/shard_map/ppermute | solution.py:287
  9.4 12.7 %collective-permute-start.6 = (bf16[512,128]{1,0:T(8,128)(2,1)S(1)}, bf16[512,128]{1,0:T(8,128)(2,1)S(1)}, u32[]{:S(2)}, u32[]{:S(2)}) collective-permute-start(bf16[512,128]{1,0:T(8,128)(2,1)S(1)} %shard_map.89.refs_0_.refs_5_), channel_id=1, source_target_pairs={{0,1},{1,0},{2,3},{3,2},{4,5},{5,4},{6,7},{7,6},{8,9},{9,8},{10,11... | collective-permute-start | bytes 393224 | tf_op jit(solution)/shard_map/ppermute | solution.py:287
  10.9 11.2 %collective-permute-start.5 = (bf16[512,128]{1,0:T(8,128)(2,1)S(1)}, bf16[512,128]{1,0:T(8,128)(2,1)S(1)}, u32[]{:S(2)}, u32[]{:S(2)}) collective-permute-start(bf16[512,128]{1,0:T(8,128)(2,1)S(1)} %shard_map.89.refs_0_.refs_5_), channel_id=1, source_target_pairs={{0,3},{1,2},{2,1},{3,0},{4,7},{5,6},{6,5},{7,4},{8,11},{9,10},{10,... | collective-permute-start | bytes 393224 | tf_op jit(solution)/shard_map/ppermute | solution.py:287
  13.5 8.7 %collective-permute-start.4 = (bf16[512,128]{1,0:T(8,128)(2,1)S(1)}, bf16[512,128]{1,0:T(8,128)(2,1)S(1)}, u32[]{:S(2)}, u32[]{:S(2)}) collective-permute-start(bf16[512,128]{1,0:T(8,128)(2,1)S(1)} %collective-permute-done.1.refs_1_), channel_id=1, source_target_pairs={{0,2},{1,3},{2,0},{3,1},{4,6},{5,7},{6,4},{7,5},{8,10},{9,11},{10,... | collective-permute-start | bytes 393224 | tf_op jit(solution)/shard_map/ppermute | solution.py:287
  15.9 7.4 %collective-permute-start.3 = (bf16[512,128]{1,0:T(8,128)(2,1)S(1)}, bf16[512,128]{1,0:T(8,128)(2,1)S(1)}, u32[]{:S(2)}, u32[]{:S(2)}) collective-permute-start(bf16[512,128]{1,0:T(8,128)(2,1)S(1)} %collective-permute-done.1.refs_1_), channel_id=1, source_target_pairs={{0,1},{1,0},{2,3},{3,2},{4,5},{5,4},{6,7},{7,6},{8,9},{9,8},{10,11... | collective-permute-start | bytes 393224 | tf_op jit(solution)/shard_map/ppermute | solution.py:287
  17.4 7.3 %collective-permute-start.2 = (bf16[512,128]{1,0:T(8,128)(2,1)S(1)}, bf16[512,128]{1,0:T(8,128)(2,1)S(1)}, u32[]{:S(2)}, u32[]{:S(2)}) collective-permute-start(bf16[512,128]{1,0:T(8,128)(2,1)S(1)} %collective-permute-done.1.refs_1_), channel_id=1, source_target_pairs={{0,3},{1,2},{2,1},{3,0},{4,7},{5,6},{6,5},{7,4},{8,11},{9,10},{10,... | collective-permute-start | bytes 393224 | tf_op jit(solution)/shard_map/ppermute | solution.py:287
  18.4 12.0 %slice-start.2 = ((s8[6291456]{0:T(1024)(128)(4,1)}), s8[4194304]{0:T(1024)(128)(4,1)S(1)}, s32[]{:S(2)}) async-start(s8[6291456]{0:T(1024)(128)(4,1)} %bitcast.12), calls=%async_computation.2 | async-start | bytes 8388608
  26.8 17.5 %collective-permute-start.13 = (bf16[512,128]{1,0:T(8,128)(2,1)S(1)}, bf16[512,128]{1,0:T(8,128)(2,1)S(1)}, u32[]{:S(2)}, u32[]{:S(2)}) collective-permute-start(bf16[512,128]{1,0:T(8,128)(2,1)S(1)} %get-tuple-element.41), channel_id=1, source_target_pairs={{0,3},{1,2},{2,1},{3,0},{4,7},{5,6},{6,5},{7,4},{8,11},{9,10},{10,... | collective-permute-start | bytes 393224 | tf_op jit(solution)/shard_map/ppermute | solution.py:287
  28.6 16.5 %collective-permute-start.14 = (bf16[512,128]{1,0:T(8,128)(2,1)S(1)}, bf16[512,128]{1,0:T(8,128)(2,1)S(1)}, u32[]{:S(2)}, u32[]{:S(2)}) collective-permute-start(bf16[512,128]{1,0:T(8,128)(2,1)S(1)} %get-tuple-element.42), channel_id=1, source_target_pairs={{0,1},{1,0},{2,3},{3,2},{4,5},{5,4},{6,7},{7,6},{8,9},{9,8},{10,11... | collective-permute-start | bytes 393224 | tf_op jit(solution)/shard_map/ppermute | solution.py:287
  29.7 15.5 %collective-permute-start.15 = (bf16[512,128]{1,0:T(8,128)(2,1)S(1)}, bf16[512,128]{1,0:T(8,128)(2,1)S(1)}, u32[]{:S(2)}, u32[]{:S(2)}) collective-permute-start(bf16[512,128]{1,0:T(8,128)(2,1)S(1)} %get-tuple-element.43), channel_id=1, source_target_pairs={{0,2},{1,3},{2,0},{3,1},{4,6},{5,7},{6,4},{7,5},{8,10},{9,11},{10,... | collective-permute-start | bytes 393224 | tf_op jit(solution)/shard_map/ppermute | solution.py:287
  33.3 4.6 %collective-permute-start.10 = (f32[8,128]{1,0:T(8,128)S(1)}, f32[8,128]{1,0:T(8,128)S(1)}, u32[]{:S(2)}, u32[]{:S(2)}) collective-permute-start(f32[8,128]{1,0:T(8,128)S(1)} %get-tuple-element.39.mine), channel_id=1, source_target_pairs={{0,4},{1,5},{2,6},{3,7},{4,0},{5,1},{6,2},{7,3},{8,12},{9,13},{10,... | collective-permute-start | bytes 12296 | tf_op jit(solution)/shard_map/ppermute | solution.py:287
  37.9 3.6 %collective-permute-start.11 = (f32[8,128]{1,0:T(8,128)S(1)}, f32[8,128]{1,0:T(8,128)S(1)}, u32[]{:S(2)}, u32[]{:S(2)}) collective-permute-start(f32[8,128]{1,0:T(8,128)S(1)} %shard_map.93.mine), channel_id=1, source_target_pairs={{0,1},{1,0},{2,3},{3,2},{4,5},{5,4},{6,7},{7,6},{8,9},{9,8},{10,11... | collective-permute-start | bytes 12296 | tf_op jit(solution)/shard_map/ppermute | solution.py:287
  41.6 9.1 %collective-permute-start.12 = (bf16[528,128]{1,0:T(8,128)(2,1)S(1)}, bf16[528,128]{1,0:T(8,128)(2,1)S(1)}, u32[]{:S(2)}, u32[]{:S(2)}) collective-permute-start(bf16[528,128]{1,0:T(8,128)(2,1)S(1)} %shard_map.95), channel_id=1, source_target_pairs={{0,2},{1,3},{2,0},{3,1},{4,6},{5,7},{6,4},{7,5},{8,10},{9,11},{10,... | collective-permute-start | bytes 405512 | tf_op jit(solution)/shard_map/ppermute | solution.py:287
  42.9 6.6 %collective-permute-start.8 = (bf16[512,128]{1,0:T(8,128)(2,1)S(1)}, bf16[512,128]{1,0:T(8,128)(2,1)S(1)}, u32[]{:S(2)}, u32[]{:S(2)}) collective-permute-start(bf16[512,128]{1,0:T(8,128)(2,1)S(1)} %get-tuple-element.36), channel_id=1, source_target_pairs={{0,3},{1,2},{2,1},{3,0},{4,7},{5,6},{6,5},{7,4},{8,11},{9,10},{10,... | collective-permute-start | bytes 393224 | tf_op jit(solution)/shard_map/ppermute | solution.py:287
  44.3 6.3 %collective-permute-start.9 = (bf16[512,128]{1,0:T(8,128)(2,1)S(1)}, bf16[512,128]{1,0:T(8,128)(2,1)S(1)}, u32[]{:S(2)}, u32[]{:S(2)}) collective-permute-start(bf16[512,128]{1,0:T(8,128)(2,1)S(1)} %get-tuple-element.37), channel_id=1, source_target_pairs={{0,1},{1,0},{2,3},{3,2},{4,5},{5,4},{6,7},{7,6},{8,9},{9,8},{10,11... | collective-permute-start | bytes 393224 | tf_op jit(solution)/shard_map/ppermute | solution.py:287
  45.2 9.3 %collective-permute-start.16 = (bf16[512,128]{1,0:T(8,128)(2,1)S(1)}, bf16[512,128]{1,0:T(8,128)(2,1)S(1)}, u32[]{:S(2)}, u32[]{:S(2)}) collective-permute-start(bf16[512,128]{1,0:T(8,128)(2,1)S(1)} %shard_map.96), channel_id=1, source_target_pairs={{0,4},{1,5},{2,6},{3,7},{4,0},{5,1},{6,2},{7,3},{8,12},{9,13},{10,... | collective-permute-start | bytes 393224 | tf_op jit(solution)/shard_map/ppermute | solution.py:287
  54.8 6.2 %collective-permute-start.17 = (bf16[512,128]{1,0:T(8,128)(2,1)S(1)}, bf16[512,128]{1,0:T(8,128)(2,1)S(1)}, u32[]{:S(2)}, u32[]{:S(2)}) collective-permute-start(bf16[512,128]{1,0:T(8,128)(2,1)S(1)} %get-tuple-element.45.refs_0_.vector), channel_id=1, source_target_pairs={{0,4},{1,5},{2,6},{3,7},{4,0},{5,1},{6,2},{7,3},{8,12},{9,13},{10,... | collective-permute-start | bytes 393224 | tf_op jit(solution)/shard_map/ppermute | solution.py:287
  55.5 8.1 %collective-permute-start.23 = (bf16[512,128]{1,0:T(8,128)(2,1)S(1)}, bf16[512,128]{1,0:T(8,128)(2,1)S(1)}, u32[]{:S(2)}, u32[]{:S(2)}) collective-permute-start(bf16[512,128]{1,0:T(8,128)(2,1)S(1)} %get-tuple-element.45.refs_0_.vector), channel_id=1, source_target_pairs={{0,2},{1,3},{2,0},{3,1},{4,6},{5,7},{6,4},{7,5},{8,10},{9,11},{10,... | collective-permute-start | bytes 393224 | tf_op jit(solution)/shard_map/ppermute | solution.py:287
  59.5 6.7 %collective-permute-start.22 = (bf16[512,128]{1,0:T(8,128)(2,1)S(1)}, bf16[512,128]{1,0:T(8,128)(2,1)S(1)}, u32[]{:S(2)}, u32[]{:S(2)}) collective-permute-start(bf16[512,128]{1,0:T(8,128)(2,1)S(1)} %get-tuple-element.45.refs_0_.vector), channel_id=1, source_target_pairs={{0,1},{1,0},{2,3},{3,2},{4,5},{5,4},{6,7},{7,6},{8,9},{9,8},{10,11... | collective-permute-start | bytes 393224 | tf_op jit(solution)/shard_map/ppermute | solution.py:287
  59.9 6.3 %collective-permute-start.21 = (bf16[512,128]{1,0:T(8,128)(2,1)S(1)}, bf16[512,128]{1,0:T(8,128)(2,1)S(1)}, u32[]{:S(2)}, u32[]{:S(2)}) collective-permute-start(bf16[512,128]{1,0:T(8,128)(2,1)S(1)} %get-tuple-element.45.refs_0_.vector), channel_id=1, source_target_pairs={{0,3},{1,2},{2,1},{3,0},{4,7},{5,6},{6,5},{7,4},{8,11},{9,10},{10,... | collective-permute-start | bytes 393224 | tf_op jit(solution)/shard_map/ppermute | solution.py:287
  61.0 6.4 %collective-permute-start.20 = (bf16[512,128]{1,0:T(8,128)(2,1)S(1)}, bf16[512,128]{1,0:T(8,128)(2,1)S(1)}, u32[]{:S(2)}, u32[]{:S(2)}) collective-permute-start(bf16[512,128]{1,0:T(8,128)(2,1)S(1)} %collective-permute-done.17.refs_1_), channel_id=1, source_target_pairs={{0,2},{1,3},{2,0},{3,1},{4,6},{5,7},{6,4},{7,5},{8,10},{9,11},{10,... | collective-permute-start | bytes 393224 | tf_op jit(solution)/shard_map/ppermute | solution.py:287
  63.1 5.0 %collective-permute-start.19 = (bf16[512,128]{1,0:T(8,128)(2,1)S(1)}, bf16[512,128]{1,0:T(8,128)(2,1)S(1)}, u32[]{:S(2)}, u32[]{:S(2)}) collective-permute-start(bf16[512,128]{1,0:T(8,128)(2,1)S(1)} %collective-permute-done.17.refs_1_), channel_id=1, source_target_pairs={{0,1},{1,0},{2,3},{3,2},{4,5},{5,4},{6,7},{7,6},{8,9},{9,8},{10,11... | collective-permute-start | bytes 393224 | tf_op jit(solution)/shard_map/ppermute | solution.py:287
  63.6 6.3 %collective-permute-start.18 = (bf16[512,128]{1,0:T(8,128)(2,1)S(1)}, bf16[512,128]{1,0:T(8,128)(2,1)S(1)}, u32[]{:S(2)}, u32[]{:S(2)}) collective-permute-start(bf16[512,128]{1,0:T(8,128)(2,1)S(1)} %collective-permute-done.17.refs_1_), channel_id=1, source_target_pairs={{0,3},{1,2},{2,1},{3,0},{4,7},{5,6},{6,5},{7,4},{8,11},{9,10},{10,... | collective-permute-start | bytes 393224 | tf_op jit(solution)/shard_map/ppermute | solution.py:287
  72.0 10.0 %collective-permute-start.27 = (bf16[512,128]{1,0:T(8,128)(2,1)S(1)}, bf16[512,128]{1,0:T(8,128)(2,1)S(1)}, u32[]{:S(2)}, u32[]{:S(2)}) collective-permute-start(bf16[512,128]{1,0:T(8,128)(2,1)S(1)} %get-tuple-element.52), channel_id=1, source_target_pairs={{0,3},{1,2},{2,1},{3,0},{4,7},{5,6},{6,5},{7,4},{8,11},{9,10},{10,... | collective-permute-start | bytes 393224 | tf_op jit(solution)/shard_map/ppermute | solution.py:287
  75.5 7.1 %collective-permute-start.28 = (bf16[512,128]{1,0:T(8,128)(2,1)S(1)}, bf16[512,128]{1,0:T(8,128)(2,1)S(1)}, u32[]{:S(2)}, u32[]{:S(2)}) collective-permute-start(bf16[512,128]{1,0:T(8,128)(2,1)S(1)} %get-tuple-element.53), channel_id=1, source_target_pairs={{0,1},{1,0},{2,3},{3,2},{4,5},{5,4},{6,7},{7,6},{8,9},{9,8},{10,11... | collective-permute-start | bytes 393224 | tf_op jit(solution)/shard_map/ppermute | solution.py:287
  75.5 7.1 %collective-permute-start.29 = (bf16[512,128]{1,0:T(8,128)(2,1)S(1)}, bf16[512,128]{1,0:T(8,128)(2,1)S(1)}, u32[]{:S(2)}, u32[]{:S(2)}) collective-permute-start(bf16[512,128]{1,0:T(8,128)(2,1)S(1)} %get-tuple-element.54), channel_id=1, source_target_pairs={{0,2},{1,3},{2,0},{3,1},{4,6},{5,7},{6,4},{7,5},{8,10},{9,11},{10,... | collective-permute-start | bytes 393224 | tf_op jit(solution)/shard_map/ppermute | solution.py:287
  79.0 6.4 %collective-permute-start.24 = (bf16[512,128]{1,0:T(8,128)(2,1)S(1)}, bf16[512,128]{1,0:T(8,128)(2,1)S(1)}, u32[]{:S(2)}, u32[]{:S(2)}) collective-permute-start(bf16[512,128]{1,0:T(8,128)(2,1)S(1)} %get-tuple-element.48), channel_id=1, source_target_pairs={{0,3},{1,2},{2,1},{3,0},{4,7},{5,6},{6,5},{7,4},{8,11},{9,10},{10,... | collective-permute-start | bytes 393224 | tf_op jit(solution)/shard_map/ppermute | solution.py:287
  81.9 5.0 %collective-permute-start.25 = (bf16[512,128]{1,0:T(8,128)(2,1)S(1)}, bf16[512,128]{1,0:T(8,128)(2,1)S(1)}, u32[]{:S(2)}, u32[]{:S(2)}) collective-permute-start(bf16[512,128]{1,0:T(8,128)(2,1)S(1)} %get-tuple-element.49), channel_id=1, source_target_pairs={{0,1},{1,0},{2,3},{3,2},{4,5},{5,4},{6,7},{7,6},{8,9},{9,8},{10,11... | collective-permute-start | bytes 393224 | tf_op jit(solution)/shard_map/ppermute | solution.py:287
  82.0 5.0 %collective-permute-start.26 = (bf16[512,128]{1,0:T(8,128)(2,1)S(1)}, bf16[512,128]{1,0:T(8,128)(2,1)S(1)}, u32[]{:S(2)}, u32[]{:S(2)}) collective-permute-start(bf16[512,128]{1,0:T(8,128)(2,1)S(1)} %get-tuple-element.50), channel_id=1, source_target_pairs={{0,2},{1,3},{2,0},{3,1},{4,6},{5,7},{6,4},{7,5},{8,10},{9,11},{10,... | collective-permute-start | bytes 393224 | tf_op jit(solution)/shard_map/ppermute | solution.py:287
  82.7 5.9 %collective-permute-start.30 = (bf16[512,128]{1,0:T(8,128)(2,1)S(1)}, bf16[512,128]{1,0:T(8,128)(2,1)S(1)}, u32[]{:S(2)}, u32[]{:S(2)}) collective-permute-start(bf16[512,128]{1,0:T(8,128)(2,1)S(1)} %shard_map.102), channel_id=1, source_target_pairs={{0,4},{1,5},{2,6},{3,7},{4,0},{5,1},{6,2},{7,3},{8,12},{9,13},{10,... | collective-permute-start | bytes 393224 | tf_op jit(solution)/shard_map/ppermute | solution.py:287
  (4 other events, 38.8 us)
